TPU v7x, 32 devices: a whole 2x2x4 slice. The times are simulated.
32 devices in a mesh: layer: 4 (over y, x), trace: 8 (over z, core).
Axes of the slice: x: 2, y: 2, z: 4, core: 2. Of those that a mesh axis runs over, the one named last changes fastest.
Arguments:
- operators: bfloat16 [4, 48, 512, 512], P('layer', 'trace'), may hold values from -0.25 to 0.25
- sources: bfloat16 [4, 2, 131072, 128], P('layer', None, 'trace'), may hold values from -6 to 6
- row_block: int32 [4, 8, 6], P('layer'), may hold values from 0 to 255, as said below
- col_block: int32 [4, 8, 6], P('layer', 'trace'), may hold values from 0 to 255, as said below
Outputs:
- traces: bfloat16 [4, 2, 131072, 128], P('layer', None, 'trace')
Inputs may be any that keep to these rules, and one draw needn't show every extreme that they name: `row_block`: for each layer and each trace index d, the 6 row blocks name distinct owners; in each layer some owner is named by every d, and so are owners 0 and 7. `col_block`: entries of trace index d lie in d * 32 to (d + 1) * 32 - 1.
All inputs are finite; a program needn't handle non-finite values.
Results may differ from a plain program's by a relative error of at most 0.0077.
Values may be sent and summed in bfloat16 or wider, within the bound.
No kernel may reach another device: no remote copies, remote signals or barrier semaphores. Data moves between devices by JAX's collectives and lax.ppermute only.
A program may use at most 128 MiB of HBM per device.

v0:
```python
import jax
import jax.numpy as jnp
from jax import lax
from jax.experimental import pallas as pl
from jax.experimental.pallas import tpu as pltpu
from jax.sharding import PartitionSpec as P


AXES = ("layer", "trace")
SMEM = pl.BlockSpec(memory_space=pltpu.SMEM)
ANY = pl.BlockSpec(memory_space=pl.ANY)
PARAMS = pltpu.CompilerParams(vmem_limit_bytes=67043328)
DMA = pltpu.SemaphoreType.DMA


def owner_of(row, owned):
    if owned & (owned - 1) == 0:
        return lax.shift_right_logical(row, jnp.int32(owned.bit_length() - 1))
    return lax.div(row, jnp.int32(owned))


def first_kernel(senders, owned, state, rows, cols, source, blocks, *refs):
    slots, refs = refs[:senders], refs[senders:]
    kept, operand, pieces, made, op_sem, in_sem, slot_sem, keep_sem = refs
    place = state[0]
    stored, _ = blocks.shape[:2]
    batches, shots = source.shape[0], source.shape[-1]

    def load(block):
        return pltpu.make_async_copy(blocks.at[block], operand.at[block], op_sem.at[block])

    def fetch(block, batch):
        return pltpu.make_async_copy(
            source.at[batch, cols[block] - place * owned],
            pieces.at[block, :, pl.ds(batch * shots, shots)],
            in_sem.at[block, batch],
        )

    def give(block, slot):
        return pltpu.make_async_copy(made.at[block], slots[slot], slot_sem.at[block])

    def keep(block, owner):
        return pltpu.make_async_copy(made.at[block], kept.at[owner], keep_sem.at[block])

    @pl.loop(0, stored)
    def _(block):
        for batch in range(batches):
            fetch(block, batch).start()
        load(block).start()

    @pl.loop(0, stored)
    def _(block):
        for batch in range(batches):
            fetch(block, batch).wait()
        load(block).wait()
        product = jnp.dot(operand[block], pieces[block], preferred_element_type=jnp.float32)
        for batch in range(batches):
            made[block, batch] = product[:, batch * shots : (batch + 1) * shots].astype(made.dtype)
        owner = owner_of(rows[place, block], owned)
        shift = lax.rem(owner - place + senders, senders)
        for slot in range(senders):

            @pl.when(shift == slot)
            def _():
                give(block, slot).start()

        keep(block, owner).start()

    @pl.loop(0, stored)
    def _(block):
        give(block, 0).wait()
        keep(block, 0).wait()


def renew_kernel(senders, owned, state, rows, cols, match, go, source, blocks, *refs):
    recv, refs = refs[:senders], refs[senders:]
    kept, operand, pieces, arrived, total, made, op_sem, in_sem, recv_sem, keep_sem = refs[1:]
    place = state[0]
    stored, _ = blocks.shape[:2]
    batches, shots = source.shape[0], source.shape[-1]

    def load(block):
        return pltpu.make_async_copy(blocks.at[block], operand.at[block], op_sem.at[block])

    def fetch(block, batch):
        return pltpu.make_async_copy(
            source.at[batch, cols[block] - place * owned],
            pieces.at[block, :, pl.ds(batch * shots, shots)],
            in_sem.at[block, batch],
        )

    def take(step):
        return pltpu.make_async_copy(recv[step], arrived.at[step], recv_sem.at[step])

    def keep(block, owner):
        return pltpu.make_async_copy(made.at[block], kept.at[owner], keep_sem.at[block])

    def hits(block):
        return match[block, senders]

    def sender_at(step):
        return lax.rem(place - step + senders, senders)

    @pl.when(go[0] > 0)
    def _():
        for step in range(senders):

            @pl.when(match[stored, sender_at(step)] > 0)
            def _():
                take(step).start()

        @pl.loop(0, stored)
        def _(block):
            @pl.when(hits(block) > 0)
            def _():
                for batch in range(batches):
                    fetch(block, batch).start()
                load(block).start()

        for step in range(senders):

            @pl.when(match[stored, sender_at(step)] > 0)
            def _():
                take(step).wait()

        @pl.loop(0, stored)
        def _(block):
            @pl.when(hits(block) > 0)
            def _():
                total[...] = jnp.zeros_like(total)

                @pl.loop(0, senders)
                def _(step):
                    @pl.when(match[block, sender_at(step)] > 0)
                    def _():
                        total[...] += arrived[step].astype(jnp.float32)

                for batch in range(batches):
                    fetch(block, batch).wait()
                for batch in range(batches):
                    lanes = pl.ds(batch * shots, shots)
                    incoming = total[batch].astype(pieces.dtype).astype(jnp.float32)
                    pieces[block, :, lanes] = (
                        incoming + pieces[block, :, lanes].astype(jnp.float32)
                    ).astype(pieces.dtype)
                load(block).wait()
                product = jnp.dot(operand[block], pieces[block], preferred_element_type=jnp.float32)
                for batch in range(batches):
                    made[block, batch] = product[:, batch * shots : (batch + 1) * shots].astype(made.dtype)
                keep(block, owner_of(rows[place, block], owned)).start()

        @pl.loop(0, stored)
        def _(block):
            @pl.when(hits(block) > 0)
            def _():
                keep(block, 0).wait()


def hit_rows(rows, senders, place, owned, stored, here):
    first = place * owned

    @pl.loop(0, senders)
    def _(sender):
        row = jnp.int32(-1)
        for other in range(stored):
            value = rows[sender, other] - first
            row = jnp.where((value >= 0) & (value < owned), value, row)
        here[sender] = row


def zero_kernel(owned, senders, stored, batches, state, rows, after, out, nothing, here, sem):
    hit_rows(rows, senders, state[0], owned, stored, here)
    nothing[...] = jnp.zeros_like(nothing)

    def free(row):
        total = jnp.int32(0)
        for sender in range(senders):
            total += (here[sender] == row).astype(jnp.int32)
        return total == 0

    def put(batch, row):
        return pltpu.make_async_copy(nothing, out.at[batch, row], sem.at[batch, row])

    @pl.loop(0, owned)
    def _(row):
        @pl.when(free(row))
        def _():
            for batch in range(batches):
                put(batch, row).start()

    @pl.loop(0, owned)
    def _(row):
        @pl.when(free(row))
        def _():
            for batch in range(batches):
                put(batch, row).wait()


def write_kernel(owned, senders, stored, batches, state, rows, recv, old, out, arrived, total, made, here, in_sem, out_sem):
    hit_rows(rows, senders, state[0], owned, stored, here)

    def take(sender):
        return pltpu.make_async_copy(recv.at[sender], arrived.at[sender], in_sem.at[sender])

    def put(sender, batch, box):
        return pltpu.make_async_copy(box.at[sender, batch], out.at[batch, here[sender]], out_sem.at[sender, batch])

    def count(sender, first, last):
        total = jnp.int32(0)
        for other in range(senders):
            same = (here[other] == here[sender]) & (other >= first) & (other < last)
            total += same.astype(jnp.int32)
        return total

    @pl.loop(0, senders)
    def _(sender):
        @pl.when(here[sender] >= 0)
        def _():
            take(sender).start()

    @pl.loop(0, senders)
    def _(sender):
        @pl.when(here[sender] >= 0)
        def _():
            take(sender).wait()

    @pl.loop(0, senders)
    def _(sender):
        @pl.when((here[sender] >= 0) & (count(sender, 0, sender) == 0))
        def _():
            more = count(sender, sender + 1, senders)

            @pl.when(more == 0)
            def _():
                for batch in range(batches):
                    put(sender, batch, arrived).start()

            @pl.when(more > 0)
            def _():
                total[...] = arrived[sender].astype(jnp.float32)

                @pl.loop(sender + 1, senders)
                def _(other):
                    @pl.when(here[other] == here[sender])
                    def _():
                        total[...] += arrived[other].astype(jnp.float32)

                made[sender] = total[...].astype(made.dtype)
                for batch in range(batches):
                    put(sender, batch, made).start()

    @pl.loop(0, senders)
    def _(sender):
        @pl.when((here[sender] >= 0) & (count(sender, 0, sender) == 0))
        def _():
            for batch in range(batches):
                put(sender, batch, made).wait()


def body(operators, sources, row_block, col_block):
    place = lax.axis_index("trace")
    depth = lax.axis_index("layer")
    senders = lax.axis_size("trace")
    layers = lax.axis_size("layer")
    blocks = operators[0]
    rows = row_block[0]
    stored, width = blocks.shape[0], blocks.shape[-1]
    batches, local, shots = sources.shape[1:]
    owned = local // width
    source = sources.reshape(batches, owned, width, shots)
    cols = col_block[0, 0]
    state = jnp.stack([place, depth]).astype(jnp.int32)
    dtype = sources.dtype
    tile = (batches, width, shots)
    slot = jax.ShapeDtypeStruct(tile, dtype)
    held = jax.ShapeDtypeStruct((senders,) + tile, dtype)

    def pairs(step):
        return [
            (i * senders + j, (i + 1) * senders + (j + step) % senders)
            for i in range(layers - 1)
            for j in range(senders)
        ]

    *slots, kept = pl.pallas_call(
        lambda *refs: first_kernel(senders, owned, *refs),
        out_shape=(slot,) * senders + (held,),
        in_specs=[SMEM] * 3 + [ANY] * 2,
        out_specs=(ANY,) * (senders + 1),
        scratch_shapes=[
            pltpu.VMEM((stored, width, width), dtype),
            pltpu.VMEM((stored, width, batches * shots), dtype),
            pltpu.VMEM((stored,) + tile, dtype),
            DMA((stored,)),
            DMA((stored, batches)),
            DMA((stored,)),
            DMA((stored,)),
        ],
        compiler_params=PARAMS,
        name="first",
    )(state, rows, cols, source, blocks)
    recv = []
    for step in range(senders):
        recv.append(lax.ppermute(slots[step], AXES, pairs(step)))

    total = layers * senders
    mine = jnp.concatenate([rows.reshape(-1), cols])
    mine, kept = lax.optimization_barrier((mine, kept))
    mine = jnp.broadcast_to(mine[None], (total, mine.shape[0]))
    known = lax.all_to_all(mine, AXES, split_axis=0, concat_axis=0, tiled=True)
    known = known.reshape(layers, senders, -1)
    blocks_all = senders * stored
    rows_all = known[:, 0, :blocks_all]
    cols_all = known[:, :, blocks_all:].reshape(layers, blocks_all)
    feeds = rows_all[:-1, :, None] == cols_all[1:, None, :]
    read = jnp.any(feeds, axis=2)
    home = jnp.repeat(jnp.arange(senders, dtype=jnp.int32), stored)
    shift = (rows_all[:-1] // owned - home[None, :]) % senders
    steps = jnp.arange(senders, dtype=jnp.int32)
    changed = jnp.any(feeds, axis=1)
    masks = []
    group = 4 if senders <= 8 else 2
    for _ in range(2, layers):
        below = jnp.concatenate([jnp.zeros((1, blocks_all), bool), changed[:-1]])
        again = below & read
        mask = jnp.any(again[:, :, None] & (shift[:, :, None] == steps), axis=(0, 1)).astype(jnp.int32)
        masks.append(mask)
        changed = jnp.any(feeds & below[:, :, None], axis=1)

    above = lax.dynamic_index_in_dim(rows_all, jnp.maximum(depth - 1, 0), 0, keepdims=False)
    above = above.reshape(senders, stored)
    match = jnp.any((above[None] == cols[:, None, None]) & (depth > 0), axis=2).astype(jnp.int32)
    match = jnp.concatenate([match, jnp.max(match, axis=0, keepdims=True)])
    match = jnp.concatenate([match, jnp.max(match, axis=1, keepdims=True)], axis=1)

    def renew(kept, go):
        return pl.pallas_call(
            lambda *refs: renew_kernel(senders, owned, *refs),
            out_shape=held,
            in_specs=[SMEM] * 5 + [ANY] * (3 + senders),
            out_specs=ANY,
            scratch_shapes=[
                pltpu.VMEM((stored, width, width), dtype),
                pltpu.VMEM((stored, width, batches * shots), dtype),
                pltpu.VMEM((senders,) + tile, dtype),
                pltpu.VMEM(tile, jnp.float32),
                pltpu.VMEM((stored,) + tile, dtype),
                DMA((stored,)),
                DMA((stored, batches)),
                DMA((senders,)),
                DMA((stored,)),
            ],
            input_output_aliases={7 + senders: 0},
            compiler_params=PARAMS,
            name="renew",
        )(state, rows, cols, match, go[None], source, blocks, *recv, kept)

    traces = pl.pallas_call(
        lambda *refs: zero_kernel(owned, senders, stored, batches, *refs),
        out_shape=jax.ShapeDtypeStruct((batches, owned, width, shots), dtype),
        in_specs=[SMEM, SMEM, ANY],
        out_specs=ANY,
        scratch_shapes=[
            pltpu.VMEM((width, shots), dtype),
            pltpu.SMEM((senders,), jnp.int32),
            DMA((batches, owned)),
        ],
        compiler_params=PARAMS,
        name="zeros",
    )(state, rows, recv[0])

    kept = renew(kept, jnp.int32(1))

    def again(step, kept):
        sent = lax.dynamic_index_in_dim(kept, (place + step) % senders, 0, keepdims=False)
        return lax.ppermute(sent, AXES, pairs(step))

    for wave, mask in enumerate(masks):
        if wave == 0:
            for low in range(0, senders, group):
                near = range(low, min(low + group, senders))

                def resend(which):
                    return lambda kept, old: tuple(
                        again(step, kept) if which >> at & 1 else old[at] for at, step in enumerate(near)
                    )

                code = sum(mask[step] << at for at, step in enumerate(near))
                recv[low : low + group] = lax.switch(
                    code, [resend(which) for which in range(1 << len(near))], kept, tuple(recv[low : low + group])
                )
        else:

            def resend_one(carry):
                left, recv = carry
                step = jnp.argmax(left).astype(jnp.int32)
                recv = lax.switch(
                    step,
                    [
                        lambda kept, recv, step=step: recv[:step] + (again(step, kept),) + recv[step + 1 :]
                        for step in range(senders)
                    ],
                    kept,
                    recv,
                )
                return jnp.where(steps == step, 0, left), recv

            recv = list(lax.while_loop(lambda carry: jnp.max(carry[0]) > 0, resend_one, (mask, tuple(recv)))[1])
        kept = renew(kept, jnp.max(mask))

    arrived = lax.all_to_all(kept, "trace", split_axis=0, concat_axis=0, tiled=True)
    traces = pl.pallas_call(
        lambda *refs: write_kernel(owned, senders, stored, batches, *refs),
        out_shape=jax.ShapeDtypeStruct((batches, owned, width, shots), dtype),
        in_specs=[SMEM, SMEM, ANY, ANY],
        out_specs=ANY,
        scratch_shapes=[
            pltpu.VMEM((senders,) + tile, dtype),
            pltpu.VMEM(tile, jnp.float32),
            pltpu.VMEM((senders,) + tile, dtype),
            pltpu.SMEM((senders,), jnp.int32),
            DMA((senders,)),
            DMA((senders, batches)),
        ],
        input_output_aliases={3: 0},
        compiler_params=PARAMS,
        name="write",
    )(state, rows, arrived, traces)
    return traces.reshape(1, batches, local, shots)


def solution(mesh):
    placed = (
        P("layer", "trace", None, None),
        P("layer", None, "trace", None),
        P("layer", None, None),
        P("layer", "trace", None),
    )
    return jax.shard_map(
        body, mesh=mesh, in_specs=placed, out_specs=P("layer", None, "trace", None), check_vma=False
    )
```

profile of v0, /device:TPU:4, one launch (start us, length us, event | category | flops | bytes accessed | tf_op | source)
XLA Modules:
  0.0 157.8 jit_solution(4616847763310693290)
XLA Ops:
  0.0 0.8 copy.18
  0.8 0.0 copy-start
  0.8 0.6 copy-done
  1.3 0.1 reshape_squeeze.3
  1.4 0.6 pad_add_fusion.1.refs_0_
  2.0 1.3 pad_add_fusion.2
  3.3 4.8 %first.1 = (bf16[2,512,128]{2,1,0:T(8,128)(2,1)}, bf16[2,512,128]{2,1,0:T(8,128)(2,1)}, bf16[2,512,128]{2,1,0:T(8,128)(2,1)}, bf16[2,512,128]{2,1,0:T(8,128)(2,1...) custom-call(s32[2]{0:T(128)} %pad_add_fusion.1.refs_0_, ...), custom_call_target="tpu_custom_call" | custom-call | tf_op jit(solution)/shard_map/first/pallas_call | solution.py:285
  8.1 1.2 broadcast_in_dim.15
  9.3 6.1 %all-to-all-start = ((s32[32,1,54]{2,1,0:T(1,128)}), s32[32,1,54]{2,1,0:T(1,128)S(1)}, u32[]{:S(2)}, u32[]{:S(2)}) async-start(s32[32,1,54]{2,1,0:T(1,128)} %broadcast_in_dim.15), calls=%async_computation | async-start | bytes 32768 | tf_op jit(solution)/shard_map/all_to_all | solution.py:310
  15.4 3.4 %collective-permute-start.72 = (bf16[2,512,128]{2,1,0:T(8,128)(2,1)}, bf16[2,512,128]{2,1,0:T(8,128)(2,1)}, u32[]{:S(2)}, u32[]{:S(2)}) collective-permute-start(bf16[2,512,128]{2,1,0:T(8,128)(2,1)} %get-tuple-element.684), channel_id=1, source_target_pairs={{0,8},{1,9},{2,10},{3,11},{4,12},{5,13},{6,14},{7,15},{8,16},{9,17... | collective-permute-start | bytes 786440 | tf_op jit(solution)/shard_map/ppermute | solution.py:304
  18.8 1.9 %collective-permute-start.73 = (bf16[2,512,128]{2,1,0:T(8,128)(2,1)}, bf16[2,512,128]{2,1,0:T(8,128)(2,1)}, u32[]{:S(2)}, u32[]{:S(2)}) collective-permute-start(bf16[2,512,128]{2,1,0:T(8,128)(2,1)} %get-tuple-element.685), channel_id=1, source_target_pairs={{0,9},{1,10},{2,11},{3,12},{4,13},{5,14},{6,15},{7,8},{8,17},{9,18... | collective-permute-start | bytes 786440 | tf_op jit(solution)/shard_map/ppermute | solution.py:304
  20.7 1.9 %collective-permute-start.74 = (bf16[2,512,128]{2,1,0:T(8,128)(2,1)}, bf16[2,512,128]{2,1,0:T(8,128)(2,1)}, u32[]{:S(2)}, u32[]{:S(2)}) collective-permute-start(bf16[2,512,128]{2,1,0:T(8,128)(2,1)} %get-tuple-element.686), channel_id=1, source_target_pairs={{0,10},{1,11},{2,12},{3,13},{4,14},{5,15},{6,8},{7,9},{8,18},{9,19... | collective-permute-start | bytes 786440 | tf_op jit(solution)/shard_map/ppermute | solution.py:304
  22.7 1.9 %collective-permute-start.75 = (bf16[2,512,128]{2,1,0:T(8,128)(2,1)}, bf16[2,512,128]{2,1,0:T(8,128)(2,1)}, u32[]{:S(2)}, u32[]{:S(2)}) collective-permute-start(bf16[2,512,128]{2,1,0:T(8,128)(2,1)} %get-tuple-element.687), channel_id=1, source_target_pairs={{0,11},{1,12},{2,13},{3,14},{4,15},{5,8},{6,9},{7,10},{8,19},{9,20... | collective-permute-start | bytes 786440 | tf_op jit(solution)/shard_map/ppermute | solution.py:304
  24.6 1.9 %collective-permute-start.76 = (bf16[2,512,128]{2,1,0:T(8,128)(2,1)}, bf16[2,512,128]{2,1,0:T(8,128)(2,1)}, u32[]{:S(2)}, u32[]{:S(2)}) collective-permute-start(bf16[2,512,128]{2,1,0:T(8,128)(2,1)} %get-tuple-element.688), channel_id=1, source_target_pairs={{0,12},{1,13},{2,14},{3,15},{4,8},{5,9},{6,10},{7,11},{8,20},{9,21... | collective-permute-start | bytes 786440 | tf_op jit(solution)/shard_map/ppermute | solution.py:304
  26.5 0.1 sub.25
  26.6 0.0 all-to-all-done
  26.6 0.1 slice.60
  26.7 0.1 eq.142
  26.8 0.1 compare_reduce_fusion.1
  26.9 0.2 fusion.2
  27.2 0.2 fusion.6
  27.4 0.1 eq.136
  27.5 0.7 fusion.11
  28.1 0.9 and_reduce_fusion
  29.0 5.2 %collective-permute-done.72.refs_7_.refs_2_ = bf16[2,512,128]{2,1,0:T(8,128)(2,1)} collective-permute-done((bf16[2,512,128]{2,1,0:T(8,128)(2,1)}, bf16[2,512,128]{2,1,0:T(8,128)(2,1)}, u32[]{:S(2)}, u32[]{:S(2)}) %collective-permute-start.72) | collective-permute-done | bytes 262176 | tf_op jit(solution)/shard_map/ppermute | solution.py:304
  34.3 15.4 %collective-permute-start.77 = (bf16[2,512,128]{2,1,0:T(8,128)(2,1)}, bf16[2,512,128]{2,1,0:T(8,128)(2,1)}, u32[]{:S(2)}, u32[]{:S(2)}) collective-permute-start(bf16[2,512,128]{2,1,0:T(8,128)(2,1)} %get-tuple-element.689), channel_id=1, source_target_pairs={{0,13},{1,14},{2,15},{3,8},{4,9},{5,10},{6,11},{7,12},{8,21},{9,22... | collective-permute-start | bytes 786440 | tf_op jit(solution)/shard_map/ppermute | solution.py:304
  49.7 0.0 collective-permute-done.73.refs_8_
  49.7 1.9 %collective-permute-start.78 = (bf16[2,512,128]{2,1,0:T(8,128)(2,1)}, bf16[2,512,128]{2,1,0:T(8,128)(2,1)}, u32[]{:S(2)}, u32[]{:S(2)}) collective-permute-start(bf16[2,512,128]{2,1,0:T(8,128)(2,1)} %get-tuple-element.690), channel_id=1, source_target_pairs={{0,14},{1,15},{2,8},{3,9},{4,10},{5,11},{6,12},{7,13},{8,22},{9,23... | collective-permute-start | bytes 786440 | tf_op jit(solution)/shard_map/ppermute | solution.py:304
  51.6 0.0 collective-permute-done.74.refs_9_
  51.7 1.9 %collective-permute-start.79 = (bf16[2,512,128]{2,1,0:T(8,128)(2,1)}, bf16[2,512,128]{2,1,0:T(8,128)(2,1)}, u32[]{:S(2)}, u32[]{:S(2)}) collective-permute-start(bf16[2,512,128]{2,1,0:T(8,128)(2,1)} %get-tuple-element.691), channel_id=1, source_target_pairs={{0,15},{1,8},{2,9},{3,10},{4,11},{5,12},{6,13},{7,14},{8,23},{9,16... | collective-permute-start | bytes 786440 | tf_op jit(solution)/shard_map/ppermute | solution.py:304
  53.6 0.5 convert_element_type.10
  54.2 0.1 add_reduce_fusion
  54.3 0.1 copy.20
  59.4 0.7 pad_add_fusion.refs_3_
  60.1 0.7 convert_reduce_fusion.1
  60.8 0.0 collective-permute-done.75.refs_10_
  60.8 0.0 collective-permute-done.76.refs_11_
  60.8 0.0 collective-permute-done.77.refs_12_
  60.8 5.6 %collective-permute-done.78.refs_13_ = bf16[2,512,128]{2,1,0:T(8,128)(2,1)} collective-permute-done((bf16[2,512,128]{2,1,0:T(8,128)(2,1)}, bf16[2,512,128]{2,1,0:T(8,128)(2,1)}, u32[]{:S(2)}, u32[]{:S(2)}) %collective-permute-start.78) | collective-permute-done | bytes 262176 | tf_op jit(solution)/shard_map/ppermute | solution.py:304
  66.3 5.5 %collective-permute-done.79.refs_14_ = bf16[2,512,128]{2,1,0:T(8,128)(2,1)} collective-permute-done((bf16[2,512,128]{2,1,0:T(8,128)(2,1)}, bf16[2,512,128]{2,1,0:T(8,128)(2,1)}, u32[]{:S(2)}, u32[]{:S(2)}) %collective-permute-start.79) | collective-permute-done | bytes 262176 | tf_op jit(solution)/shard_map/ppermute | solution.py:304
  71.9 4.9 %renew.3.refs_15_ = bf16[8,2,512,128]{3,2,1,0:T(8,128)(2,1)} custom-call(s32[2]{0:T(128)} %pad_add_fusion.1.refs_0_, s32[8,6]{1,0:T(8,128)} %bitcast.174, s32[6]{0:T(128)} %bitcast.187, s32[7,9]{1,0:T(8,128)} %pad_add_fusion.refs_3_, s32[1]{0:T(128)} %constant.901.clone.1.refs_4_, ...), custom_call_target="tpu_custom_call", output_to_operand_aliasing={{}: (15, {})} | custom-call | tf_op jit(solution)/shard_map/renew/pallas_call | solution.py:337
  76.8 12.5 %conditional.4 = ((bf16[2,512,128]{2,1,0:T(8,128)(2,1)}, bf16[2,512,128]{2,1,0:T(8,128)(2,1)}, bf16[2,512,128]{2,1,0:T(8,128)(2,1)}, bf16[2,512,128]{2,1,0:T(8,128)(2,1)})) conditional(s32[]{:T(128)} %bitcast.83, (bf16[2,512,128]{2,1,0:T(8,128)(2,1)}, bf16[2,512,128]{2,1,0:T(8,128)(2,1)}, ...), branch_computations={%region_25.26_spmd, %region_26.27_spmd, %region_27.28_spmd, %regio... | conditional | flops 60 | bytes 6292292 | solution.py:389
  76.8 1.0 dynamic-slice_bitcast_fusion.44
  77.8 2.2 %collective-permute-start.44 = (bf16[2,512,128]{2,1,0:T(8,128)(2,1)S(1)}, bf16[2,512,128]{2,1,0:T(8,128)(2,1)}, u32[]{:S(2)}, u32[]{:S(2)}) collective-permute-start(bf16[2,512,128]{2,1,0:T(8,128)(2,1)S(1)} %dynamic-slice_bitcast_fusion.44), channel_id=1, source_target_pairs={{0,15},{1,8},{2,9},{3,10},{4,11},{5,12},{6,13},{7,14},{8,23},{9,16... | collective-permute-start | bytes 786440 | tf_op jit(solution)/shard_map/cond/branch_8_fun/ppermute | solution.py:376
  80.0 9.3 %collective-permute-done.44 = bf16[2,512,128]{2,1,0:T(8,128)(2,1)} collective-permute-done((bf16[2,512,128]{2,1,0:T(8,128)(2,1)S(1)}, bf16[2,512,128]{2,1,0:T(8,128)(2,1)}, u32[]{:S(2)}, u32[]{:S(2)}) %collective-permute-start.44) | collective-permute-done | bytes 262176 | tf_op jit(solution)/shard_map/cond/branch_8_fun/ppermute | solution.py:376
  89.3 1.7 %conditional.3 = (bf16[2,512,128]{2,1,0:T(8,128)(2,1)}, bf16[2,512,128]{2,1,0:T(8,128)(2,1)}, bf16[2,512,128]{2,1,0:T(8,128)(2,1)}, bf16[2,512,128]{2,1,0:T(8,128)(2,1)}) conditional(s32[]{:T(128)} %bitcast.82, (bf16[2,512,128]{2,1,0:T(8,128)(2,1)}, bf16[2,512,128]{2,1,0:T(8,128)(2,1)}, ...), branch_computations={%region_9.10_spmd, %region_10.11_spmd, %region_11.12_spmd, %region... | conditional | flops 59 | bytes 6292272 | solution.py:389
  89.3 1.7 %copy.91 = bf16[2,512,128]{2,1,0:T(8,128)(2,1)} copy(bf16[2,512,128]{2,1,0:T(8,128)(2,1)} %get-tuple-element.985) | data formatting | bytes 524288 | tf_op jit(solution)/shard_map/cond
  91.0 5.6 %renew.4.refs_15_ = bf16[8,2,512,128]{3,2,1,0:T(8,128)(2,1)} custom-call(s32[2]{0:T(128)} %pad_add_fusion.1.refs_0_, s32[8,6]{1,0:T(8,128)} %bitcast.175, s32[6]{0:T(128)} %bitcast.188, s32[7,9]{1,0:T(8,128)} %pad_add_fusion.refs_3_, s32[1]{0:T(128)} %bitcast.84.refs_4_, bf16[2,32,512,128]{3,2,1,0:T(8,128)(2,1)} %bitcast.167, ...), custom_call_target="tpu_custom_call", output_to_operand_aliasing={{}: (15, {})} | custom-call | tf_op jit(solution)/shard_map/renew/pallas_call | solution.py:337
  96.5 2.2 %while.25 = (s32[8]{0:T(128)}, bf16[2,512,128]{2,1,0:T(8,128)(2,1)}, bf16[2,512,128]{2,1,0:T(8,128)(2,1)}, bf16[2,512,128]{2,1,0:T(8,128)(2,1)}, bf16[2,512,128]...) while((s32[8]{0:T(128)}, ...), condition=%wide.region_52.54_spmd.clone, body=%wide.region_42.52_spmd.clone.sunk | while | flops 89 | bytes 1573980 | solution.py:408
  96.5 1.3 reduce_max.54
  98.7 1.7 %renew.5 = bf16[8,2,512,128]{3,2,1,0:T(8,128)(2,1)} custom-call(s32[2]{0:T(128)} %pad_add_fusion.1.refs_0_, s32[8,6]{1,0:T(8,128)} %bitcast.176, s32[6]{0:T(128)} %bitcast.189, s32[7,9]{1,0:T(8,128)} %pad_add_fusion.refs_3_, s32[1]{0:T(128)} %bitcast.81.refs_4_, bf16[2,32,512,128]{3,2,1,0:T(8,128)(2,1)} %bitcast.168, ...), custom_call_target="tpu_custom_call", output_to_operand_aliasing={{}: (15, {})} | custom-call | tf_op jit(solution)/shard_map/renew/pallas_call | solution.py:337
  100.4 4.4 %all-to-all-start.1 = ((bf16[8,2,512,128]{3,2,1,0:T(8,128)(2,1)}), bf16[8,2,512,128]{3,2,1,0:T(8,128)(2,1)}, u32[]{:S(2)}, u32[]{:S(2)}) async-start(bf16[8,2,512,128]{3,2,1,0:T(8,128)(2,1)} %renew.5), calls=%async_computation.1 | async-start | bytes 4194304 | tf_op jit(solution)/shard_map/all_to_all | solution.py:411
  104.8 4.1 %zeros.1.refs_3_ = bf16[2,32,512,128]{3,2,1,0:T(8,128)(2,1)} custom-call(s32[2]{0:T(128)} %pad_add_fusion.1.refs_0_, s32[8,6]{1,0:T(8,128)} %bitcast.177, bf16[2,512,128]{2,1,0:T(8,128)(2,1)} %collective-permute-done.72.refs_7_.refs_2_), custom_call_target="tpu_custom_call" | custom-call | tf_op jit(solution)/shard_map/zeros/pallas_call | solution.py:358
  108.9 44.9 %all-to-all-done.1.refs_2_ = bf16[8,2,512,128]{3,2,1,0:T(8,128)(2,1)} async-done(((bf16[8,2,512,128]{3,2,1,0:T(8,128)(2,1)}), bf16[8,2,512,128]{3,2,1,0:T(8,128)(2,1)}, u32[]{:S(2)}, u32[]{:S(2)}) %all-to-all-start.1) | async-done | bytes 2097184 | tf_op jit(solution)/shard_map/all_to_all | solution.py:411
  153.8 3.9 %write.1 = bf16[2,32,512,128]{3,2,1,0:T(8,128)(2,1)} custom-call(s32[2]{0:T(128)} %pad_add_fusion.1.refs_0_, s32[8,6]{1,0:T(8,128)} %bitcast.178, bf16[8,2,512,128]{3,2,1,0:T(8,128)(2,1)} %all-to-all-done.1.refs_2_, bf16[2,32,512,128]{3,2,1,0:T(8,128)(2,1)} %zeros.1.refs_3_), custom_call_target="tpu_custom_call", output_to_operand_aliasing={{}: (3, {})} | custom-call | tf_op jit(solution)/shard_map/write/pallas_call | solution.py:412
  (11 shorter events, 0.1 us)
Async XLA Ops:
  0.8 0.6 copy-start
  9.3 17.3 %all-to-all-start = ((s32[32,1,54]{2,1,0:T(1,128)}), s32[32,1,54]{2,1,0:T(1,128)S(1)}, u32[]{:S(2)}, u32[]{:S(2)}) async-start(s32[32,1,54]{2,1,0:T(1,128)} %broadcast_in_dim.15), calls=%async_computation | async-start | bytes 32768 | tf_op jit(solution)/shard_map/all_to_all | solution.py:310
  15.4 18.9 %collective-permute-start.72 = (bf16[2,512,128]{2,1,0:T(8,128)(2,1)}, bf16[2,512,128]{2,1,0:T(8,128)(2,1)}, u32[]{:S(2)}, u32[]{:S(2)}) collective-permute-start(bf16[2,512,128]{2,1,0:T(8,128)(2,1)} %get-tuple-element.684), channel_id=1, source_target_pairs={{0,8},{1,9},{2,10},{3,11},{4,12},{5,13},{6,14},{7,15},{8,16},{9,17... | collective-permute-start | bytes 786440 | tf_op jit(solution)/shard_map/ppermute | solution.py:304
  18.8 30.9 %collective-permute-start.73 = (bf16[2,512,128]{2,1,0:T(8,128)(2,1)}, bf16[2,512,128]{2,1,0:T(8,128)(2,1)}, u32[]{:S(2)}, u32[]{:S(2)}) collective-permute-start(bf16[2,512,128]{2,1,0:T(8,128)(2,1)} %get-tuple-element.685), channel_id=1, source_target_pairs={{0,9},{1,10},{2,11},{3,12},{4,13},{5,14},{6,15},{7,8},{8,17},{9,18... | collective-permute-start | bytes 786440 | tf_op jit(solution)/shard_map/ppermute | solution.py:304
  20.7 30.9 %collective-permute-start.74 = (bf16[2,512,128]{2,1,0:T(8,128)(2,1)}, bf16[2,512,128]{2,1,0:T(8,128)(2,1)}, u32[]{:S(2)}, u32[]{:S(2)}) collective-permute-start(bf16[2,512,128]{2,1,0:T(8,128)(2,1)} %get-tuple-element.686), channel_id=1, source_target_pairs={{0,10},{1,11},{2,12},{3,13},{4,14},{5,15},{6,8},{7,9},{8,18},{9,19... | collective-permute-start | bytes 786440 | tf_op jit(solution)/shard_map/ppermute | solution.py:304
  22.7 38.1 %collective-permute-start.75 = (bf16[2,512,128]{2,1,0:T(8,128)(2,1)}, bf16[2,512,128]{2,1,0:T(8,128)(2,1)}, u32[]{:S(2)}, u32[]{:S(2)}) collective-permute-start(bf16[2,512,128]{2,1,0:T(8,128)(2,1)} %get-tuple-element.687), channel_id=1, source_target_pairs={{0,11},{1,12},{2,13},{3,14},{4,15},{5,8},{6,9},{7,10},{8,19},{9,20... | collective-permute-start | bytes 786440 | tf_op jit(solution)/shard_map/ppermute | solution.py:304
  24.6 36.2 %collective-permute-start.76 = (bf16[2,512,128]{2,1,0:T(8,128)(2,1)}, bf16[2,512,128]{2,1,0:T(8,128)(2,1)}, u32[]{:S(2)}, u32[]{:S(2)}) collective-permute-start(bf16[2,512,128]{2,1,0:T(8,128)(2,1)} %get-tuple-element.688), channel_id=1, source_target_pairs={{0,12},{1,13},{2,14},{3,15},{4,8},{5,9},{6,10},{7,11},{8,20},{9,21... | collective-permute-start | bytes 786440 | tf_op jit(solution)/shard_map/ppermute | solution.py:304
  34.3 26.5 %collective-permute-start.77 = (bf16[2,512,128]{2,1,0:T(8,128)(2,1)}, bf16[2,512,128]{2,1,0:T(8,128)(2,1)}, u32[]{:S(2)}, u32[]{:S(2)}) collective-permute-start(bf16[2,512,128]{2,1,0:T(8,128)(2,1)} %get-tuple-element.689), channel_id=1, source_target_pairs={{0,13},{1,14},{2,15},{3,8},{4,9},{5,10},{6,11},{7,12},{8,21},{9,22... | collective-permute-start | bytes 786440 | tf_op jit(solution)/shard_map/ppermute | solution.py:304
  49.7 16.6 %collective-permute-start.78 = (bf16[2,512,128]{2,1,0:T(8,128)(2,1)}, bf16[2,512,128]{2,1,0:T(8,128)(2,1)}, u32[]{:S(2)}, u32[]{:S(2)}) collective-permute-start(bf16[2,512,128]{2,1,0:T(8,128)(2,1)} %get-tuple-element.690), channel_id=1, source_target_pairs={{0,14},{1,15},{2,8},{3,9},{4,10},{5,11},{6,12},{7,13},{8,22},{9,23... | collective-permute-start | bytes 786440 | tf_op jit(solution)/shard_map/ppermute | solution.py:304
  51.7 20.2 %collective-permute-start.79 = (bf16[2,512,128]{2,1,0:T(8,128)(2,1)}, bf16[2,512,128]{2,1,0:T(8,128)(2,1)}, u32[]{:S(2)}, u32[]{:S(2)}) collective-permute-start(bf16[2,512,128]{2,1,0:T(8,128)(2,1)} %get-tuple-element.691), channel_id=1, source_target_pairs={{0,15},{1,8},{2,9},{3,10},{4,11},{5,12},{6,13},{7,14},{8,23},{9,16... | collective-permute-start | bytes 786440 | tf_op jit(solution)/shard_map/ppermute | solution.py:304
  77.8 11.5 %collective-permute-start.44 = (bf16[2,512,128]{2,1,0:T(8,128)(2,1)S(1)}, bf16[2,512,128]{2,1,0:T(8,128)(2,1)}, u32[]{:S(2)}, u32[]{:S(2)}) collective-permute-start(bf16[2,512,128]{2,1,0:T(8,128)(2,1)S(1)} %dynamic-slice_bitcast_fusion.44), channel_id=1, source_target_pairs={{0,15},{1,8},{2,9},{3,10},{4,11},{5,12},{6,13},{7,14},{8,23},{9,16... | collective-permute-start | bytes 786440 | tf_op jit(solution)/shard_map/cond/branch_8_fun/ppermute | solution.py:376
  100.4 53.4 %all-to-all-start.1 = ((bf16[8,2,512,128]{3,2,1,0:T(8,128)(2,1)}), bf16[8,2,512,128]{3,2,1,0:T(8,128)(2,1)}, u32[]{:S(2)}, u32[]{:S(2)}) async-start(bf16[8,2,512,128]{3,2,1,0:T(8,128)(2,1)} %renew.5), calls=%async_computation.1 | async-start | bytes 4194304 | tf_op jit(solution)/shard_map/all_to_all | solution.py:411
where the time goes:
time: 159 us; the launch traced here: 158 us
  waiting for transfers between devices  70.6 us (44%)
  starting transfers between devices  43 us (27%)
  Pallas kernels  24.9 us (16%)
  other arithmetic  6.64 us (4%)
  local copies, waits for them, and re-layouts  6.43 us (4%)
  between operations  5.38 us (3%)
    all_to_all x1, waiting for transfers between devices, body(): lax.all_to_all(kept, 'trace', split_axis=0, concat_axis=0, tiled=True)  44.9 us
    ppermute x8, starting transfers between devices, body(): recv.append(lax.ppermute(slots[step], AXES, pairs(step)))  30.3 us
    ppermute x8, waiting for transfers between devices, body(): recv.append(lax.ppermute(slots[step], AXES, pairs(step)))  16.3 us
    pallas_call x3, Pallas kernels, renew(): pl.pallas_call(lambda *refs: renew_kernel(senders, owned, *refs), out_sha...  12.1 us
    ppermute x1, waiting for transfers between devices, again(): return lax.ppermute(sent, AXES, pairs(step))  9.26 us
    all_to_all x1, starting transfers between devices, body(): known = lax.all_to_all(mine, AXES, split_axis=0, concat_axis=0, tiled=True)  6.11 us
    pallas_call x1, Pallas kernels, body(): pl.pallas_call(lambda *refs: first_kernel(senders, owned, *refs), out_sha...  4.81 us
    all_to_all x1, starting transfers between devices, body(): lax.all_to_all(kept, 'trace', split_axis=0, concat_axis=0, tiled=True)  4.38 us
  transfers between devices with their start and end apart: 11, of which 5 were waited for; matrix products, arithmetic and copies ran while one was open for 3% of the time, Pallas kernels for 3%

commit v1 on v0

--- a/solution.py
+++ b/solution.py
@@ -392,8 +392,8 @@
         else:
 
             def resend_one(carry):
-                left, recv = carry
-                step = jnp.argmax(left).astype(jnp.int32)
+                left, mask, recv = carry
+                step = jnp.argmax(mask).astype(jnp.int32)
                 recv = lax.switch(
                     step,
                     [
@@ -403,9 +403,9 @@
                     kept,
                     recv,
                 )
-                return jnp.where(steps == step, 0, left), recv
-
-            recv = list(lax.while_loop(lambda carry: jnp.max(carry[0]) > 0, resend_one, (mask, tuple(recv)))[1])
+                return left - 1, jnp.where(steps == step, 0, mask), recv
+
+            recv = list(lax.while_loop(lambda carry: carry[0] > 0, resend_one, (jnp.sum(mask), mask, tuple(recv)))[2])
         kept = renew(kept, jnp.max(mask))
 
     arrived = lax.all_to_all(kept, "trace", split_axis=0, concat_axis=0, tiled=True)

time: 159 us -> 158 us (level)
    reduce_max x2 -> x0, other arithmetic: 2.04 us -> none  [the longest x1 1.34 us: body(): jnp.max(carry[0]) > 0]
where the time goes in v1:
time: 158 us; the launch traced here: 157 us
  waiting for transfers between devices  70.5 us (45%)
  starting transfers between devices  43 us (27%)
  Pallas kernels  24.9 us (16%)
  local copies, waits for them, and re-layouts  6.43 us (4%)
  between operations  5.38 us (3%)
  other arithmetic  5.34 us (3%)
    all_to_all x1, waiting for transfers between devices, body(): lax.all_to_all(kept, 'trace', split_axis=0, concat_axis=0, tiled=True)  44.9 us
    ppermute x8, starting transfers between devices, body(): recv.append(lax.ppermute(slots[step], AXES, pairs(step)))  30.3 us
    ppermute x8, waiting for transfers between devices, body(): recv.append(lax.ppermute(slots[step], AXES, pairs(step)))  16.3 us
    pallas_call x3, Pallas kernels, renew(): pl.pallas_call(lambda *refs: renew_kernel(senders, owned, *refs), out_sha...  12.1 us
    ppermute x1, waiting for transfers between devices, again(): return lax.ppermute(sent, AXES, pairs(step))  9.26 us
    all_to_all x1, starting transfers between devices, body(): known = lax.all_to_all(mine, AXES, split_axis=0, concat_axis=0, tiled=True)  6.11 us
    pallas_call x1, Pallas kernels, body(): pl.pallas_call(lambda *refs: first_kernel(senders, owned, *refs), out_sha...  4.81 us
    all_to_all x1, starting transfers between devices, body(): lax.all_to_all(kept, 'trace', split_axis=0, concat_axis=0, tiled=True)  4.38 us
  transfers between devices with their start and end apart: 11, of which 5 were waited for; matrix products, arithmetic and copies ran while one was open for 3% of the time, Pallas kernels for 3%

profile of v1, /device:TPU:4, one launch (start us, length us, event | category | flops | bytes accessed | tf_op | source)
XLA Modules:
  0.0 156.5 jit_solution(6256571247095346745)
XLA Ops:
  0.0 0.8 copy.18
  0.8 0.0 copy-start
  0.8 0.6 copy-done
  1.3 0.1 reshape_squeeze.3
  1.4 0.6 pad_add_fusion.1.refs_0_
  2.0 1.3 pad_add_fusion.2
  3.3 4.8 %first.1 = (bf16[2,512,128]{2,1,0:T(8,128)(2,1)}, bf16[2,512,128]{2,1,0:T(8,128)(2,1)}, bf16[2,512,128]{2,1,0:T(8,128)(2,1)}, bf16[2,512,128]{2,1,0:T(8,128)(2,1...) custom-call(s32[2]{0:T(128)} %pad_add_fusion.1.refs_0_, ...), custom_call_target="tpu_custom_call" | custom-call | tf_op jit(solution)/shard_map/first/pallas_call | solution.py:285
  8.1 1.2 broadcast_in_dim.19
  9.3 6.1 %all-to-all-start = ((s32[32,1,54]{2,1,0:T(1,128)}), s32[32,1,54]{2,1,0:T(1,128)S(1)}, u32[]{:S(2)}, u32[]{:S(2)}) async-start(s32[32,1,54]{2,1,0:T(1,128)} %broadcast_in_dim.19), calls=%async_computation | async-start | bytes 32768 | tf_op jit(solution)/shard_map/all_to_all | solution.py:310
  15.4 3.4 %collective-permute-start.72 = (bf16[2,512,128]{2,1,0:T(8,128)(2,1)}, bf16[2,512,128]{2,1,0:T(8,128)(2,1)}, u32[]{:S(2)}, u32[]{:S(2)}) collective-permute-start(bf16[2,512,128]{2,1,0:T(8,128)(2,1)} %get-tuple-element.799), channel_id=1, source_target_pairs={{0,8},{1,9},{2,10},{3,11},{4,12},{5,13},{6,14},{7,15},{8,16},{9,17... | collective-permute-start | bytes 786440 | tf_op jit(solution)/shard_map/ppermute | solution.py:304
  18.8 1.9 %collective-permute-start.73 = (bf16[2,512,128]{2,1,0:T(8,128)(2,1)}, bf16[2,512,128]{2,1,0:T(8,128)(2,1)}, u32[]{:S(2)}, u32[]{:S(2)}) collective-permute-start(bf16[2,512,128]{2,1,0:T(8,128)(2,1)} %get-tuple-element.800), channel_id=1, source_target_pairs={{0,9},{1,10},{2,11},{3,12},{4,13},{5,14},{6,15},{7,8},{8,17},{9,18... | collective-permute-start | bytes 786440 | tf_op jit(solution)/shard_map/ppermute | solution.py:304
  20.7 1.9 %collective-permute-start.74 = (bf16[2,512,128]{2,1,0:T(8,128)(2,1)}, bf16[2,512,128]{2,1,0:T(8,128)(2,1)}, u32[]{:S(2)}, u32[]{:S(2)}) collective-permute-start(bf16[2,512,128]{2,1,0:T(8,128)(2,1)} %get-tuple-element.801), channel_id=1, source_target_pairs={{0,10},{1,11},{2,12},{3,13},{4,14},{5,15},{6,8},{7,9},{8,18},{9,19... | collective-permute-start | bytes 786440 | tf_op jit(solution)/shard_map/ppermute | solution.py:304
  22.7 1.9 %collective-permute-start.75 = (bf16[2,512,128]{2,1,0:T(8,128)(2,1)}, bf16[2,512,128]{2,1,0:T(8,128)(2,1)}, u32[]{:S(2)}, u32[]{:S(2)}) collective-permute-start(bf16[2,512,128]{2,1,0:T(8,128)(2,1)} %get-tuple-element.802), channel_id=1, source_target_pairs={{0,11},{1,12},{2,13},{3,14},{4,15},{5,8},{6,9},{7,10},{8,19},{9,20... | collective-permute-start | bytes 786440 | tf_op jit(solution)/shard_map/ppermute | solution.py:304
  24.6 1.9 %collective-permute-start.76 = (bf16[2,512,128]{2,1,0:T(8,128)(2,1)}, bf16[2,512,128]{2,1,0:T(8,128)(2,1)}, u32[]{:S(2)}, u32[]{:S(2)}) collective-permute-start(bf16[2,512,128]{2,1,0:T(8,128)(2,1)} %get-tuple-element.803), channel_id=1, source_target_pairs={{0,12},{1,13},{2,14},{3,15},{4,8},{5,9},{6,10},{7,11},{8,20},{9,21... | collective-permute-start | bytes 786440 | tf_op jit(solution)/shard_map/ppermute | solution.py:304
  26.5 0.1 sub.28
  26.6 0.0 all-to-all-done
  26.6 0.1 slice.60
  26.7 0.1 eq.148
  26.8 0.1 compare_reduce_fusion.1
  26.9 0.2 fusion.2
  27.2 0.2 fusion.6
  27.4 0.1 eq.142
  27.5 0.7 fusion.11
  28.1 0.9 and_reduce_fusion
  29.0 5.2 %collective-permute-done.72.refs_7_.refs_2_ = bf16[2,512,128]{2,1,0:T(8,128)(2,1)} collective-permute-done((bf16[2,512,128]{2,1,0:T(8,128)(2,1)}, bf16[2,512,128]{2,1,0:T(8,128)(2,1)}, u32[]{:S(2)}, u32[]{:S(2)}) %collective-permute-start.72) | collective-permute-done | bytes 262176 | tf_op jit(solution)/shard_map/ppermute | solution.py:304
  34.3 15.4 %collective-permute-start.77 = (bf16[2,512,128]{2,1,0:T(8,128)(2,1)}, bf16[2,512,128]{2,1,0:T(8,128)(2,1)}, u32[]{:S(2)}, u32[]{:S(2)}) collective-permute-start(bf16[2,512,128]{2,1,0:T(8,128)(2,1)} %get-tuple-element.804), channel_id=1, source_target_pairs={{0,13},{1,14},{2,15},{3,8},{4,9},{5,10},{6,11},{7,12},{8,21},{9,22... | collective-permute-start | bytes 786440 | tf_op jit(solution)/shard_map/ppermute | solution.py:304
  49.7 0.0 collective-permute-done.73.refs_8_
  49.7 1.9 %collective-permute-start.78 = (bf16[2,512,128]{2,1,0:T(8,128)(2,1)}, bf16[2,512,128]{2,1,0:T(8,128)(2,1)}, u32[]{:S(2)}, u32[]{:S(2)}) collective-permute-start(bf16[2,512,128]{2,1,0:T(8,128)(2,1)} %get-tuple-element.805), channel_id=1, source_target_pairs={{0,14},{1,15},{2,8},{3,9},{4,10},{5,11},{6,12},{7,13},{8,22},{9,23... | collective-permute-start | bytes 786440 | tf_op jit(solution)/shard_map/ppermute | solution.py:304
  51.6 0.0 collective-permute-done.74.refs_9_
  51.7 1.9 %collective-permute-start.79 = (bf16[2,512,128]{2,1,0:T(8,128)(2,1)}, bf16[2,512,128]{2,1,0:T(8,128)(2,1)}, u32[]{:S(2)}, u32[]{:S(2)}) collective-permute-start(bf16[2,512,128]{2,1,0:T(8,128)(2,1)} %get-tuple-element.806), channel_id=1, source_target_pairs={{0,15},{1,8},{2,9},{3,10},{4,11},{5,12},{6,13},{7,14},{8,23},{9,16... | collective-permute-start | bytes 786440 | tf_op jit(solution)/shard_map/ppermute | solution.py:304
  53.6 0.5 convert_element_type.10
  54.2 0.1 add_reduce_fusion
  54.3 0.1 copy.20
  59.4 0.7 pad_add_fusion.refs_3_
  60.1 0.7 convert_reduce_fusion.2
  60.8 0.0 collective-permute-done.75.refs_10_
  60.8 0.0 collective-permute-done.76.refs_11_
  60.8 0.0 collective-permute-done.77.refs_12_
  60.8 5.5 %collective-permute-done.78.refs_13_ = bf16[2,512,128]{2,1,0:T(8,128)(2,1)} collective-permute-done((bf16[2,512,128]{2,1,0:T(8,128)(2,1)}, bf16[2,512,128]{2,1,0:T(8,128)(2,1)}, u32[]{:S(2)}, u32[]{:S(2)}) %collective-permute-start.78) | collective-permute-done | bytes 262176 | tf_op jit(solution)/shard_map/ppermute | solution.py:304
  66.3 5.5 %collective-permute-done.79.refs_14_ = bf16[2,512,128]{2,1,0:T(8,128)(2,1)} collective-permute-done((bf16[2,512,128]{2,1,0:T(8,128)(2,1)}, bf16[2,512,128]{2,1,0:T(8,128)(2,1)}, u32[]{:S(2)}, u32[]{:S(2)}) %collective-permute-start.79) | collective-permute-done | bytes 262176 | tf_op jit(solution)/shard_map/ppermute | solution.py:304
  71.9 4.9 %renew.3.refs_15_ = bf16[8,2,512,128]{3,2,1,0:T(8,128)(2,1)} custom-call(s32[2]{0:T(128)} %pad_add_fusion.1.refs_0_, s32[8,6]{1,0:T(8,128)} %bitcast.174, s32[6]{0:T(128)} %bitcast.187, s32[7,9]{1,0:T(8,128)} %pad_add_fusion.refs_3_, s32[1]{0:T(128)} %constant.916.clone.1.refs_4_, ...), custom_call_target="tpu_custom_call", output_to_operand_aliasing={{}: (15, {})} | custom-call | tf_op jit(solution)/shard_map/renew/pallas_call | solution.py:337
  76.8 12.5 %conditional.4 = ((bf16[2,512,128]{2,1,0:T(8,128)(2,1)}, bf16[2,512,128]{2,1,0:T(8,128)(2,1)}, bf16[2,512,128]{2,1,0:T(8,128)(2,1)}, bf16[2,512,128]{2,1,0:T(8,128)(2,1)})) conditional(s32[]{:T(128)} %bitcast.83, (bf16[2,512,128]{2,1,0:T(8,128)(2,1)}, bf16[2,512,128]{2,1,0:T(8,128)(2,1)}, ...), branch_computations={%region_26.27_spmd, %region_27.28_spmd, %region_28.29_spmd, %regio... | conditional | flops 60 | bytes 6292292 | solution.py:389
  76.8 1.0 dynamic-slice_bitcast_fusion.44
  77.8 2.2 %collective-permute-start.44 = (bf16[2,512,128]{2,1,0:T(8,128)(2,1)S(1)}, bf16[2,512,128]{2,1,0:T(8,128)(2,1)}, u32[]{:S(2)}, u32[]{:S(2)}) collective-permute-start(bf16[2,512,128]{2,1,0:T(8,128)(2,1)S(1)} %dynamic-slice_bitcast_fusion.44), channel_id=1, source_target_pairs={{0,15},{1,8},{2,9},{3,10},{4,11},{5,12},{6,13},{7,14},{8,23},{9,16... | collective-permute-start | bytes 786440 | tf_op jit(solution)/shard_map/cond/branch_8_fun/ppermute | solution.py:376
  80.0 9.3 %collective-permute-done.44 = bf16[2,512,128]{2,1,0:T(8,128)(2,1)} collective-permute-done((bf16[2,512,128]{2,1,0:T(8,128)(2,1)S(1)}, bf16[2,512,128]{2,1,0:T(8,128)(2,1)}, u32[]{:S(2)}, u32[]{:S(2)}) %collective-permute-start.44) | collective-permute-done | bytes 262176 | tf_op jit(solution)/shard_map/cond/branch_8_fun/ppermute | solution.py:376
  89.3 1.7 %conditional.3 = (bf16[2,512,128]{2,1,0:T(8,128)(2,1)}, bf16[2,512,128]{2,1,0:T(8,128)(2,1)}, bf16[2,512,128]{2,1,0:T(8,128)(2,1)}, bf16[2,512,128]{2,1,0:T(8,128)(2,1)}) conditional(s32[]{:T(128)} %bitcast.82, (bf16[2,512,128]{2,1,0:T(8,128)(2,1)}, bf16[2,512,128]{2,1,0:T(8,128)(2,1)}, ...), branch_computations={%region_10.11_spmd, %region_11.12_spmd, %region_12.13_spmd, %regio... | conditional | flops 59 | bytes 6292272 | solution.py:389
  89.3 1.7 %copy.91 = bf16[2,512,128]{2,1,0:T(8,128)(2,1)} copy(bf16[2,512,128]{2,1,0:T(8,128)(2,1)} %get-tuple-element.1111) | data formatting | bytes 524288 | tf_op jit(solution)/shard_map/cond
  91.0 5.5 %renew.4.refs_15_ = bf16[8,2,512,128]{3,2,1,0:T(8,128)(2,1)} custom-call(s32[2]{0:T(128)} %pad_add_fusion.1.refs_0_, s32[8,6]{1,0:T(8,128)} %bitcast.175, s32[6]{0:T(128)} %bitcast.188, s32[7,9]{1,0:T(8,128)} %pad_add_fusion.refs_3_, s32[1]{0:T(128)} %bitcast.84.refs_4_, bf16[2,32,512,128]{3,2,1,0:T(8,128)(2,1)} %bitcast.167, ...), custom_call_target="tpu_custom_call", output_to_operand_aliasing={{}: (15, {})} | custom-call | tf_op jit(solution)/shard_map/renew/pallas_call | solution.py:337
  96.5 0.9 while.29
  97.4 1.7 %renew.5 = bf16[8,2,512,128]{3,2,1,0:T(8,128)(2,1)} custom-call(s32[2]{0:T(128)} %pad_add_fusion.1.refs_0_, s32[8,6]{1,0:T(8,128)} %bitcast.176, s32[6]{0:T(128)} %bitcast.189, s32[7,9]{1,0:T(8,128)} %pad_add_fusion.refs_3_, s32[1]{0:T(128)} %bitcast.81.refs_4_, bf16[2,32,512,128]{3,2,1,0:T(8,128)(2,1)} %bitcast.168, ...), custom_call_target="tpu_custom_call", output_to_operand_aliasing={{}: (15, {})} | custom-call | tf_op jit(solution)/shard_map/renew/pallas_call | solution.py:337
  99.0 4.4 %all-to-all-start.1 = ((bf16[8,2,512,128]{3,2,1,0:T(8,128)(2,1)}), bf16[8,2,512,128]{3,2,1,0:T(8,128)(2,1)}, u32[]{:S(2)}, u32[]{:S(2)}) async-start(bf16[8,2,512,128]{3,2,1,0:T(8,128)(2,1)} %renew.5), calls=%async_computation.1 | async-start | bytes 4194304 | tf_op jit(solution)/shard_map/all_to_all | solution.py:411
  103.4 4.1 %zeros.1.refs_3_ = bf16[2,32,512,128]{3,2,1,0:T(8,128)(2,1)} custom-call(s32[2]{0:T(128)} %pad_add_fusion.1.refs_0_, s32[8,6]{1,0:T(8,128)} %bitcast.177, bf16[2,512,128]{2,1,0:T(8,128)(2,1)} %collective-permute-done.72.refs_7_.refs_2_), custom_call_target="tpu_custom_call" | custom-call | tf_op jit(solution)/shard_map/zeros/pallas_call | solution.py:358
  107.5 44.9 %all-to-all-done.1.refs_2_ = bf16[8,2,512,128]{3,2,1,0:T(8,128)(2,1)} async-done(((bf16[8,2,512,128]{3,2,1,0:T(8,128)(2,1)}), bf16[8,2,512,128]{3,2,1,0:T(8,128)(2,1)}, u32[]{:S(2)}, u32[]{:S(2)}) %all-to-all-start.1) | async-done | bytes 2097184 | tf_op jit(solution)/shard_map/all_to_all | solution.py:411
  152.5 3.9 %write.1 = bf16[2,32,512,128]{3,2,1,0:T(8,128)(2,1)} custom-call(s32[2]{0:T(128)} %pad_add_fusion.1.refs_0_, s32[8,6]{1,0:T(8,128)} %bitcast.178, bf16[8,2,512,128]{3,2,1,0:T(8,128)(2,1)} %all-to-all-done.1.refs_2_, bf16[2,32,512,128]{3,2,1,0:T(8,128)(2,1)} %zeros.1.refs_3_), custom_call_target="tpu_custom_call", output_to_operand_aliasing={{}: (3, {})} | custom-call | tf_op jit(solution)/shard_map/write/pallas_call | solution.py:412
  (11 shorter events, 0.1 us)
Async XLA Ops:
  0.8 0.6 copy-start
  9.3 17.3 %all-to-all-start = ((s32[32,1,54]{2,1,0:T(1,128)}), s32[32,1,54]{2,1,0:T(1,128)S(1)}, u32[]{:S(2)}, u32[]{:S(2)}) async-start(s32[32,1,54]{2,1,0:T(1,128)} %broadcast_in_dim.19), calls=%async_computation | async-start | bytes 32768 | tf_op jit(solution)/shard_map/all_to_all | solution.py:310
  15.4 18.9 %collective-permute-start.72 = (bf16[2,512,128]{2,1,0:T(8,128)(2,1)}, bf16[2,512,128]{2,1,0:T(8,128)(2,1)}, u32[]{:S(2)}, u32[]{:S(2)}) collective-permute-start(bf16[2,512,128]{2,1,0:T(8,128)(2,1)} %get-tuple-element.799), channel_id=1, source_target_pairs={{0,8},{1,9},{2,10},{3,11},{4,12},{5,13},{6,14},{7,15},{8,16},{9,17... | collective-permute-start | bytes 786440 | tf_op jit(solution)/shard_map/ppermute | solution.py:304
  18.8 30.9 %collective-permute-start.73 = (bf16[2,512,128]{2,1,0:T(8,128)(2,1)}, bf16[2,512,128]{2,1,0:T(8,128)(2,1)}, u32[]{:S(2)}, u32[]{:S(2)}) collective-permute-start(bf16[2,512,128]{2,1,0:T(8,128)(2,1)} %get-tuple-element.800), channel_id=1, source_target_pairs={{0,9},{1,10},{2,11},{3,12},{4,13},{5,14},{6,15},{7,8},{8,17},{9,18... | collective-permute-start | bytes 786440 | tf_op jit(solution)/shard_map/ppermute | solution.py:304
  20.7 30.9 %collective-permute-start.74 = (bf16[2,512,128]{2,1,0:T(8,128)(2,1)}, bf16[2,512,128]{2,1,0:T(8,128)(2,1)}, u32[]{:S(2)}, u32[]{:S(2)}) collective-permute-start(bf16[2,512,128]{2,1,0:T(8,128)(2,1)} %get-tuple-element.801), channel_id=1, source_target_pairs={{0,10},{1,11},{2,12},{3,13},{4,14},{5,15},{6,8},{7,9},{8,18},{9,19... | collective-permute-start | bytes 786440 | tf_op jit(solution)/shard_map/ppermute | solution.py:304
  22.7 38.1 %collective-permute-start.75 = (bf16[2,512,128]{2,1,0:T(8,128)(2,1)}, bf16[2,512,128]{2,1,0:T(8,128)(2,1)}, u32[]{:S(2)}, u32[]{:S(2)}) collective-permute-start(bf16[2,512,128]{2,1,0:T(8,128)(2,1)} %get-tuple-element.802), channel_id=1, source_target_pairs={{0,11},{1,12},{2,13},{3,14},{4,15},{5,8},{6,9},{7,10},{8,19},{9,20... | collective-permute-start | bytes 786440 | tf_op jit(solution)/shard_map/ppermute | solution.py:304
  24.6 36.2 %collective-permute-start.76 = (bf16[2,512,128]{2,1,0:T(8,128)(2,1)}, bf16[2,512,128]{2,1,0:T(8,128)(2,1)}, u32[]{:S(2)}, u32[]{:S(2)}) collective-permute-start(bf16[2,512,128]{2,1,0:T(8,128)(2,1)} %get-tuple-element.803), channel_id=1, source_target_pairs={{0,12},{1,13},{2,14},{3,15},{4,8},{5,9},{6,10},{7,11},{8,20},{9,21... | collective-permute-start | bytes 786440 | tf_op jit(solution)/shard_map/ppermute | solution.py:304
  34.3 26.5 %collective-permute-start.77 = (bf16[2,512,128]{2,1,0:T(8,128)(2,1)}, bf16[2,512,128]{2,1,0:T(8,128)(2,1)}, u32[]{:S(2)}, u32[]{:S(2)}) collective-permute-start(bf16[2,512,128]{2,1,0:T(8,128)(2,1)} %get-tuple-element.804), channel_id=1, source_target_pairs={{0,13},{1,14},{2,15},{3,8},{4,9},{5,10},{6,11},{7,12},{8,21},{9,22... | collective-permute-start | bytes 786440 | tf_op jit(solution)/shard_map/ppermute | solution.py:304
  49.7 16.6 %collective-permute-start.78 = (bf16[2,512,128]{2,1,0:T(8,128)(2,1)}, bf16[2,512,128]{2,1,0:T(8,128)(2,1)}, u32[]{:S(2)}, u32[]{:S(2)}) collective-permute-start(bf16[2,512,128]{2,1,0:T(8,128)(2,1)} %get-tuple-element.805), channel_id=1, source_target_pairs={{0,14},{1,15},{2,8},{3,9},{4,10},{5,11},{6,12},{7,13},{8,22},{9,23... | collective-permute-start | bytes 786440 | tf_op jit(solution)/shard_map/ppermute | solution.py:304
  51.7 20.2 %collective-permute-start.79 = (bf16[2,512,128]{2,1,0:T(8,128)(2,1)}, bf16[2,512,128]{2,1,0:T(8,128)(2,1)}, u32[]{:S(2)}, u32[]{:S(2)}) collective-permute-start(bf16[2,512,128]{2,1,0:T(8,128)(2,1)} %get-tuple-element.806), channel_id=1, source_target_pairs={{0,15},{1,8},{2,9},{3,10},{4,11},{5,12},{6,13},{7,14},{8,23},{9,16... | collective-permute-start | bytes 786440 | tf_op jit(solution)/shard_map/ppermute | solution.py:304
  77.8 11.5 %collective-permute-start.44 = (bf16[2,512,128]{2,1,0:T(8,128)(2,1)S(1)}, bf16[2,512,128]{2,1,0:T(8,128)(2,1)}, u32[]{:S(2)}, u32[]{:S(2)}) collective-permute-start(bf16[2,512,128]{2,1,0:T(8,128)(2,1)S(1)} %dynamic-slice_bitcast_fusion.44), channel_id=1, source_target_pairs={{0,15},{1,8},{2,9},{3,10},{4,11},{5,12},{6,13},{7,14},{8,23},{9,16... | collective-permute-start | bytes 786440 | tf_op jit(solution)/shard_map/cond/branch_8_fun/ppermute | solution.py:376
  99.0 53.4 %all-to-all-start.1 = ((bf16[8,2,512,128]{3,2,1,0:T(8,128)(2,1)}), bf16[8,2,512,128]{3,2,1,0:T(8,128)(2,1)}, u32[]{:S(2)}, u32[]{:S(2)}) async-start(bf16[8,2,512,128]{3,2,1,0:T(8,128)(2,1)} %renew.5), calls=%async_computation.1 | async-start | bytes 4194304 | tf_op jit(solution)/shard_map/all_to_all | solution.py:411

commit v2 on v1

--- a/solution.py
+++ b/solution.py
@@ -196,7 +196,9 @@
                 put(batch, row).wait()
 
 
-def write_kernel(owned, senders, stored, batches, state, rows, recv, old, out, arrived, total, made, here, in_sem, out_sem):
+def write_kernel(owned, senders, stored, batches, state, rows, fixed, recv, *refs):
+    fixes, refs = refs[:senders], refs[senders:]
+    _, out, arrived, total, made, here, in_sem, out_sem = refs
     hit_rows(rows, senders, state[0], owned, stored, here)
 
     def take(sender):
@@ -212,11 +214,16 @@
             total += same.astype(jnp.int32)
         return total
 
-    @pl.loop(0, senders)
-    def _(sender):
-        @pl.when(here[sender] >= 0)
+    for step in range(senders):
+        sender = lax.rem(state[0] - step + senders, senders)
+
+        @pl.when((here[sender] >= 0) & (fixed[sender] == 0))
         def _():
             take(sender).start()
+
+        @pl.when((here[sender] >= 0) & (fixed[sender] > 0))
+        def _():
+            pltpu.make_async_copy(fixes[step], arrived.at[sender], in_sem.at[sender]).start()
 
     @pl.loop(0, senders)
     def _(sender):
@@ -275,10 +282,10 @@
     slot = jax.ShapeDtypeStruct(tile, dtype)
     held = jax.ShapeDtypeStruct((senders,) + tile, dtype)
 
-    def pairs(step):
+    def pairs(step, down=1):
         return [
-            (i * senders + j, (i + 1) * senders + (j + step) % senders)
-            for i in range(layers - 1)
+            (i * senders + j, (i + down) * senders + (j + step) % senders)
+            for i in range(layers - down)
             for j in range(senders)
         ]
 
@@ -315,17 +322,25 @@
     feeds = rows_all[:-1, :, None] == cols_all[1:, None, :]
     read = jnp.any(feeds, axis=2)
     home = jnp.repeat(jnp.arange(senders, dtype=jnp.int32), stored)
-    shift = (rows_all[:-1] // owned - home[None, :]) % senders
+    shift_all = (rows_all // owned - home[None, :]) % senders
+    shift = shift_all[:-1]
     steps = jnp.arange(senders, dtype=jnp.int32)
     changed = jnp.any(feeds, axis=1)
+    later = jnp.zeros(changed.shape, bool)
     masks = []
     group = 4 if senders <= 8 else 2
-    for _ in range(2, layers):
+    for wave in range(2, layers):
         below = jnp.concatenate([jnp.zeros((1, blocks_all), bool), changed[:-1]])
         again = below & read
         mask = jnp.any(again[:, :, None] & (shift[:, :, None] == steps), axis=(0, 1)).astype(jnp.int32)
         masks.append(mask)
         changed = jnp.any(feeds & below[:, :, None], axis=1)
+        if wave > 2:
+            later |= changed
+    late_mask = jnp.any(later[:, :, None] & (shift_all[1:, :, None] == steps), axis=(0, 1)).astype(jnp.int32)
+    mine_later = lax.dynamic_index_in_dim(later, jnp.maximum(depth - 1, 0), 0, keepdims=False) & (depth > 0)
+    to_me = (rows // owned == place).reshape(-1) & mine_later
+    fixed = jnp.any(to_me.reshape(senders, stored), axis=1).astype(jnp.int32)
 
     above = lax.dynamic_index_in_dim(rows_all, jnp.maximum(depth - 1, 0), 0, keepdims=False)
     above = above.reshape(senders, stored)
@@ -371,48 +386,47 @@
 
     kept = renew(kept, jnp.int32(1))
 
-    def again(step, kept):
+    def again(step, kept, down=1):
         sent = lax.dynamic_index_in_dim(kept, (place + step) % senders, 0, keepdims=False)
-        return lax.ppermute(sent, AXES, pairs(step))
-
-    for wave, mask in enumerate(masks):
-        if wave == 0:
-            for low in range(0, senders, group):
-                near = range(low, min(low + group, senders))
-
-                def resend(which):
-                    return lambda kept, old: tuple(
-                        again(step, kept) if which >> at & 1 else old[at] for at, step in enumerate(near)
-                    )
-
-                code = sum(mask[step] << at for at, step in enumerate(near))
-                recv[low : low + group] = lax.switch(
-                    code, [resend(which) for which in range(1 << len(near))], kept, tuple(recv[low : low + group])
+        return lax.ppermute(sent, AXES, pairs(step, down))
+
+    def one_by_one(mask, send, came):
+        def resend(carry):
+            left, mask, came = carry
+            step = jnp.argmax(mask).astype(jnp.int32)
+            branches = [
+                lambda came, step=step: came[:step] + (send(step),) + came[step + 1 :] for step in range(senders)
+            ]
+            return left - 1, jnp.where(steps == step, 0, mask), lax.switch(step, branches, came)
+
+        return lax.while_loop(lambda carry: carry[0] > 0, resend, (jnp.sum(mask), mask, tuple(came)))[2]
+
+    if masks:
+        for low in range(0, senders, group):
+            near = range(low, min(low + group, senders))
+
+            def resend(which):
+                return lambda kept, old: tuple(
+                    again(step, kept) if which >> at & 1 else old[at] for at, step in enumerate(near)
                 )
-        else:
-
-            def resend_one(carry):
-                left, mask, recv = carry
-                step = jnp.argmax(mask).astype(jnp.int32)
-                recv = lax.switch(
-                    step,
-                    [
-                        lambda kept, recv, step=step: recv[:step] + (again(step, kept),) + recv[step + 1 :]
-                        for step in range(senders)
-                    ],
-                    kept,
-                    recv,
-                )
-                return left - 1, jnp.where(steps == step, 0, mask), recv
-
-            recv = list(lax.while_loop(lambda carry: carry[0] > 0, resend_one, (jnp.sum(mask), mask, tuple(recv)))[2])
-        kept = renew(kept, jnp.max(mask))
-
+
+            code = sum(masks[0][step] << at for at, step in enumerate(near))
+            recv[low : low + group] = lax.switch(
+                code, [resend(which) for which in range(1 << len(near))], kept, tuple(recv[low : low + group])
+            )
+        kept = renew(kept, jnp.max(masks[0]))
     arrived = lax.all_to_all(kept, "trace", split_axis=0, concat_axis=0, tiled=True)
+
+    late = kept
+    for mask in masks[1:]:
+        recv = list(one_by_one(mask, lambda step, late=late: again(step, late), recv))
+        late = renew(late, jnp.max(mask))
+    fixes = one_by_one(late_mask, lambda step: again(step, late, 0), recv)
+
     traces = pl.pallas_call(
         lambda *refs: write_kernel(owned, senders, stored, batches, *refs),
         out_shape=jax.ShapeDtypeStruct((batches, owned, width, shots), dtype),
-        in_specs=[SMEM, SMEM, ANY, ANY],
+        in_specs=[SMEM] * 3 + [ANY] * (senders + 2),
         out_specs=ANY,
         scratch_shapes=[
             pltpu.VMEM((senders,) + tile, dtype),
@@ -422,10 +436,10 @@
             DMA((senders,)),
             DMA((senders, batches)),
         ],
-        input_output_aliases={3: 0},
+        input_output_aliases={4 + senders: 0},
         compiler_params=PARAMS,
         name="write",
-    )(state, rows, arrived, traces)
+    )(state, rows, fixed, arrived, *fixes, traces)
     return traces.reshape(1, batches, local, shots)
 
 

time: 158 us -> 155 us (0.981)
  waiting for transfers between devices: 70.5 us -> 62.7 us
  other arithmetic: 5.34 us -> 8.27 us
    all_to_all x1, waiting for transfers between devices: 44.9 us -> 39.7 us  [body(): lax.all_to_all(kept, 'trace', split_axis=0, concat_axis=0, tiled=True)]
    ppermute x8, waiting for transfers between devices: 16.3 us -> 13.8 us  [body(): recv.append(lax.ppermute(slots[step], AXES, pairs(step)))]
  transfers between devices with their start and end apart: 11 -> 11, of which waited for: 5 -> 5; matrix products, arithmetic and copies ran while one was open for 3% -> 6% of each run, Pallas kernels for 3% -> 4%
where the time goes in v2:
time: 155 us; the launch traced here: 154 us
  waiting for transfers between devices  62.7 us (40%)
  starting transfers between devices  43.2 us (28%)
  Pallas kernels  25 us (16%)
  other arithmetic  8.27 us (5%)
  local copies, waits for them, and re-layouts  7.97 us (5%)
  between operations  5.58 us (4%)
  loops' own time  1.55 us (1%)
    all_to_all x1, waiting for transfers between devices, body(): lax.all_to_all(kept, 'trace', split_axis=0, concat_axis=0, tiled=True)  39.7 us
    ppermute x8, starting transfers between devices, body(): recv.append(lax.ppermute(slots[step], AXES, pairs(step)))  30.3 us
    ppermute x8, waiting for transfers between devices, body(): recv.append(lax.ppermute(slots[step], AXES, pairs(step)))  13.8 us
    pallas_call x3, Pallas kernels, renew(): pl.pallas_call(lambda *refs: renew_kernel(senders, owned, *refs), out_sha...  12.2 us
    ppermute x1, waiting for transfers between devices, again(): return lax.ppermute(sent, AXES, pairs(step, down))  9.25 us
    all_to_all x1, starting transfers between devices, body(): known = lax.all_to_all(mine, AXES, split_axis=0, concat_axis=0, tiled=True)  6.13 us
    pallas_call x1, Pallas kernels, body(): pl.pallas_call(lambda *refs: first_kernel(senders, owned, *refs), out_sha...  4.8 us
    all_to_all x1, starting transfers between devices, body(): lax.all_to_all(kept, 'trace', split_axis=0, concat_axis=0, tiled=True)  4.5 us
  transfers between devices with their start and end apart: 11, of which 5 were waited for; matrix products, arithmetic and copies ran while one was open for 6% of the time, Pallas kernels for 4%

profile of v2, /device:TPU:4, one launch (start us, length us, event | category | flops | bytes accessed | tf_op | source)
XLA Modules:
  0.0 154.3 jit_solution(13989408791306277249)
XLA Ops:
  0.0 0.8 copy.18
  0.8 0.6 copy-done.1
  1.4 0.1 reshape_squeeze.3
  1.4 0.6 pad_add_fusion.1.refs_0_
  2.0 1.3 pad_add_fusion.2
  3.3 4.8 %first.1 = (bf16[2,512,128]{2,1,0:T(8,128)(2,1)}, bf16[2,512,128]{2,1,0:T(8,128)(2,1)}, bf16[2,512,128]{2,1,0:T(8,128)(2,1)}, bf16[2,512,128]{2,1,0:T(8,128)(2,1...) custom-call(s32[2]{0:T(128)} %pad_add_fusion.1.refs_0_, ...), custom_call_target="tpu_custom_call" | custom-call | tf_op jit(solution)/shard_map/first/pallas_call | solution.py:292
  8.1 1.3 broadcast_in_dim.47
  9.4 6.1 %all-to-all-start = ((s32[32,1,54]{2,1,0:T(1,128)}), s32[32,1,54]{2,1,0:T(1,128)S(1)}, u32[]{:S(2)}, u32[]{:S(2)}) async-start(s32[32,1,54]{2,1,0:T(1,128)} %broadcast_in_dim.47), calls=%async_computation | async-start | bytes 32768 | tf_op jit(solution)/shard_map/all_to_all | solution.py:317
  15.6 3.4 %collective-permute-start.80 = (bf16[2,512,128]{2,1,0:T(8,128)(2,1)}, bf16[2,512,128]{2,1,0:T(8,128)(2,1)}, u32[]{:S(2)}, u32[]{:S(2)}) collective-permute-start(bf16[2,512,128]{2,1,0:T(8,128)(2,1)} %get-tuple-element.1208), channel_id=1, source_target_pairs={{0,8},{1,9},{2,10},{3,11},{4,12},{5,13},{6,14},{7,15},{8,16},{9,17... | collective-permute-start | bytes 786440 | tf_op jit(solution)/shard_map/ppermute | solution.py:311
  19.0 1.9 %collective-permute-start.81 = (bf16[2,512,128]{2,1,0:T(8,128)(2,1)}, bf16[2,512,128]{2,1,0:T(8,128)(2,1)}, u32[]{:S(2)}, u32[]{:S(2)}) collective-permute-start(bf16[2,512,128]{2,1,0:T(8,128)(2,1)} %get-tuple-element.1209), channel_id=1, source_target_pairs={{0,9},{1,10},{2,11},{3,12},{4,13},{5,14},{6,15},{7,8},{8,17},{9,18... | collective-permute-start | bytes 786440 | tf_op jit(solution)/shard_map/ppermute | solution.py:311
  20.9 1.9 %collective-permute-start.82 = (bf16[2,512,128]{2,1,0:T(8,128)(2,1)}, bf16[2,512,128]{2,1,0:T(8,128)(2,1)}, u32[]{:S(2)}, u32[]{:S(2)}) collective-permute-start(bf16[2,512,128]{2,1,0:T(8,128)(2,1)} %get-tuple-element.1210), channel_id=1, source_target_pairs={{0,10},{1,11},{2,12},{3,13},{4,14},{5,15},{6,8},{7,9},{8,18},{9,19... | collective-permute-start | bytes 786440 | tf_op jit(solution)/shard_map/ppermute | solution.py:311
  22.8 1.9 %collective-permute-start.83 = (bf16[2,512,128]{2,1,0:T(8,128)(2,1)}, bf16[2,512,128]{2,1,0:T(8,128)(2,1)}, u32[]{:S(2)}, u32[]{:S(2)}) collective-permute-start(bf16[2,512,128]{2,1,0:T(8,128)(2,1)} %get-tuple-element.1211), channel_id=1, source_target_pairs={{0,11},{1,12},{2,13},{3,14},{4,15},{5,8},{6,9},{7,10},{8,19},{9,20... | collective-permute-start | bytes 786440 | tf_op jit(solution)/shard_map/ppermute | solution.py:311
  24.7 1.9 %collective-permute-start.84 = (bf16[2,512,128]{2,1,0:T(8,128)(2,1)}, bf16[2,512,128]{2,1,0:T(8,128)(2,1)}, u32[]{:S(2)}, u32[]{:S(2)}) collective-permute-start(bf16[2,512,128]{2,1,0:T(8,128)(2,1)} %get-tuple-element.1212), channel_id=1, source_target_pairs={{0,12},{1,13},{2,14},{3,15},{4,8},{5,9},{6,10},{7,11},{8,20},{9,21... | collective-permute-start | bytes 786440 | tf_op jit(solution)/shard_map/ppermute | solution.py:311
  26.7 0.1 sub.35
  26.8 0.0 all-to-all-done
  26.8 0.1 slice.66
  26.9 0.1 eq.188
  27.0 0.1 compare_reduce_fusion.1
  27.1 0.1 fusion.4
  27.2 0.2 compare_reduce_fusion
  27.5 0.1 fusion.9
  27.7 0.7 fusion.20
  28.3 0.1 fusion.11
  28.5 0.1 and.419
  28.6 0.1 eq.191
  28.7 0.9 and_reduce_fusion
  29.6 0.8 and_reduce_fusion.1
  30.4 4.0 %collective-permute-done.80.refs_7_.refs_2_ = bf16[2,512,128]{2,1,0:T(8,128)(2,1)} collective-permute-done((bf16[2,512,128]{2,1,0:T(8,128)(2,1)}, bf16[2,512,128]{2,1,0:T(8,128)(2,1)}, u32[]{:S(2)}, u32[]{:S(2)}) %collective-permute-start.80) | collective-permute-done | bytes 262176 | tf_op jit(solution)/shard_map/ppermute | solution.py:311
  34.4 15.4 %collective-permute-start.85 = (bf16[2,512,128]{2,1,0:T(8,128)(2,1)}, bf16[2,512,128]{2,1,0:T(8,128)(2,1)}, u32[]{:S(2)}, u32[]{:S(2)}) collective-permute-start(bf16[2,512,128]{2,1,0:T(8,128)(2,1)} %get-tuple-element.1213), channel_id=1, source_target_pairs={{0,13},{1,14},{2,15},{3,8},{4,9},{5,10},{6,11},{7,12},{8,21},{9,22... | collective-permute-start | bytes 786440 | tf_op jit(solution)/shard_map/ppermute | solution.py:311
  49.9 0.0 collective-permute-done.81.refs_8_
  49.9 1.9 %collective-permute-start.86 = (bf16[2,512,128]{2,1,0:T(8,128)(2,1)}, bf16[2,512,128]{2,1,0:T(8,128)(2,1)}, u32[]{:S(2)}, u32[]{:S(2)}) collective-permute-start(bf16[2,512,128]{2,1,0:T(8,128)(2,1)} %get-tuple-element.1214), channel_id=1, source_target_pairs={{0,14},{1,15},{2,8},{3,9},{4,10},{5,11},{6,12},{7,13},{8,22},{9,23... | collective-permute-start | bytes 786440 | tf_op jit(solution)/shard_map/ppermute | solution.py:311
  51.8 0.0 collective-permute-done.82.refs_9_
  51.8 1.9 %collective-permute-start.87 = (bf16[2,512,128]{2,1,0:T(8,128)(2,1)}, bf16[2,512,128]{2,1,0:T(8,128)(2,1)}, u32[]{:S(2)}, u32[]{:S(2)}) collective-permute-start(bf16[2,512,128]{2,1,0:T(8,128)(2,1)} %get-tuple-element.1215), channel_id=1, source_target_pairs={{0,15},{1,8},{2,9},{3,10},{4,11},{5,12},{6,13},{7,14},{8,23},{9,16... | collective-permute-start | bytes 786440 | tf_op jit(solution)/shard_map/ppermute | solution.py:311
  53.8 0.6 convert_element_type.15.refs_2_
  54.3 0.6 convert_element_type.18
  54.9 0.5 convert_element_type.19
  55.4 0.1 add_reduce_fusion
  55.5 0.1 copy.20
  60.8 0.7 pad_add_fusion.refs_3_
  61.4 0.7 convert_reduce_fusion.1
  62.2 0.0 collective-permute-done.83.refs_10_
  62.2 0.0 collective-permute-done.84.refs_11_
  62.2 0.0 collective-permute-done.85.refs_12_
  62.2 4.3 %collective-permute-done.86.refs_13_ = bf16[2,512,128]{2,1,0:T(8,128)(2,1)} collective-permute-done((bf16[2,512,128]{2,1,0:T(8,128)(2,1)}, bf16[2,512,128]{2,1,0:T(8,128)(2,1)}, u32[]{:S(2)}, u32[]{:S(2)}) %collective-permute-start.86) | collective-permute-done | bytes 262176 | tf_op jit(solution)/shard_map/ppermute | solution.py:311
  66.5 5.5 %collective-permute-done.87.refs_14_ = bf16[2,512,128]{2,1,0:T(8,128)(2,1)} collective-permute-done((bf16[2,512,128]{2,1,0:T(8,128)(2,1)}, bf16[2,512,128]{2,1,0:T(8,128)(2,1)}, u32[]{:S(2)}, u32[]{:S(2)}) %collective-permute-start.87) | collective-permute-done | bytes 262176 | tf_op jit(solution)/shard_map/ppermute | solution.py:311
  72.0 4.9 %renew.3.refs_15_ = bf16[8,2,512,128]{3,2,1,0:T(8,128)(2,1)} custom-call(s32[2]{0:T(128)} %pad_add_fusion.1.refs_0_, s32[8,6]{1,0:T(8,128)} %bitcast.190, s32[6]{0:T(128)} %bitcast.204, s32[7,9]{1,0:T(8,128)} %pad_add_fusion.refs_3_, s32[1]{0:T(128)} %constant.1072.clone.1.refs_4_, ...), custom_call_target="tpu_custom_call", output_to_operand_aliasing={{}: (15, {})} | custom-call | tf_op jit(solution)/shard_map/renew/pallas_call | solution.py:352
  76.9 12.5 %conditional.5 = ((bf16[2,512,128]{2,1,0:T(8,128)(2,1)}, bf16[2,512,128]{2,1,0:T(8,128)(2,1)}, bf16[2,512,128]{2,1,0:T(8,128)(2,1)}, bf16[2,512,128]{2,1,0:T(8,128)(2,1)})) conditional(s32[]{:T(128)} %bitcast.92, (bf16[2,512,128]{2,1,0:T(8,128)(2,1)}, bf16[2,512,128]{2,1,0:T(8,128)(2,1)}, ...), branch_computations={%region_26.27_spmd, %region_27.28_spmd, %region_28.29_spmd, %regio... | conditional | flops 60 | bytes 6292292 | solution.py:414
  76.9 1.0 dynamic-slice_bitcast_fusion.44
  77.9 2.2 %collective-permute-start.44 = (bf16[2,512,128]{2,1,0:T(8,128)(2,1)S(1)}, bf16[2,512,128]{2,1,0:T(8,128)(2,1)}, u32[]{:S(2)}, u32[]{:S(2)}) collective-permute-start(bf16[2,512,128]{2,1,0:T(8,128)(2,1)S(1)} %dynamic-slice_bitcast_fusion.44), channel_id=1, source_target_pairs={{0,15},{1,8},{2,9},{3,10},{4,11},{5,12},{6,13},{7,14},{8,23},{9,16... | collective-permute-start | bytes 786440 | tf_op jit(solution)/shard_map/cond/branch_8_fun/ppermute | solution.py:391
  80.2 9.3 %collective-permute-done.44 = bf16[2,512,128]{2,1,0:T(8,128)(2,1)} collective-permute-done((bf16[2,512,128]{2,1,0:T(8,128)(2,1)S(1)}, bf16[2,512,128]{2,1,0:T(8,128)(2,1)}, u32[]{:S(2)}, u32[]{:S(2)}) %collective-permute-start.44) | collective-permute-done | bytes 262176 | tf_op jit(solution)/shard_map/cond/branch_8_fun/ppermute | solution.py:391
  89.4 1.7 %conditional.4 = (bf16[2,512,128]{2,1,0:T(8,128)(2,1)}, bf16[2,512,128]{2,1,0:T(8,128)(2,1)}, bf16[2,512,128]{2,1,0:T(8,128)(2,1)}, bf16[2,512,128]{2,1,0:T(8,128)(2,1)}) conditional(s32[]{:T(128)} %bitcast.91, (bf16[2,512,128]{2,1,0:T(8,128)(2,1)}, bf16[2,512,128]{2,1,0:T(8,128)(2,1)}, ...), branch_computations={%region_10.11_spmd, %region_11.12_spmd, %region_12.13_spmd, %regio... | conditional | flops 59 | bytes 6292272 | solution.py:414
  89.4 1.7 %copy.153 = bf16[2,512,128]{2,1,0:T(8,128)(2,1)} copy(bf16[2,512,128]{2,1,0:T(8,128)(2,1)} %get-tuple-element.1744) | data formatting | bytes 524288 | tf_op jit(solution)/shard_map/cond
  91.1 5.5 %renew.4 = bf16[8,2,512,128]{3,2,1,0:T(8,128)(2,1)} custom-call(s32[2]{0:T(128)} %pad_add_fusion.1.refs_0_, s32[8,6]{1,0:T(8,128)} %bitcast.191, s32[6]{0:T(128)} %bitcast.205, s32[7,9]{1,0:T(8,128)} %pad_add_fusion.refs_3_, s32[1]{0:T(128)} %bitcast.90.refs_4_, bf16[2,32,512,128]{3,2,1,0:T(8,128)(2,1)} %bitcast.183, ...), custom_call_target="tpu_custom_call", output_to_operand_aliasing={{}: (15, {})} | custom-call | tf_op jit(solution)/shard_map/renew/pallas_call | solution.py:352
  96.6 0.0 copy-start.3
  96.6 0.0 copy-start
  96.7 4.5 %all-to-all-start.1 = ((bf16[8,2,512,128]{3,2,1,0:T(8,128)(2,1)}), bf16[8,2,512,128]{3,2,1,0:T(8,128)(2,1)}, u32[]{:S(2)}, u32[]{:S(2)}) async-start(bf16[8,2,512,128]{3,2,1,0:T(8,128)(2,1)} %renew.4), calls=%async_computation.1 | async-start | bytes 4194304 | tf_op jit(solution)/shard_map/all_to_all | solution.py:418
  101.2 0.7 convert_reduce_fusion.3
  101.8 1.3 copy.312.refs_15_
  103.2 0.9 while.58
  104.0 1.8 %renew.5 = bf16[8,2,512,128]{3,2,1,0:T(8,128)(2,1)} custom-call(s32[2]{0:T(128)} %pad_add_fusion.1.refs_0_, s32[8,6]{1,0:T(8,128)} %bitcast.192, s32[6]{0:T(128)} %bitcast.206, s32[7,9]{1,0:T(8,128)} %pad_add_fusion.refs_3_, s32[1]{0:T(128)} %bitcast.93.refs_4_, bf16[2,32,512,128]{3,2,1,0:T(8,128)(2,1)} %bitcast.184, ...), custom_call_target="tpu_custom_call", output_to_operand_aliasing={{}: (15, {})} | custom-call | tf_op jit(solution)/shard_map/renew/pallas_call | solution.py:352
  105.8 4.1 %zeros.1.refs_12_ = bf16[2,32,512,128]{3,2,1,0:T(8,128)(2,1)} custom-call(s32[2]{0:T(128)} %pad_add_fusion.1.refs_0_, s32[8,6]{1,0:T(8,128)} %bitcast.193, bf16[2,512,128]{2,1,0:T(8,128)(2,1)} %collective-permute-done.80.refs_7_.refs_2_), custom_call_target="tpu_custom_call" | custom-call | tf_op jit(solution)/shard_map/zeros/pallas_call | solution.py:373
  109.9 0.6 while.59
  110.5 39.7 %all-to-all-done.1.refs_3_ = bf16[8,2,512,128]{3,2,1,0:T(8,128)(2,1)} async-done(((bf16[8,2,512,128]{3,2,1,0:T(8,128)(2,1)}), bf16[8,2,512,128]{3,2,1,0:T(8,128)(2,1)}, u32[]{:S(2)}, u32[]{:S(2)}) %all-to-all-start.1) | async-done | bytes 2097184 | tf_op jit(solution)/shard_map/all_to_all | solution.py:418
  150.2 3.9 %write.1 = bf16[2,32,512,128]{3,2,1,0:T(8,128)(2,1)} custom-call(s32[2]{0:T(128)} %pad_add_fusion.1.refs_0_, s32[8,6]{1,0:T(8,128)} %bitcast.194, s32[8]{0:T(128)} %convert_element_type.15.refs_2_, bf16[8,2,512,128]{3,2,1,0:T(8,128)(2,1)} %all-to-all-done.1.refs_3_, ...), custom_call_target="tpu_custom_call", output_to_operand_aliasing={{}: (12, {})} | custom-call | tf_op jit(solution)/shard_map/write/pallas_call | solution.py:426
  (21 shorter events, 0.2 us)
Async XLA Ops:
  0.8 0.6 copy-start.1
  9.4 17.3 %all-to-all-start = ((s32[32,1,54]{2,1,0:T(1,128)}), s32[32,1,54]{2,1,0:T(1,128)S(1)}, u32[]{:S(2)}, u32[]{:S(2)}) async-start(s32[32,1,54]{2,1,0:T(1,128)} %broadcast_in_dim.47), calls=%async_computation | async-start | bytes 32768 | tf_op jit(solution)/shard_map/all_to_all | solution.py:317
  15.6 18.9 %collective-permute-start.80 = (bf16[2,512,128]{2,1,0:T(8,128)(2,1)}, bf16[2,512,128]{2,1,0:T(8,128)(2,1)}, u32[]{:S(2)}, u32[]{:S(2)}) collective-permute-start(bf16[2,512,128]{2,1,0:T(8,128)(2,1)} %get-tuple-element.1208), channel_id=1, source_target_pairs={{0,8},{1,9},{2,10},{3,11},{4,12},{5,13},{6,14},{7,15},{8,16},{9,17... | collective-permute-start | bytes 786440 | tf_op jit(solution)/shard_map/ppermute | solution.py:311
  19.0 30.9 %collective-permute-start.81 = (bf16[2,512,128]{2,1,0:T(8,128)(2,1)}, bf16[2,512,128]{2,1,0:T(8,128)(2,1)}, u32[]{:S(2)}, u32[]{:S(2)}) collective-permute-start(bf16[2,512,128]{2,1,0:T(8,128)(2,1)} %get-tuple-element.1209), channel_id=1, source_target_pairs={{0,9},{1,10},{2,11},{3,12},{4,13},{5,14},{6,15},{7,8},{8,17},{9,18... | collective-permute-start | bytes 786440 | tf_op jit(solution)/shard_map/ppermute | solution.py:311
  20.9 30.9 %collective-permute-start.82 = (bf16[2,512,128]{2,1,0:T(8,128)(2,1)}, bf16[2,512,128]{2,1,0:T(8,128)(2,1)}, u32[]{:S(2)}, u32[]{:S(2)}) collective-permute-start(bf16[2,512,128]{2,1,0:T(8,128)(2,1)} %get-tuple-element.1210), channel_id=1, source_target_pairs={{0,10},{1,11},{2,12},{3,13},{4,14},{5,15},{6,8},{7,9},{8,18},{9,19... | collective-permute-start | bytes 786440 | tf_op jit(solution)/shard_map/ppermute | solution.py:311
  22.8 39.4 %collective-permute-start.83 = (bf16[2,512,128]{2,1,0:T(8,128)(2,1)}, bf16[2,512,128]{2,1,0:T(8,128)(2,1)}, u32[]{:S(2)}, u32[]{:S(2)}) collective-permute-start(bf16[2,512,128]{2,1,0:T(8,128)(2,1)} %get-tuple-element.1211), channel_id=1, source_target_pairs={{0,11},{1,12},{2,13},{3,14},{4,15},{5,8},{6,9},{7,10},{8,19},{9,20... | collective-permute-start | bytes 786440 | tf_op jit(solution)/shard_map/ppermute | solution.py:311
  24.7 37.4 %collective-permute-start.84 = (bf16[2,512,128]{2,1,0:T(8,128)(2,1)}, bf16[2,512,128]{2,1,0:T(8,128)(2,1)}, u32[]{:S(2)}, u32[]{:S(2)}) collective-permute-start(bf16[2,512,128]{2,1,0:T(8,128)(2,1)} %get-tuple-element.1212), channel_id=1, source_target_pairs={{0,12},{1,13},{2,14},{3,15},{4,8},{5,9},{6,10},{7,11},{8,20},{9,21... | collective-permute-start | bytes 786440 | tf_op jit(solution)/shard_map/ppermute | solution.py:311
  28.5 33.7 %copy-start.2 = (pred[8]{0:T(512)(128)(4,1)}, pred[8]{0:T(512)(128)(4,1)S(1)}, u32[]{:S(2)}) copy-start(pred[8]{0:T(512)(128)(4,1)S(1)} %fusion.11) | copy-start | bytes 28
  34.4 27.8 %collective-permute-start.85 = (bf16[2,512,128]{2,1,0:T(8,128)(2,1)}, bf16[2,512,128]{2,1,0:T(8,128)(2,1)}, u32[]{:S(2)}, u32[]{:S(2)}) collective-permute-start(bf16[2,512,128]{2,1,0:T(8,128)(2,1)} %get-tuple-element.1213), channel_id=1, source_target_pairs={{0,13},{1,14},{2,15},{3,8},{4,9},{5,10},{6,11},{7,12},{8,21},{9,22... | collective-permute-start | bytes 786440 | tf_op jit(solution)/shard_map/ppermute | solution.py:311
  49.9 16.6 %collective-permute-start.86 = (bf16[2,512,128]{2,1,0:T(8,128)(2,1)}, bf16[2,512,128]{2,1,0:T(8,128)(2,1)}, u32[]{:S(2)}, u32[]{:S(2)}) collective-permute-start(bf16[2,512,128]{2,1,0:T(8,128)(2,1)} %get-tuple-element.1214), channel_id=1, source_target_pairs={{0,14},{1,15},{2,8},{3,9},{4,10},{5,11},{6,12},{7,13},{8,22},{9,23... | collective-permute-start | bytes 786440 | tf_op jit(solution)/shard_map/ppermute | solution.py:311
  51.8 20.2 %collective-permute-start.87 = (bf16[2,512,128]{2,1,0:T(8,128)(2,1)}, bf16[2,512,128]{2,1,0:T(8,128)(2,1)}, u32[]{:S(2)}, u32[]{:S(2)}) collective-permute-start(bf16[2,512,128]{2,1,0:T(8,128)(2,1)} %get-tuple-element.1215), channel_id=1, source_target_pairs={{0,15},{1,8},{2,9},{3,10},{4,11},{5,12},{6,13},{7,14},{8,23},{9,16... | collective-permute-start | bytes 786440 | tf_op jit(solution)/shard_map/ppermute | solution.py:311
  77.9 11.5 %collective-permute-start.44 = (bf16[2,512,128]{2,1,0:T(8,128)(2,1)S(1)}, bf16[2,512,128]{2,1,0:T(8,128)(2,1)}, u32[]{:S(2)}, u32[]{:S(2)}) collective-permute-start(bf16[2,512,128]{2,1,0:T(8,128)(2,1)S(1)} %dynamic-slice_bitcast_fusion.44), channel_id=1, source_target_pairs={{0,15},{1,8},{2,9},{3,10},{4,11},{5,12},{6,13},{7,14},{8,23},{9,16... | collective-permute-start | bytes 786440 | tf_op jit(solution)/shard_map/cond/branch_8_fun/ppermute | solution.py:391
  96.6 4.5 %copy-start.3 = (pred[8]{0:T(512)(128)(4,1)S(1)}, pred[8]{0:T(512)(128)(4,1)}, u32[]{:S(2)}) copy-start(pred[8]{0:T(512)(128)(4,1)} %copy-done.2) | copy-start | bytes 28
  96.6 5.2 %copy-start = (bf16[8,2,512,128]{3,2,1,0:T(8,128)(2,1)S(1)}, bf16[8,2,512,128]{3,2,1,0:T(8,128)(2,1)}, u32[]{:S(2)}) copy-start(bf16[8,2,512,128]{3,2,1,0:T(8,128)(2,1)} %renew.4) | copy-start | bytes 6291460
  96.7 53.5 %all-to-all-start.1 = ((bf16[8,2,512,128]{3,2,1,0:T(8,128)(2,1)}), bf16[8,2,512,128]{3,2,1,0:T(8,128)(2,1)}, u32[]{:S(2)}, u32[]{:S(2)}) async-start(bf16[8,2,512,128]{3,2,1,0:T(8,128)(2,1)} %renew.4), calls=%async_computation.1 | async-start | bytes 4194304 | tf_op jit(solution)/shard_map/all_to_all | solution.py:418
  101.8 1.3 copy-start.4

commit v3 on v2

--- a/solution.py
+++ b/solution.py
@@ -19,19 +19,37 @@
     return lax.div(row, jnp.int32(owned))
 
 
-def first_kernel(senders, owned, state, rows, cols, source, blocks, *refs):
+def read_table(table, senders, stored):
+    held = senders * stored
+
+    def rows(sender, block):
+        return table[sender * stored + block]
+
+    def cols(block):
+        return table[held + block]
+
+    def more(at):
+        return table[held + stored + 1 + at]
+
+    return rows, cols, table[held + stored], more
+
+
+def first_kernel(senders, owned, rows_ref, cols_ref, source, blocks, *refs):
     slots, refs = refs[:senders], refs[senders:]
     kept, operand, pieces, made, op_sem, in_sem, slot_sem, keep_sem = refs
-    place = state[0]
     stored, _ = blocks.shape[:2]
+    place = lax.axis_index("trace")
     batches, shots = source.shape[0], source.shape[-1]
+
+    def rows(sender, block):
+        return rows_ref[0, sender, block]
 
     def load(block):
         return pltpu.make_async_copy(blocks.at[block], operand.at[block], op_sem.at[block])
 
     def fetch(block, batch):
         return pltpu.make_async_copy(
-            source.at[batch, cols[block] - place * owned],
+            source.at[batch, cols_ref[0, 0, block] - place * owned],
             pieces.at[block, :, pl.ds(batch * shots, shots)],
             in_sem.at[block, batch],
         )
@@ -56,7 +74,7 @@
         product = jnp.dot(operand[block], pieces[block], preferred_element_type=jnp.float32)
         for batch in range(batches):
             made[block, batch] = product[:, batch * shots : (batch + 1) * shots].astype(made.dtype)
-        owner = owner_of(rows[place, block], owned)
+        owner = owner_of(rows(place, block), owned)
         shift = lax.rem(owner - place + senders, senders)
         for slot in range(senders):
 
@@ -72,11 +90,17 @@
         keep(block, 0).wait()
 
 
-def renew_kernel(senders, owned, state, rows, cols, match, go, source, blocks, *refs):
-    recv, refs = refs[:senders], refs[senders:]
-    kept, operand, pieces, arrived, total, made, op_sem, in_sem, recv_sem, keep_sem = refs[1:]
-    place = state[0]
+def renew_kernel(senders, owned, others, resent, table, source, blocks, *refs):
+    recv, refs = refs[:senders], refs[senders + 1 + resent + others :]
+    slots, refs = refs[:resent], refs[resent:]
+    kept, operand, pieces, arrived, total, made, op_sem, in_sem, recv_sem, keep_sem, slot_sem = refs
     stored, _ = blocks.shape[:2]
+    rows, cols, place, more = read_table(table, senders, stored)
+    go = more(0) > 0
+
+    def match(block, sender):
+        return more(1 + block * (senders + 1) + sender)
+
     batches, shots = source.shape[0], source.shape[-1]
 
     def load(block):
@@ -84,7 +108,7 @@
 
     def fetch(block, batch):
         return pltpu.make_async_copy(
-            source.at[batch, cols[block] - place * owned],
+            source.at[batch, cols(block) - place * owned],
             pieces.at[block, :, pl.ds(batch * shots, shots)],
             in_sem.at[block, batch],
         )
@@ -95,17 +119,20 @@
     def keep(block, owner):
         return pltpu.make_async_copy(made.at[block], kept.at[owner], keep_sem.at[block])
 
+    def give(block, slot):
+        return pltpu.make_async_copy(made.at[block], slots[slot], slot_sem.at[block])
+
     def hits(block):
-        return match[block, senders]
+        return match(block, senders)
 
     def sender_at(step):
         return lax.rem(place - step + senders, senders)
 
-    @pl.when(go[0] > 0)
+    @pl.when(go)
     def _():
         for step in range(senders):
 
-            @pl.when(match[stored, sender_at(step)] > 0)
+            @pl.when(match(stored, sender_at(step)) > 0)
             def _():
                 take(step).start()
 
@@ -119,7 +146,7 @@
 
         for step in range(senders):
 
-            @pl.when(match[stored, sender_at(step)] > 0)
+            @pl.when(match(stored, sender_at(step)) > 0)
             def _():
                 take(step).wait()
 
@@ -131,7 +158,7 @@
 
                 @pl.loop(0, senders)
                 def _(step):
-                    @pl.when(match[block, sender_at(step)] > 0)
+                    @pl.when(match(block, sender_at(step)) > 0)
                     def _():
                         total[...] += arrived[step].astype(jnp.float32)
 
@@ -147,13 +174,21 @@
                 product = jnp.dot(operand[block], pieces[block], preferred_element_type=jnp.float32)
                 for batch in range(batches):
                     made[block, batch] = product[:, batch * shots : (batch + 1) * shots].astype(made.dtype)
-                keep(block, owner_of(rows[place, block], owned)).start()
+                owner = owner_of(rows(place, block), owned)
+                keep(block, owner).start()
+                for slot in range(resent):
+
+                    @pl.when(lax.rem(owner - place + senders, senders) == slot)
+                    def _():
+                        give(block, slot).start()
 
         @pl.loop(0, stored)
         def _(block):
             @pl.when(hits(block) > 0)
             def _():
                 keep(block, 0).wait()
+                if resent:
+                    give(block, 0).wait()
 
 
 def hit_rows(rows, senders, place, owned, stored, here):
@@ -163,13 +198,14 @@
     def _(sender):
         row = jnp.int32(-1)
         for other in range(stored):
-            value = rows[sender, other] - first
+            value = rows(sender, other) - first
             row = jnp.where((value >= 0) & (value < owned), value, row)
         here[sender] = row
 
 
-def zero_kernel(owned, senders, stored, batches, state, rows, after, out, nothing, here, sem):
-    hit_rows(rows, senders, state[0], owned, stored, here)
+def zero_kernel(owned, senders, stored, batches, table, after, out, nothing, here, sem):
+    rows, _, place, _ = read_table(table, senders, stored)
+    hit_rows(rows, senders, place, owned, stored, here)
     nothing[...] = jnp.zeros_like(nothing)
 
     def free(row):
@@ -196,10 +232,11 @@
                 put(batch, row).wait()
 
 
-def write_kernel(owned, senders, stored, batches, state, rows, fixed, recv, *refs):
+def write_kernel(owned, senders, stored, batches, table, recv, *refs):
     fixes, refs = refs[:senders], refs[senders:]
     _, out, arrived, total, made, here, in_sem, out_sem = refs
-    hit_rows(rows, senders, state[0], owned, stored, here)
+    rows, _, place, fixed = read_table(table, senders, stored)
+    hit_rows(rows, senders, place, owned, stored, here)
 
     def take(sender):
         return pltpu.make_async_copy(recv.at[sender], arrived.at[sender], in_sem.at[sender])
@@ -215,13 +252,13 @@
         return total
 
     for step in range(senders):
-        sender = lax.rem(state[0] - step + senders, senders)
-
-        @pl.when((here[sender] >= 0) & (fixed[sender] == 0))
+        sender = lax.rem(place - step + senders, senders)
+
+        @pl.when((here[sender] >= 0) & (fixed(sender) == 0))
         def _():
             take(sender).start()
 
-        @pl.when((here[sender] >= 0) & (fixed[sender] > 0))
+        @pl.when((here[sender] >= 0) & (fixed(sender) > 0))
         def _():
             pltpu.make_async_copy(fixes[step], arrived.at[sender], in_sem.at[sender]).start()
 
@@ -276,23 +313,23 @@
     owned = local // width
     source = sources.reshape(batches, owned, width, shots)
     cols = col_block[0, 0]
-    state = jnp.stack([place, depth]).astype(jnp.int32)
+    table = jnp.concatenate([rows.reshape(-1), cols, place[None].astype(jnp.int32)])
     dtype = sources.dtype
     tile = (batches, width, shots)
     slot = jax.ShapeDtypeStruct(tile, dtype)
     held = jax.ShapeDtypeStruct((senders,) + tile, dtype)
 
-    def pairs(step, down=1):
+    def pairs(step, down=1, top=0):
         return [
             (i * senders + j, (i + down) * senders + (j + step) % senders)
-            for i in range(layers - down)
+            for i in range(top, layers - down)
             for j in range(senders)
         ]
 
     *slots, kept = pl.pallas_call(
         lambda *refs: first_kernel(senders, owned, *refs),
         out_shape=(slot,) * senders + (held,),
-        in_specs=[SMEM] * 3 + [ANY] * 2,
+        in_specs=[SMEM] * 2 + [ANY] * 2,
         out_specs=(ANY,) * (senders + 1),
         scratch_shapes=[
             pltpu.VMEM((stored, width, width), dtype),
@@ -305,20 +342,19 @@
         ],
         compiler_params=PARAMS,
         name="first",
-    )(state, rows, cols, source, blocks)
-    recv = []
-    for step in range(senders):
-        recv.append(lax.ppermute(slots[step], AXES, pairs(step)))
+    )(row_block, col_block, source, blocks)
+    recv = [None] * senders
+    for step in sorted(range(senders), key=lambda step: abs(2 * step - senders)):
+        recv[step] = lax.ppermute(slots[step], AXES, pairs(step))
 
     total = layers * senders
-    mine = jnp.concatenate([rows.reshape(-1), cols])
-    mine, kept = lax.optimization_barrier((mine, kept))
+    mine, kept = lax.optimization_barrier((table, kept))
     mine = jnp.broadcast_to(mine[None], (total, mine.shape[0]))
     known = lax.all_to_all(mine, AXES, split_axis=0, concat_axis=0, tiled=True)
     known = known.reshape(layers, senders, -1)
     blocks_all = senders * stored
     rows_all = known[:, 0, :blocks_all]
-    cols_all = known[:, :, blocks_all:].reshape(layers, blocks_all)
+    cols_all = known[:, :, blocks_all : blocks_all + stored].reshape(layers, blocks_all)
     feeds = rows_all[:-1, :, None] == cols_all[1:, None, :]
     read = jnp.any(feeds, axis=2)
     home = jnp.repeat(jnp.arange(senders, dtype=jnp.int32), stored)
@@ -348,12 +384,13 @@
     match = jnp.concatenate([match, jnp.max(match, axis=0, keepdims=True)])
     match = jnp.concatenate([match, jnp.max(match, axis=1, keepdims=True)], axis=1)
 
-    def renew(kept, go):
+    def renew(kept, go, slots=(), after=()):
+        resent = len(slots)
         return pl.pallas_call(
-            lambda *refs: renew_kernel(senders, owned, *refs),
-            out_shape=held,
-            in_specs=[SMEM] * 5 + [ANY] * (3 + senders),
-            out_specs=ANY,
+            lambda *refs: renew_kernel(senders, owned, len(after), resent, *refs),
+            out_shape=(slot,) * resent + (held,),
+            in_specs=[SMEM] + [ANY] * (3 + senders + resent + len(after)),
+            out_specs=(ANY,) * (resent + 1),
             scratch_shapes=[
                 pltpu.VMEM((stored, width, width), dtype),
                 pltpu.VMEM((stored, width, batches * shots), dtype),
@@ -364,31 +401,28 @@
                 DMA((stored, batches)),
                 DMA((senders,)),
                 DMA((stored,)),
+                DMA((stored,)),
             ],
-            input_output_aliases={7 + senders: 0},
+            input_output_aliases={3 + senders + at: at for at in range(resent + 1)},
             compiler_params=PARAMS,
             name="renew",
-        )(state, rows, cols, match, go[None], source, blocks, *recv, kept)
+        )(jnp.concatenate([table, go[None], match.reshape(-1)]), source, blocks, *recv, *slots, kept, *after)
 
     traces = pl.pallas_call(
         lambda *refs: zero_kernel(owned, senders, stored, batches, *refs),
         out_shape=jax.ShapeDtypeStruct((batches, owned, width, shots), dtype),
-        in_specs=[SMEM, SMEM, ANY],
+        in_specs=[SMEM, ANY],
         out_specs=ANY,
-        scratch_shapes=[
-            pltpu.VMEM((width, shots), dtype),
-            pltpu.SMEM((senders,), jnp.int32),
-            DMA((batches, owned)),
-        ],
+        scratch_shapes=[pltpu.VMEM((width, shots), dtype), pltpu.SMEM((senders,), jnp.int32), DMA((batches, owned))],
         compiler_params=PARAMS,
         name="zeros",
-    )(state, rows, recv[0])
-
-    kept = renew(kept, jnp.int32(1))
-
-    def again(step, kept, down=1):
+    )(table, mine)
+
+    *slots, kept = renew(kept, jnp.int32(1), tuple(slots), (traces,))
+
+    def again(step, kept, down, top):
         sent = lax.dynamic_index_in_dim(kept, (place + step) % senders, 0, keepdims=False)
-        return lax.ppermute(sent, AXES, pairs(step, down))
+        return lax.ppermute(sent, AXES, pairs(step, down, top))
 
     def one_by_one(mask, send, came):
         def resend(carry):
@@ -406,27 +440,31 @@
             near = range(low, min(low + group, senders))
 
             def resend(which):
-                return lambda kept, old: tuple(
-                    again(step, kept) if which >> at & 1 else old[at] for at, step in enumerate(near)
+                return lambda new, old: tuple(
+                    lax.ppermute(new[at], AXES, pairs(step, 1, 1)) if which >> at & 1 else old[at]
+                    for at, step in enumerate(near)
                 )
 
             code = sum(masks[0][step] << at for at, step in enumerate(near))
             recv[low : low + group] = lax.switch(
-                code, [resend(which) for which in range(1 << len(near))], kept, tuple(recv[low : low + group])
+                code,
+                [resend(which) for which in range(1 << len(near))],
+                tuple(slots[low : low + group]),
+                tuple(recv[low : low + group]),
             )
-        kept = renew(kept, jnp.max(masks[0]))
+        (kept,) = renew(kept, jnp.where(depth >= 2, jnp.max(masks[0]), 0))
     arrived = lax.all_to_all(kept, "trace", split_axis=0, concat_axis=0, tiled=True)
 
     late = kept
-    for mask in masks[1:]:
-        recv = list(one_by_one(mask, lambda step, late=late: again(step, late), recv))
-        late = renew(late, jnp.max(mask))
-    fixes = one_by_one(late_mask, lambda step: again(step, late, 0), recv)
+    for wave, mask in enumerate(masks[1:], 3):
+        recv = list(one_by_one(mask, lambda step, late=late, wave=wave: again(step, late, 1, wave - 1), recv))
+        (late,) = renew(late, jnp.where(depth >= wave, jnp.max(mask), 0))
+    fixes = one_by_one(late_mask, lambda step: again(step, late, 0, 0), recv)
 
     traces = pl.pallas_call(
         lambda *refs: write_kernel(owned, senders, stored, batches, *refs),
         out_shape=jax.ShapeDtypeStruct((batches, owned, width, shots), dtype),
-        in_specs=[SMEM] * 3 + [ANY] * (senders + 2),
+        in_specs=[SMEM] + [ANY] * (senders + 2),
         out_specs=ANY,
         scratch_shapes=[
             pltpu.VMEM((senders,) + tile, dtype),
@@ -436,10 +474,10 @@
             DMA((senders,)),
             DMA((senders, batches)),
         ],
-        input_output_aliases={4 + senders: 0},
+        input_output_aliases={2 + senders: 0},
         compiler_params=PARAMS,
         name="write",
-    )(state, rows, fixed, arrived, *fixes, traces)
+    )(jnp.concatenate([table, fixed]), arrived, *fixes, traces)
     return traces.reshape(1, batches, local, shots)
 
 

time: 155 us -> 150 us (0.968)
  local copies, waits for them, and re-layouts: 7.97 us -> 12.4 us
  starting transfers between devices: 43.2 us -> 38.8 us
  waiting for transfers between devices: 62.7 us -> 58.8 us
  Pallas kernels: 25 us -> 23.3 us
    ppermute x9, waiting for transfers between devices: 23.1 us -> 14.1 us  [the longest x1 8.95 us: resend(): lax.ppermute(new[at], AXES, pairs(step, 1, 1))]
    all_to_all x1, waiting for transfers between devices: 39.7 us -> 44.7 us  [body(): lax.all_to_all(kept, 'trace', split_axis=0, concat_axis=0, tiled=True)]
    ppermute x9, starting transfers between devices: 32.6 us -> 28.1 us  [the longest x8 26.2 us: body(): recv[step] = lax.ppermute(slots[step], AXES, pairs(step))]
    concatenate x0 -> x3, local copies, waits for them, and re-layouts: none -> 3.86 us  [renew(): jnp.concatenate([table, go[None], match.reshape(-1)])]
    cond x1 -> x0, local copies, waits for them, and re-layouts: 1.67 us -> none
    pallas_call x3, Pallas kernels: 12.2 us -> 10.6 us  [renew(): pl.pallas_call(lambda *refs: renew_kernel(senders, owned, len(after), res...]
  transfers between devices with their start and end apart: 11 -> 11, of which waited for: 5 -> 3; matrix products, arithmetic and copies ran while one was open for 6% -> 12% of each run, Pallas kernels for 4% -> 3%
where the time goes in v3:
time: 150 us; the launch traced here: 149 us
  waiting for transfers between devices  58.8 us (39%)
  starting transfers between devices  38.8 us (26%)
  Pallas kernels  23.3 us (16%)
  local copies, waits for them, and re-layouts  12.4 us (8%)
  other arithmetic  8.28 us (6%)
  between operations  6.54 us (4%)
    all_to_all x1, waiting for transfers between devices, body(): lax.all_to_all(kept, 'trace', split_axis=0, concat_axis=0, tiled=True)  44.7 us
    ppermute x8, starting transfers between devices, body(): recv[step] = lax.ppermute(slots[step], AXES, pairs(step))  26.2 us
    pallas_call x3, Pallas kernels, renew(): pl.pallas_call(lambda *refs: renew_kernel(senders, owned, len(after), res...  10.6 us
    ppermute x1, waiting for transfers between devices, resend(): lax.ppermute(new[at], AXES, pairs(step, 1, 1))  8.95 us
    all_to_all x1, starting transfers between devices, body(): known = lax.all_to_all(mine, AXES, split_axis=0, concat_axis=0, tiled=True)  6.15 us
    ppermute x8, waiting for transfers between devices, body(): recv[step] = lax.ppermute(slots[step], AXES, pairs(step))  5.13 us
    pallas_call x1, Pallas kernels, body(): pl.pallas_call(lambda *refs: first_kernel(senders, owned, *refs), out_sha...  4.82 us
    all_to_all x1, starting transfers between devices, body(): lax.all_to_all(kept, 'trace', split_axis=0, concat_axis=0, tiled=True)  4.59 us
  transfers between devices with their start and end apart: 11, of which 3 were waited for; matrix products, arithmetic and copies ran while one was open for 12% of the time, Pallas kernels for 3%

profile of v3, /device:TPU:4, one launch (start us, length us, event | category | flops | bytes accessed | tf_op | source)
XLA Modules:
  0.0 149.5 jit_solution(16944950924018762201)
XLA Ops:
  0.0 0.8 copy.29.refs_0_
  0.8 0.6 copy-done.1
  1.3 0.6 reshape_squeeze.3
  1.9 4.8 %first.1 = (bf16[2,512,128]{2,1,0:T(8,128)(2,1)}, bf16[2,512,128]{2,1,0:T(8,128)(2,1)}, bf16[2,512,128]{2,1,0:T(8,128)(2,1)}, bf16[2,512,128]{2,1,0:T(8,128)(2,1...) custom-call(s32[1,8,6]{2,1,0:T(8,128)} %copy-done.1, ...), custom_call_target="tpu_custom_call" | custom-call | tf_op jit(solution)/shard_map/first/pallas_call | solution.py:329
  6.7 0.7 pad_add_fusion.1.refs_0_
  7.5 0.6 broadcast_in_dim.53
  8.1 6.1 %all-to-all-start = ((s32[32,1,55]{2,1,0:T(1,128)}), s32[32,1,55]{2,1,0:T(1,128)}, u32[]{:S(2)}, u32[]{:S(2)}) async-start(s32[32,1,55]{2,1,0:T(1,128)} %broadcast_in_dim.53), calls=%async_computation | async-start | bytes 32768 | tf_op jit(solution)/shard_map/all_to_all | solution.py:353
  14.2 3.4 %collective-permute-start.80 = (bf16[2,512,128]{2,1,0:T(8,128)(2,1)}, bf16[2,512,128]{2,1,0:T(8,128)(2,1)}, u32[]{:S(2)}, u32[]{:S(2)}) collective-permute-start(bf16[2,512,128]{2,1,0:T(8,128)(2,1)} %get-tuple-element.1229.refs_11_), channel_id=1, source_target_pairs={{0,8},{1,9},{2,10},{3,11},{4,12},{5,13},{6,14},{7,15},{8,16},{9,17... | collective-permute-start | bytes 786440 | tf_op jit(solution)/shard_map/ppermute | solution.py:348
  17.6 1.9 %collective-permute-start.81 = (bf16[2,512,128]{2,1,0:T(8,128)(2,1)}, bf16[2,512,128]{2,1,0:T(8,128)(2,1)}, u32[]{:S(2)}, u32[]{:S(2)}) collective-permute-start(bf16[2,512,128]{2,1,0:T(8,128)(2,1)} %get-tuple-element.1230.refs_12_), channel_id=1, source_target_pairs={{0,9},{1,10},{2,11},{3,12},{4,13},{5,14},{6,15},{7,8},{8,17},{9,18... | collective-permute-start | bytes 786440 | tf_op jit(solution)/shard_map/ppermute | solution.py:348
  19.5 1.9 %collective-permute-start.82 = (bf16[2,512,128]{2,1,0:T(8,128)(2,1)}, bf16[2,512,128]{2,1,0:T(8,128)(2,1)}, u32[]{:S(2)}, u32[]{:S(2)}) collective-permute-start(bf16[2,512,128]{2,1,0:T(8,128)(2,1)} %get-tuple-element.1231.refs_13_), channel_id=1, source_target_pairs={{0,10},{1,11},{2,12},{3,13},{4,14},{5,15},{6,8},{7,9},{8,18},{9,19... | collective-permute-start | bytes 786440 | tf_op jit(solution)/shard_map/ppermute | solution.py:348
  21.5 1.9 %collective-permute-start.83 = (bf16[2,512,128]{2,1,0:T(8,128)(2,1)}, bf16[2,512,128]{2,1,0:T(8,128)(2,1)}, u32[]{:S(2)}, u32[]{:S(2)}) collective-permute-start(bf16[2,512,128]{2,1,0:T(8,128)(2,1)} %get-tuple-element.1232.refs_14_), channel_id=1, source_target_pairs={{0,11},{1,12},{2,13},{3,14},{4,15},{5,8},{6,9},{7,10},{8,19},{9,20... | collective-permute-start | bytes 786440 | tf_op jit(solution)/shard_map/ppermute | solution.py:348
  23.4 1.9 %collective-permute-start.84 = (bf16[2,512,128]{2,1,0:T(8,128)(2,1)}, bf16[2,512,128]{2,1,0:T(8,128)(2,1)}, u32[]{:S(2)}, u32[]{:S(2)}) collective-permute-start(bf16[2,512,128]{2,1,0:T(8,128)(2,1)} %get-tuple-element.1233.refs_15_), channel_id=1, source_target_pairs={{0,12},{1,13},{2,14},{3,15},{4,8},{5,9},{6,10},{7,11},{8,20},{9,21... | collective-permute-start | bytes 786440 | tf_op jit(solution)/shard_map/ppermute | solution.py:348
  25.4 0.6 sub.35
  26.0 0.6 broadcast_in_dim.58.refs_1_
  26.6 4.0 %zeros.1.refs_20_.refs_10_ = bf16[2,32,512,128]{3,2,1,0:T(8,128)(2,1)} custom-call(s32[55]{0:T(128)} %copy-done.4, s32[32,55]{1,0:T(8,128)} %broadcast_in_dim.58.refs_1_), custom_call_target="tpu_custom_call" | custom-call | tf_op jit(solution)/shard_map/zeros/pallas_call | solution.py:411
  30.6 0.7 slice.65
  31.3 0.7 slice.67
  32.0 0.8 slice.66
  32.8 0.1 eq.129
  32.9 0.9 and_reduce_fusion
  33.9 0.1 eq.123
  34.0 0.1 compare_reduce_fusion.1
  34.1 0.1 fusion.4
  34.2 0.2 compare_reduce_fusion
  34.5 0.7 add_select_fusion.1
  35.1 0.1 add_reduce_fusion
  35.3 0.1 copy.32
  35.4 0.2 fusion.9
  35.5 0.1 pad_add_fusion
  35.6 0.1 and.162
  35.7 0.7 convert_reduce_fusion.1
  36.4 0.8 and_reduce_fusion.1
  37.2 0.0 collective-permute-done.80.refs_3_
  37.2 11.3 %collective-permute-start.85 = (bf16[2,512,128]{2,1,0:T(8,128)(2,1)}, bf16[2,512,128]{2,1,0:T(8,128)(2,1)}, u32[]{:S(2)}, u32[]{:S(2)}) collective-permute-start(bf16[2,512,128]{2,1,0:T(8,128)(2,1)} %get-tuple-element.1234.refs_16_), channel_id=1, source_target_pairs={{0,13},{1,14},{2,15},{3,8},{4,9},{5,10},{6,11},{7,12},{8,21},{9,22... | collective-permute-start | bytes 786440 | tf_op jit(solution)/shard_map/ppermute | solution.py:348
  48.5 0.0 collective-permute-done.81.refs_4_
  48.5 1.9 %collective-permute-start.86 = (bf16[2,512,128]{2,1,0:T(8,128)(2,1)}, bf16[2,512,128]{2,1,0:T(8,128)(2,1)}, u32[]{:S(2)}, u32[]{:S(2)}) collective-permute-start(bf16[2,512,128]{2,1,0:T(8,128)(2,1)} %get-tuple-element.1235.refs_17_), channel_id=1, source_target_pairs={{0,14},{1,15},{2,8},{3,9},{4,10},{5,11},{6,12},{7,13},{8,22},{9,23... | collective-permute-start | bytes 786440 | tf_op jit(solution)/shard_map/ppermute | solution.py:348
  50.5 0.0 collective-permute-done.82.refs_5_
  50.5 1.9 %collective-permute-start.87 = (bf16[2,512,128]{2,1,0:T(8,128)(2,1)}, bf16[2,512,128]{2,1,0:T(8,128)(2,1)}, u32[]{:S(2)}, u32[]{:S(2)}) collective-permute-start(bf16[2,512,128]{2,1,0:T(8,128)(2,1)} %get-tuple-element.1236.refs_18_), channel_id=1, source_target_pairs={{0,15},{1,8},{2,9},{3,10},{4,11},{5,12},{6,13},{7,14},{8,23},{9,16... | collective-permute-start | bytes 786440 | tf_op jit(solution)/shard_map/ppermute | solution.py:348
  52.4 0.6 convert_reduce_fusion.4
  53.0 0.5 convert_element_type.19
  53.6 0.6 convert_element_type.15
  54.2 0.5 convert_element_type.18
  54.7 0.1 reshape.72
  56.1 1.3 concatenate.39.refs_0_
  57.4 1.2 concatenate.37.refs_0_
  58.6 1.3 concatenate.38.refs_0_
  59.9 0.7 fusion.21
  65.6 0.6 convert_reduce_fusion.3
  66.2 0.0 collective-permute-done.86.refs_9_
  66.2 5.1 %collective-permute-done.87.refs_10_ = bf16[2,512,128]{2,1,0:T(8,128)(2,1)} collective-permute-done((bf16[2,512,128]{2,1,0:T(8,128)(2,1)}, bf16[2,512,128]{2,1,0:T(8,128)(2,1)}, u32[]{:S(2)}, u32[]{:S(2)}) %collective-permute-start.87) | collective-permute-done | bytes 262176 | tf_op jit(solution)/shard_map/ppermute | solution.py:348
  71.4 4.8 %renew.3 = (bf16[2,512,128]{2,1,0:T(8,128)(2,1)}, bf16[2,512,128]{2,1,0:T(8,128)(2,1)}, bf16[2,512,128]{2,1,0:T(8,128)(2,1)}, bf16[2,512,128]{2,1,0:T(8,128)(2,1...) custom-call(s32[119]{0:T(128)} %concatenate.38.refs_0_, ...), custom_call_target="tpu_custom_call", output_to_operand_aliasing={{0}: (11, {}), {1}: (12, {}), {2}: (13, {}), {3}: (14, {}),... | custom-call | tf_op jit(solution)/shard_map/renew/pallas_call | solution.py:389
  76.2 10.9 %conditional.5 = ((bf16[2,512,128]{2,1,0:T(8,128)(2,1)}, bf16[2,512,128]{2,1,0:T(8,128)(2,1)}, bf16[2,512,128]{2,1,0:T(8,128)(2,1)}, bf16[2,512,128]{2,1,0:T(8,128)(2,1)})) conditional(s32[]{:T(128)} %bitcast.27, (bf16[2,512,128]{2,1,0:T(8,128)(2,1)}, bf16[2,512,128]{2,1,0:T(8,128)(2,1)}, ...), branch_computations={%region_26.27_spmd, %region_27.28_spmd, %region_28.29_spmd, %regio... | conditional | bytes 4194504 | solution.py:449
  76.3 1.9 %collective-permute-start.44 = (bf16[2,512,128]{2,1,0:T(8,128)(2,1)}, bf16[2,512,128]{2,1,0:T(8,128)(2,1)}, u32[]{:S(2)}, u32[]{:S(2)}) collective-permute-start(bf16[2,512,128]{2,1,0:T(8,128)(2,1)} %get-tuple-element.964), channel_id=1, source_target_pairs={{8,23},{9,16},{10,17},{11,18},{12,19},{13,20},{14,21},{15,22},{16,... | collective-permute-start | bytes 786440 | tf_op jit(solution)/shard_map/cond/branch_8_fun/ppermute | solution.py:444
  78.2 9.0 %collective-permute-done.44 = bf16[2,512,128]{2,1,0:T(8,128)(2,1)} collective-permute-done((bf16[2,512,128]{2,1,0:T(8,128)(2,1)}, bf16[2,512,128]{2,1,0:T(8,128)(2,1)}, u32[]{:S(2)}, u32[]{:S(2)}) %collective-permute-start.44) | collective-permute-done | bytes 262176 | tf_op jit(solution)/shard_map/cond/branch_8_fun/ppermute | solution.py:444
  87.1 4.7 %renew.4 = bf16[8,2,512,128]{3,2,1,0:T(8,128)(2,1)} custom-call(s32[119]{0:T(128)} %concatenate.37.refs_0_, bf16[2,32,512,128]{3,2,1,0:T(8,128)(2,1)} %bitcast.70, bf16[6,512,512]{2,1,0:T(8,128)(2,1)} %bitcast.74, bf16[2,512,128]{2,1,0:T(8,128)(2,1)} %get-tuple-element.1848.refs_3_, ...), custom_call_target="tpu_custom_call", output_to_operand_aliasing={{}: (11, {})} | custom-call | tf_op jit(solution)/shard_map/renew/pallas_call | solution.py:389
  91.9 0.0 copy-start.2
  91.9 4.6 %all-to-all-start.1 = ((bf16[8,2,512,128]{3,2,1,0:T(8,128)(2,1)}), bf16[8,2,512,128]{3,2,1,0:T(8,128)(2,1)}, u32[]{:S(2)}, u32[]{:S(2)}) async-start(bf16[8,2,512,128]{3,2,1,0:T(8,128)(2,1)} %renew.4), calls=%async_computation.1 | async-start | bytes 4194304 | tf_op jit(solution)/shard_map/all_to_all | solution.py:456
  96.5 0.7 pad_add_fusion.2.refs_0_
  97.2 1.4 copy.332.refs_11_
  98.6 0.7 while.58
  99.3 1.0 renew.5
  100.3 0.6 while.59
  100.9 44.7 %all-to-all-done.1.refs_1_ = bf16[8,2,512,128]{3,2,1,0:T(8,128)(2,1)} async-done(((bf16[8,2,512,128]{3,2,1,0:T(8,128)(2,1)}), bf16[8,2,512,128]{3,2,1,0:T(8,128)(2,1)}, u32[]{:S(2)}, u32[]{:S(2)}) %all-to-all-start.1) | async-done | bytes 2097184 | tf_op jit(solution)/shard_map/all_to_all | solution.py:456
  145.7 3.8 %write.1 = bf16[2,32,512,128]{3,2,1,0:T(8,128)(2,1)} custom-call(s32[63]{0:T(128)} %pad_add_fusion.2.refs_0_, bf16[8,2,512,128]{3,2,1,0:T(8,128)(2,1)} %all-to-all-done.1.refs_1_, bf16[2,512,128]{2,1,0:T(8,128)(2,1)} %get-tuple-element.1263.refs_2_, bf16[2,512,128]{2,1,0:T(8,128)(2,1)} %get-tuple-element.1264.refs_3_, ...), custom_call_target="tpu_custom_call", output_to_operand_aliasing={{}: (10, {})} | custom-call | tf_op jit(solution)/shard_map/write/pallas_call | solution.py:464
  (28 shorter events, 0.2 us)
Async XLA Ops:
  0.8 0.6 copy-start.1
  7.5 18.5 %copy-start.4 = (s32[55]{0:T(128)}, s32[55]{0:T(128)S(1)}, u32[]{:S(2)}) copy-start(s32[55]{0:T(128)S(1)} %pad_add_fusion.1.refs_0_) | copy-start | bytes 664
  8.1 22.5 %all-to-all-start = ((s32[32,1,55]{2,1,0:T(1,128)}), s32[32,1,55]{2,1,0:T(1,128)}, u32[]{:S(2)}, u32[]{:S(2)}) async-start(s32[32,1,55]{2,1,0:T(1,128)} %broadcast_in_dim.53), calls=%async_computation | async-start | bytes 32768 | tf_op jit(solution)/shard_map/all_to_all | solution.py:353
  14.2 23.0 %collective-permute-start.80 = (bf16[2,512,128]{2,1,0:T(8,128)(2,1)}, bf16[2,512,128]{2,1,0:T(8,128)(2,1)}, u32[]{:S(2)}, u32[]{:S(2)}) collective-permute-start(bf16[2,512,128]{2,1,0:T(8,128)(2,1)} %get-tuple-element.1229.refs_11_), channel_id=1, source_target_pairs={{0,8},{1,9},{2,10},{3,11},{4,12},{5,13},{6,14},{7,15},{8,16},{9,17... | collective-permute-start | bytes 786440 | tf_op jit(solution)/shard_map/ppermute | solution.py:348
  17.6 30.9 %collective-permute-start.81 = (bf16[2,512,128]{2,1,0:T(8,128)(2,1)}, bf16[2,512,128]{2,1,0:T(8,128)(2,1)}, u32[]{:S(2)}, u32[]{:S(2)}) collective-permute-start(bf16[2,512,128]{2,1,0:T(8,128)(2,1)} %get-tuple-element.1230.refs_12_), channel_id=1, source_target_pairs={{0,9},{1,10},{2,11},{3,12},{4,13},{5,14},{6,15},{7,8},{8,17},{9,18... | collective-permute-start | bytes 786440 | tf_op jit(solution)/shard_map/ppermute | solution.py:348
  19.5 30.9 %collective-permute-start.82 = (bf16[2,512,128]{2,1,0:T(8,128)(2,1)}, bf16[2,512,128]{2,1,0:T(8,128)(2,1)}, u32[]{:S(2)}, u32[]{:S(2)}) collective-permute-start(bf16[2,512,128]{2,1,0:T(8,128)(2,1)} %get-tuple-element.1231.refs_13_), channel_id=1, source_target_pairs={{0,10},{1,11},{2,12},{3,13},{4,14},{5,15},{6,8},{7,9},{8,18},{9,19... | collective-permute-start | bytes 786440 | tf_op jit(solution)/shard_map/ppermute | solution.py:348
  21.5 44.7 %collective-permute-start.83 = (bf16[2,512,128]{2,1,0:T(8,128)(2,1)}, bf16[2,512,128]{2,1,0:T(8,128)(2,1)}, u32[]{:S(2)}, u32[]{:S(2)}) collective-permute-start(bf16[2,512,128]{2,1,0:T(8,128)(2,1)} %get-tuple-element.1232.refs_14_), channel_id=1, source_target_pairs={{0,11},{1,12},{2,13},{3,14},{4,15},{5,8},{6,9},{7,10},{8,19},{9,20... | collective-permute-start | bytes 786440 | tf_op jit(solution)/shard_map/ppermute | solution.py:348
  23.4 42.8 %collective-permute-start.84 = (bf16[2,512,128]{2,1,0:T(8,128)(2,1)}, bf16[2,512,128]{2,1,0:T(8,128)(2,1)}, u32[]{:S(2)}, u32[]{:S(2)}) collective-permute-start(bf16[2,512,128]{2,1,0:T(8,128)(2,1)} %get-tuple-element.1233.refs_15_), channel_id=1, source_target_pairs={{0,12},{1,13},{2,14},{3,15},{4,8},{5,9},{6,10},{7,11},{8,20},{9,21... | collective-permute-start | bytes 786440 | tf_op jit(solution)/shard_map/ppermute | solution.py:348
  37.2 29.0 %collective-permute-start.85 = (bf16[2,512,128]{2,1,0:T(8,128)(2,1)}, bf16[2,512,128]{2,1,0:T(8,128)(2,1)}, u32[]{:S(2)}, u32[]{:S(2)}) collective-permute-start(bf16[2,512,128]{2,1,0:T(8,128)(2,1)} %get-tuple-element.1234.refs_16_), channel_id=1, source_target_pairs={{0,13},{1,14},{2,15},{3,8},{4,9},{5,10},{6,11},{7,12},{8,21},{9,22... | collective-permute-start | bytes 786440 | tf_op jit(solution)/shard_map/ppermute | solution.py:348
  48.5 17.7 %collective-permute-start.86 = (bf16[2,512,128]{2,1,0:T(8,128)(2,1)}, bf16[2,512,128]{2,1,0:T(8,128)(2,1)}, u32[]{:S(2)}, u32[]{:S(2)}) collective-permute-start(bf16[2,512,128]{2,1,0:T(8,128)(2,1)} %get-tuple-element.1235.refs_17_), channel_id=1, source_target_pairs={{0,14},{1,15},{2,8},{3,9},{4,10},{5,11},{6,12},{7,13},{8,22},{9,23... | collective-permute-start | bytes 786440 | tf_op jit(solution)/shard_map/ppermute | solution.py:348
  50.5 20.9 %collective-permute-start.87 = (bf16[2,512,128]{2,1,0:T(8,128)(2,1)}, bf16[2,512,128]{2,1,0:T(8,128)(2,1)}, u32[]{:S(2)}, u32[]{:S(2)}) collective-permute-start(bf16[2,512,128]{2,1,0:T(8,128)(2,1)} %get-tuple-element.1236.refs_18_), channel_id=1, source_target_pairs={{0,15},{1,8},{2,9},{3,10},{4,11},{5,12},{6,13},{7,14},{8,23},{9,16... | collective-permute-start | bytes 786440 | tf_op jit(solution)/shard_map/ppermute | solution.py:348
  76.3 10.9 %collective-permute-start.44 = (bf16[2,512,128]{2,1,0:T(8,128)(2,1)}, bf16[2,512,128]{2,1,0:T(8,128)(2,1)}, u32[]{:S(2)}, u32[]{:S(2)}) collective-permute-start(bf16[2,512,128]{2,1,0:T(8,128)(2,1)} %get-tuple-element.964), channel_id=1, source_target_pairs={{8,23},{9,16},{10,17},{11,18},{12,19},{13,20},{14,21},{15,22},{16,... | collective-permute-start | bytes 786440 | tf_op jit(solution)/shard_map/cond/branch_8_fun/ppermute | solution.py:444
  91.9 4.6 %copy-start.2 = (s32[1,1,6]{2,1,0:T(1,128)S(1)}, s32[1,1,6]{2,1,0:T(1,128)}, u32[]{:S(2)}) copy-start(s32[1,1,6]{2,1,0:T(1,128)} %refs_1_.1) | copy-start | bytes 76
  91.9 4.6 %copy-start.3 = (s32[48]{0:T(128)S(1)}, s32[48]{0:T(128)}, u32[]{:S(2)}) copy-start(s32[48]{0:T(128)} %reshape_squeeze.3) | copy-start | bytes 580
  91.9 4.6 %copy-start.5 = (s32[8]{0:T(128)S(1)}, s32[8]{0:T(128)}, u32[]{:S(2)}) copy-start(s32[8]{0:T(128)} %convert_element_type.15) | copy-start | bytes 100
  91.9 5.3 %copy-start = (bf16[8,2,512,128]{3,2,1,0:T(8,128)(2,1)S(1)}, bf16[8,2,512,128]{3,2,1,0:T(8,128)(2,1)}, u32[]{:S(2)}) copy-start(bf16[8,2,512,128]{3,2,1,0:T(8,128)(2,1)} %renew.4) | copy-start | bytes 6291460
  91.9 53.7 %all-to-all-start.1 = ((bf16[8,2,512,128]{3,2,1,0:T(8,128)(2,1)}), bf16[8,2,512,128]{3,2,1,0:T(8,128)(2,1)}, u32[]{:S(2)}, u32[]{:S(2)}) async-start(bf16[8,2,512,128]{3,2,1,0:T(8,128)(2,1)} %renew.4), calls=%async_computation.1 | async-start | bytes 4194304 | tf_op jit(solution)/shard_map/all_to_all | solution.py:456
  97.2 1.4 copy-start.6

commit v4 on v3

--- a/solution.py
+++ b/solution.py
@@ -233,9 +233,8 @@
 
 
 def write_kernel(owned, senders, stored, batches, table, recv, *refs):
-    fixes, refs = refs[:senders], refs[senders:]
     _, out, arrived, total, made, here, in_sem, out_sem = refs
-    rows, _, place, fixed = read_table(table, senders, stored)
+    rows, _, place, _ = read_table(table, senders, stored)
     hit_rows(rows, senders, place, owned, stored, here)
 
     def take(sender):
@@ -251,16 +250,11 @@
             total += same.astype(jnp.int32)
         return total
 
-    for step in range(senders):
-        sender = lax.rem(place - step + senders, senders)
-
-        @pl.when((here[sender] >= 0) & (fixed(sender) == 0))
+    @pl.loop(0, senders)
+    def _(sender):
+        @pl.when(here[sender] >= 0)
         def _():
             take(sender).start()
-
-        @pl.when((here[sender] >= 0) & (fixed(sender) > 0))
-        def _():
-            pltpu.make_async_copy(fixes[step], arrived.at[sender], in_sem.at[sender]).start()
 
     @pl.loop(0, senders)
     def _(sender):
@@ -319,10 +313,10 @@
     slot = jax.ShapeDtypeStruct(tile, dtype)
     held = jax.ShapeDtypeStruct((senders,) + tile, dtype)
 
-    def pairs(step, down=1, top=0):
+    def pairs(step, top=0):
         return [
-            (i * senders + j, (i + down) * senders + (j + step) % senders)
-            for i in range(top, layers - down)
+            (i * senders + j, (i + 1) * senders + (j + step) % senders)
+            for i in range(top, layers - 1)
             for j in range(senders)
         ]
 
@@ -358,25 +352,16 @@
     feeds = rows_all[:-1, :, None] == cols_all[1:, None, :]
     read = jnp.any(feeds, axis=2)
     home = jnp.repeat(jnp.arange(senders, dtype=jnp.int32), stored)
-    shift_all = (rows_all // owned - home[None, :]) % senders
-    shift = shift_all[:-1]
+    shift = (rows_all[:-1] // owned - home[None, :]) % senders
     steps = jnp.arange(senders, dtype=jnp.int32)
     changed = jnp.any(feeds, axis=1)
-    later = jnp.zeros(changed.shape, bool)
     masks = []
-    group = 4 if senders <= 8 else 2
     for wave in range(2, layers):
         below = jnp.concatenate([jnp.zeros((1, blocks_all), bool), changed[:-1]])
         again = below & read
         mask = jnp.any(again[:, :, None] & (shift[:, :, None] == steps), axis=(0, 1)).astype(jnp.int32)
         masks.append(mask)
         changed = jnp.any(feeds & below[:, :, None], axis=1)
-        if wave > 2:
-            later |= changed
-    late_mask = jnp.any(later[:, :, None] & (shift_all[1:, :, None] == steps), axis=(0, 1)).astype(jnp.int32)
-    mine_later = lax.dynamic_index_in_dim(later, jnp.maximum(depth - 1, 0), 0, keepdims=False) & (depth > 0)
-    to_me = (rows // owned == place).reshape(-1) & mine_later
-    fixed = jnp.any(to_me.reshape(senders, stored), axis=1).astype(jnp.int32)
 
     above = lax.dynamic_index_in_dim(rows_all, jnp.maximum(depth - 1, 0), 0, keepdims=False)
     above = above.reshape(senders, stored)
@@ -413,58 +398,42 @@
         out_shape=jax.ShapeDtypeStruct((batches, owned, width, shots), dtype),
         in_specs=[SMEM, ANY],
         out_specs=ANY,
-        scratch_shapes=[pltpu.VMEM((width, shots), dtype), pltpu.SMEM((senders,), jnp.int32), DMA((batches, owned))],
+        scratch_shapes=[
+            pltpu.VMEM((width, shots), dtype),
+            pltpu.SMEM((senders,), jnp.int32),
+            DMA((batches, owned)),
+        ],
         compiler_params=PARAMS,
         name="zeros",
     )(table, mine)
 
     *slots, kept = renew(kept, jnp.int32(1), tuple(slots), (traces,))
-
-    def again(step, kept, down, top):
-        sent = lax.dynamic_index_in_dim(kept, (place + step) % senders, 0, keepdims=False)
-        return lax.ppermute(sent, AXES, pairs(step, down, top))
-
-    def one_by_one(mask, send, came):
-        def resend(carry):
-            left, mask, came = carry
-            step = jnp.argmax(mask).astype(jnp.int32)
-            branches = [
-                lambda came, step=step: came[:step] + (send(step),) + came[step + 1 :] for step in range(senders)
-            ]
-            return left - 1, jnp.where(steps == step, 0, mask), lax.switch(step, branches, came)
-
-        return lax.while_loop(lambda carry: carry[0] > 0, resend, (jnp.sum(mask), mask, tuple(came)))[2]
-
-    if masks:
+    for wave, mask in enumerate(masks, 2):
+        group = 4 if wave == 2 and senders <= 8 else 2
         for low in range(0, senders, group):
             near = range(low, min(low + group, senders))
 
             def resend(which):
                 return lambda new, old: tuple(
-                    lax.ppermute(new[at], AXES, pairs(step, 1, 1)) if which >> at & 1 else old[at]
+                    lax.ppermute(new[at], AXES, pairs(step, wave - 1)) if which >> at & 1 else old[at]
                     for at, step in enumerate(near)
                 )
 
-            code = sum(masks[0][step] << at for at, step in enumerate(near))
+            code = sum(mask[step] << at for at, step in enumerate(near))
             recv[low : low + group] = lax.switch(
                 code,
                 [resend(which) for which in range(1 << len(near))],
                 tuple(slots[low : low + group]),
                 tuple(recv[low : low + group]),
             )
-        (kept,) = renew(kept, jnp.where(depth >= 2, jnp.max(masks[0]), 0))
+        go = jnp.where(depth >= wave, jnp.max(mask), 0)
+        *slots, kept = renew(kept, go, tuple(slots) if wave + 1 < layers else ())
     arrived = lax.all_to_all(kept, "trace", split_axis=0, concat_axis=0, tiled=True)
-
-    late = kept
-    for wave, mask in enumerate(masks[1:], 3):
-        recv = list(one_by_one(mask, lambda step, late=late, wave=wave: again(step, late, 1, wave - 1), recv))
-        (late,) = renew(late, jnp.where(depth >= wave, jnp.max(mask), 0))
-    fixes = one_by_one(late_mask, lambda step: again(step, late, 0, 0), recv)
 
     traces = pl.pallas_call(
         lambda *refs: write_kernel(owned, senders, stored, batches, *refs),
         out_shape=jax.ShapeDtypeStruct((batches, owned, width, shots), dtype),
-        in_specs=[SMEM] + [ANY] * (senders + 2),
+        in_specs=[SMEM] + [ANY] * 2,
         out_specs=ANY,
         scratch_shapes=[
             pltpu.VMEM((senders,) + tile, dtype),
@@ -474,10 +443,10 @@
             DMA((senders,)),
             DMA((senders, batches)),
         ],
-        input_output_aliases={2 + senders: 0},
+        input_output_aliases={2: 0},
         compiler_params=PARAMS,
         name="write",
-    )(jnp.concatenate([table, fixed]), arrived, *fixes, traces)
+    )(table, arrived, traces)
     return traces.reshape(1, batches, local, shots)
 
 

time: 150 us -> 152 us (1.013)
  blocking collectives: 0 us -> 53.9 us
  waiting for transfers between devices: 58.8 us -> 10.2 us
  between operations: 6.54 us -> 11.6 us
  other arithmetic: 8.28 us -> 3.71 us
  starting transfers between devices: 38.8 us -> 36.2 us
    all_to_all x0 -> x1, blocking collectives: none -> 53.9 us  [body(): lax.all_to_all(kept, 'trace', split_axis=0, concat_axis=0, tiled=True)]
    all_to_all x1 -> x0, waiting for transfers between devices: 44.7 us -> none  [body(): lax.all_to_all(kept, 'trace', split_axis=0, concat_axis=0, tiled=True)]
    all_to_all x1 -> x0, starting transfers between devices: 4.59 us -> none  [body(): lax.all_to_all(kept, 'trace', split_axis=0, concat_axis=0, tiled=True)]
    ppermute x8, waiting for transfers between devices: 5.13 us -> 1.17 us  [body(): recv[step] = lax.ppermute(slots[step], AXES, pairs(step))]
  transfers between devices with their start and end apart: 11 -> 10, of which waited for: 3 -> 2; matrix products, arithmetic and copies ran while one was open for 12% -> 8% of each run, Pallas kernels for 3% -> 3%
where the time goes in v4:
time: 152 us; the launch traced here: 151 us
  blocking collectives  53.9 us (35%)
  starting transfers between devices  36.2 us (24%)
  Pallas kernels  23.4 us (15%)
  between operations  11.6 us (8%)
  local copies, waits for them, and re-layouts  11.4 us (8%)
  waiting for transfers between devices  10.2 us (7%)
  other arithmetic  3.71 us (2%)
    all_to_all x1, blocking collectives, body(): lax.all_to_all(kept, 'trace', split_axis=0, concat_axis=0, tiled=True)  53.9 us
    ppermute x8, starting transfers between devices, body(): recv[step] = lax.ppermute(slots[step], AXES, pairs(step))  27.4 us
    pallas_call x3, Pallas kernels, renew(): pl.pallas_call(lambda *refs: renew_kernel(senders, owned, len(after), res...  10.7 us
    ppermute x1, waiting for transfers between devices, resend(): lax.ppermute(new[at], AXES, pairs(step, wave - 1))  9.06 us
    all_to_all x1, starting transfers between devices, body(): known = lax.all_to_all(mine, AXES, split_axis=0, concat_axis=0, tiled=True)  6.11 us
    pallas_call x1, Pallas kernels, body(): pl.pallas_call(lambda *refs: first_kernel(senders, owned, *refs), out_sha...  4.85 us
    pallas_call x1, Pallas kernels, body(): pl.pallas_call(lambda *refs: zero_kernel(owned, senders, stored, batches,...  4.02 us
    pallas_call x1, Pallas kernels, body(): pl.pallas_call(lambda *refs: write_kernel(owned, senders, stored, batches...  3.82 us
  transfers between devices with their start and end apart: 10, of which 2 were waited for; matrix products, arithmetic and copies ran while one was open for 8% of the time, Pallas kernels for 3%

profile of v4, /device:TPU:4, one launch (start us, length us, event | category | flops | bytes accessed | tf_op | source)
XLA Modules:
  0.0 150.6 jit_solution(16010529403770073913)
XLA Ops:
  0.0 0.8 copy.34.refs_0_
  0.8 0.0 copy-start
  0.8 0.6 copy-done
  1.4 0.6 reshape_squeeze.3
  2.0 4.8 %first.1 = (bf16[2,512,128]{2,1,0:T(8,128)(2,1)}, bf16[2,512,128]{2,1,0:T(8,128)(2,1)}, bf16[2,512,128]{2,1,0:T(8,128)(2,1)}, bf16[2,512,128]{2,1,0:T(8,128)(2,1...) custom-call(s32[1,8,6]{2,1,0:T(8,128)} %copy-done, ...), custom_call_target="tpu_custom_call" | custom-call | tf_op jit(solution)/shard_map/first/pallas_call | solution.py:323
  6.8 0.7 pad_add_fusion.1.refs_0_
  7.5 0.0 copy-start.1
  7.5 0.6 broadcast_in_dim.17
  8.2 6.1 %all-to-all-start = ((s32[32,1,55]{2,1,0:T(1,128)}), s32[32,1,55]{2,1,0:T(1,128)}, u32[]{:S(2)}, u32[]{:S(2)}) async-start(s32[32,1,55]{2,1,0:T(1,128)} %broadcast_in_dim.17), calls=%async_computation | async-start | bytes 32768 | tf_op jit(solution)/shard_map/all_to_all | solution.py:347
  14.3 3.4 %collective-permute-start.80 = (bf16[2,512,128]{2,1,0:T(8,128)(2,1)}, bf16[2,512,128]{2,1,0:T(8,128)(2,1)}, u32[]{:S(2)}, u32[]{:S(2)}) collective-permute-start(bf16[2,512,128]{2,1,0:T(8,128)(2,1)} %get-tuple-element.516.refs_11_), channel_id=1, source_target_pairs={{0,8},{1,9},{2,10},{3,11},{4,12},{5,13},{6,14},{7,15},{8,16},{9,17... | collective-permute-start | bytes 786440 | tf_op jit(solution)/shard_map/ppermute | solution.py:342
  17.7 1.9 %collective-permute-start.81 = (bf16[2,512,128]{2,1,0:T(8,128)(2,1)}, bf16[2,512,128]{2,1,0:T(8,128)(2,1)}, u32[]{:S(2)}, u32[]{:S(2)}) collective-permute-start(bf16[2,512,128]{2,1,0:T(8,128)(2,1)} %get-tuple-element.517.refs_12_), channel_id=1, source_target_pairs={{0,9},{1,10},{2,11},{3,12},{4,13},{5,14},{6,15},{7,8},{8,17},{9,18... | collective-permute-start | bytes 786440 | tf_op jit(solution)/shard_map/ppermute | solution.py:342
  19.6 1.9 %collective-permute-start.82 = (bf16[2,512,128]{2,1,0:T(8,128)(2,1)}, bf16[2,512,128]{2,1,0:T(8,128)(2,1)}, u32[]{:S(2)}, u32[]{:S(2)}) collective-permute-start(bf16[2,512,128]{2,1,0:T(8,128)(2,1)} %get-tuple-element.518.refs_13_), channel_id=1, source_target_pairs={{0,10},{1,11},{2,12},{3,13},{4,14},{5,15},{6,8},{7,9},{8,18},{9,19... | collective-permute-start | bytes 786440 | tf_op jit(solution)/shard_map/ppermute | solution.py:342
  21.5 1.9 %collective-permute-start.83 = (bf16[2,512,128]{2,1,0:T(8,128)(2,1)}, bf16[2,512,128]{2,1,0:T(8,128)(2,1)}, u32[]{:S(2)}, u32[]{:S(2)}) collective-permute-start(bf16[2,512,128]{2,1,0:T(8,128)(2,1)} %get-tuple-element.519.refs_14_), channel_id=1, source_target_pairs={{0,11},{1,12},{2,13},{3,14},{4,15},{5,8},{6,9},{7,10},{8,19},{9,20... | collective-permute-start | bytes 786440 | tf_op jit(solution)/shard_map/ppermute | solution.py:342
  23.4 1.9 %collective-permute-start.84 = (bf16[2,512,128]{2,1,0:T(8,128)(2,1)}, bf16[2,512,128]{2,1,0:T(8,128)(2,1)}, u32[]{:S(2)}, u32[]{:S(2)}) collective-permute-start(bf16[2,512,128]{2,1,0:T(8,128)(2,1)} %get-tuple-element.520.refs_15_), channel_id=1, source_target_pairs={{0,12},{1,13},{2,14},{3,15},{4,8},{5,9},{6,10},{7,11},{8,20},{9,21... | collective-permute-start | bytes 786440 | tf_op jit(solution)/shard_map/ppermute | solution.py:342
  25.4 0.6 sub.24
  26.0 0.0 copy-done.1
  26.0 0.6 broadcast_in_dim.41.refs_1_
  26.6 4.0 %zeros.1.refs_20_.refs_2_ = bf16[2,32,512,128]{3,2,1,0:T(8,128)(2,1)} custom-call(s32[55]{0:T(128)} %copy-done.1, s32[32,55]{1,0:T(8,128)} %broadcast_in_dim.41.refs_1_), custom_call_target="tpu_custom_call" | custom-call | tf_op jit(solution)/shard_map/zeros/pallas_call | solution.py:396
  30.6 0.0 all-to-all-done
  30.6 0.7 slice.90
  31.3 0.7 slice.92
  32.1 0.8 slice.91
  32.8 0.6 add_select_fusion
  33.5 0.1 eq.28
  33.5 0.1 compare_reduce_fusion.1
  33.7 0.2 fusion
  33.9 0.1 eq.62
  34.0 0.9 and_reduce_fusion
  35.0 0.1 add_reduce_fusion
  35.1 0.1 copy.36
  35.2 0.1 fusion.4
  35.3 0.7 convert_reduce_fusion.1
  36.0 0.0 collective-permute-done.80.refs_3_
  36.1 12.5 %collective-permute-start.85 = (bf16[2,512,128]{2,1,0:T(8,128)(2,1)}, bf16[2,512,128]{2,1,0:T(8,128)(2,1)}, u32[]{:S(2)}, u32[]{:S(2)}) collective-permute-start(bf16[2,512,128]{2,1,0:T(8,128)(2,1)} %get-tuple-element.521.refs_16_), channel_id=1, source_target_pairs={{0,13},{1,14},{2,15},{3,8},{4,9},{5,10},{6,11},{7,12},{8,21},{9,22... | collective-permute-start | bytes 786440 | tf_op jit(solution)/shard_map/ppermute | solution.py:342
  48.6 0.0 collective-permute-done.81.refs_4_
  48.6 1.9 %collective-permute-start.86 = (bf16[2,512,128]{2,1,0:T(8,128)(2,1)}, bf16[2,512,128]{2,1,0:T(8,128)(2,1)}, u32[]{:S(2)}, u32[]{:S(2)}) collective-permute-start(bf16[2,512,128]{2,1,0:T(8,128)(2,1)} %get-tuple-element.522.refs_17_), channel_id=1, source_target_pairs={{0,14},{1,15},{2,8},{3,9},{4,10},{5,11},{6,12},{7,13},{8,22},{9,23... | collective-permute-start | bytes 786440 | tf_op jit(solution)/shard_map/ppermute | solution.py:342
  50.5 0.0 collective-permute-done.82.refs_5_
  50.5 1.9 %collective-permute-start.87 = (bf16[2,512,128]{2,1,0:T(8,128)(2,1)}, bf16[2,512,128]{2,1,0:T(8,128)(2,1)}, u32[]{:S(2)}, u32[]{:S(2)}) collective-permute-start(bf16[2,512,128]{2,1,0:T(8,128)(2,1)} %get-tuple-element.523.refs_18_), channel_id=1, source_target_pairs={{0,15},{1,8},{2,9},{3,10},{4,11},{5,12},{6,13},{7,14},{8,23},{9,16... | collective-permute-start | bytes 786440 | tf_op jit(solution)/shard_map/ppermute | solution.py:342
  52.4 0.1 pad_add_fusion
  52.5 0.1 reshape.146
  53.8 1.3 concatenate.34.refs_0_
  55.1 1.3 concatenate.32.refs_0_
  56.4 1.2 concatenate.33.refs_0_
  57.6 0.7 fusion.9
  63.3 0.7 fusion.10
  69.1 0.0 collective-permute-done.83.refs_6_
  69.1 0.0 collective-permute-done.84.refs_7_
  69.1 0.0 collective-permute-done.85.refs_8_
  69.1 0.0 collective-permute-done.86.refs_9_
  69.1 1.2 collective-permute-done.87.refs_10_
  70.3 4.9 %renew.3 = (bf16[2,512,128]{2,1,0:T(8,128)(2,1)}, bf16[2,512,128]{2,1,0:T(8,128)(2,1)}, bf16[2,512,128]{2,1,0:T(8,128)(2,1)}, bf16[2,512,128]{2,1,0:T(8,128)(2,1...) custom-call(s32[119]{0:T(128)} %concatenate.33.refs_0_, ...), custom_call_target="tpu_custom_call", output_to_operand_aliasing={{0}: (11, {}), {1}: (12, {}), {2}: (13, {}), {3}: (14, {}),... | custom-call | tf_op jit(solution)/shard_map/renew/pallas_call | solution.py:374
  75.2 11.7 %conditional.7 = ((bf16[2,512,128]{2,1,0:T(8,128)(2,1)}, bf16[2,512,128]{2,1,0:T(8,128)(2,1)}, bf16[2,512,128]{2,1,0:T(8,128)(2,1)}, bf16[2,512,128]{2,1,0:T(8,128)(2,1)})) conditional(s32[]{:T(128)} %bitcast.11, (bf16[2,512,128]{2,1,0:T(8,128)(2,1)}, bf16[2,512,128]{2,1,0:T(8,128)(2,1)}, ...), branch_computations={%region_26.27_spmd, %region_27.28_spmd, %region_28.29_spmd, %regio... | conditional | bytes 4194504 | solution.py:423
  75.2 2.7 %collective-permute-start.44 = (bf16[2,512,128]{2,1,0:T(8,128)(2,1)}, bf16[2,512,128]{2,1,0:T(8,128)(2,1)}, u32[]{:S(2)}, u32[]{:S(2)}) collective-permute-start(bf16[2,512,128]{2,1,0:T(8,128)(2,1)} %get-tuple-element.416), channel_id=1, source_target_pairs={{8,23},{9,16},{10,17},{11,18},{12,19},{13,20},{14,21},{15,22},{16,... | collective-permute-start | bytes 786440 | tf_op jit(solution)/shard_map/cond/branch_8_fun/ppermute | solution.py:418
  77.8 9.1 %collective-permute-done.44 = bf16[2,512,128]{2,1,0:T(8,128)(2,1)} collective-permute-done((bf16[2,512,128]{2,1,0:T(8,128)(2,1)}, bf16[2,512,128]{2,1,0:T(8,128)(2,1)}, u32[]{:S(2)}, u32[]{:S(2)}) %collective-permute-start.44) | collective-permute-done | bytes 262176 | tf_op jit(solution)/shard_map/cond/branch_8_fun/ppermute | solution.py:418
  86.9 4.9 %renew.4 = (bf16[2,512,128]{2,1,0:T(8,128)(2,1)}, bf16[2,512,128]{2,1,0:T(8,128)(2,1)}, bf16[2,512,128]{2,1,0:T(8,128)(2,1)}, bf16[2,512,128]{2,1,0:T(8,128)(2,1...) custom-call(s32[119]{0:T(128)} %concatenate.34.refs_0_, ...), custom_call_target="tpu_custom_call", output_to_operand_aliasing={{0}: (11, {}), {1}: (12, {}), {2}: (13, {}), {3}: (14, {}),... | custom-call | tf_op jit(solution)/shard_map/renew/pallas_call | solution.py:374
  91.9 1.0 renew.5
  92.9 53.9 %all_to_all.11.refs_1_ = bf16[8,2,512,128]{3,2,1,0:T(8,128)(2,1)} all-to-all(bf16[8,2,512,128]{3,2,1,0:T(8,128)(2,1)} %renew.5), channel_id=1, replica_groups=mesh['layer'=4,'trace'=8] {'trace'}, dimensions={0} | all-to-all | bytes 4194304 | tf_op jit(solution)/shard_map/all_to_all | solution.py:431
  146.8 3.8 %write.1 = bf16[2,32,512,128]{3,2,1,0:T(8,128)(2,1)} custom-call(s32[55]{0:T(128)} %copy-done.1, bf16[8,2,512,128]{3,2,1,0:T(8,128)(2,1)} %all_to_all.11.refs_1_, bf16[2,32,512,128]{3,2,1,0:T(8,128)(2,1)} %zeros.1.refs_20_.refs_2_), custom_call_target="tpu_custom_call", output_to_operand_aliasing={{}: (2, {})} | custom-call | tf_op jit(solution)/shard_map/write/pallas_call | solution.py:433
  (14 shorter events, 0.2 us)
Async XLA Ops:
  0.8 0.6 copy-start
  7.5 18.4 %copy-start.1 = (s32[55]{0:T(128)}, s32[55]{0:T(128)S(1)}, u32[]{:S(2)}) copy-start(s32[55]{0:T(128)S(1)} %pad_add_fusion.1.refs_0_) | copy-start | bytes 664
  8.2 22.5 %all-to-all-start = ((s32[32,1,55]{2,1,0:T(1,128)}), s32[32,1,55]{2,1,0:T(1,128)}, u32[]{:S(2)}, u32[]{:S(2)}) async-start(s32[32,1,55]{2,1,0:T(1,128)} %broadcast_in_dim.17), calls=%async_computation | async-start | bytes 32768 | tf_op jit(solution)/shard_map/all_to_all | solution.py:347
  14.3 21.8 %collective-permute-start.80 = (bf16[2,512,128]{2,1,0:T(8,128)(2,1)}, bf16[2,512,128]{2,1,0:T(8,128)(2,1)}, u32[]{:S(2)}, u32[]{:S(2)}) collective-permute-start(bf16[2,512,128]{2,1,0:T(8,128)(2,1)} %get-tuple-element.516.refs_11_), channel_id=1, source_target_pairs={{0,8},{1,9},{2,10},{3,11},{4,12},{5,13},{6,14},{7,15},{8,16},{9,17... | collective-permute-start | bytes 786440 | tf_op jit(solution)/shard_map/ppermute | solution.py:342
  17.7 30.9 %collective-permute-start.81 = (bf16[2,512,128]{2,1,0:T(8,128)(2,1)}, bf16[2,512,128]{2,1,0:T(8,128)(2,1)}, u32[]{:S(2)}, u32[]{:S(2)}) collective-permute-start(bf16[2,512,128]{2,1,0:T(8,128)(2,1)} %get-tuple-element.517.refs_12_), channel_id=1, source_target_pairs={{0,9},{1,10},{2,11},{3,12},{4,13},{5,14},{6,15},{7,8},{8,17},{9,18... | collective-permute-start | bytes 786440 | tf_op jit(solution)/shard_map/ppermute | solution.py:342
  19.6 30.9 %collective-permute-start.82 = (bf16[2,512,128]{2,1,0:T(8,128)(2,1)}, bf16[2,512,128]{2,1,0:T(8,128)(2,1)}, u32[]{:S(2)}, u32[]{:S(2)}) collective-permute-start(bf16[2,512,128]{2,1,0:T(8,128)(2,1)} %get-tuple-element.518.refs_13_), channel_id=1, source_target_pairs={{0,10},{1,11},{2,12},{3,13},{4,14},{5,15},{6,8},{7,9},{8,18},{9,19... | collective-permute-start | bytes 786440 | tf_op jit(solution)/shard_map/ppermute | solution.py:342
  21.5 47.5 %collective-permute-start.83 = (bf16[2,512,128]{2,1,0:T(8,128)(2,1)}, bf16[2,512,128]{2,1,0:T(8,128)(2,1)}, u32[]{:S(2)}, u32[]{:S(2)}) collective-permute-start(bf16[2,512,128]{2,1,0:T(8,128)(2,1)} %get-tuple-element.519.refs_14_), channel_id=1, source_target_pairs={{0,11},{1,12},{2,13},{3,14},{4,15},{5,8},{6,9},{7,10},{8,19},{9,20... | collective-permute-start | bytes 786440 | tf_op jit(solution)/shard_map/ppermute | solution.py:342
  23.4 45.6 %collective-permute-start.84 = (bf16[2,512,128]{2,1,0:T(8,128)(2,1)}, bf16[2,512,128]{2,1,0:T(8,128)(2,1)}, u32[]{:S(2)}, u32[]{:S(2)}) collective-permute-start(bf16[2,512,128]{2,1,0:T(8,128)(2,1)} %get-tuple-element.520.refs_15_), channel_id=1, source_target_pairs={{0,12},{1,13},{2,14},{3,15},{4,8},{5,9},{6,10},{7,11},{8,20},{9,21... | collective-permute-start | bytes 786440 | tf_op jit(solution)/shard_map/ppermute | solution.py:342
  36.1 33.0 %collective-permute-start.85 = (bf16[2,512,128]{2,1,0:T(8,128)(2,1)}, bf16[2,512,128]{2,1,0:T(8,128)(2,1)}, u32[]{:S(2)}, u32[]{:S(2)}) collective-permute-start(bf16[2,512,128]{2,1,0:T(8,128)(2,1)} %get-tuple-element.521.refs_16_), channel_id=1, source_target_pairs={{0,13},{1,14},{2,15},{3,8},{4,9},{5,10},{6,11},{7,12},{8,21},{9,22... | collective-permute-start | bytes 786440 | tf_op jit(solution)/shard_map/ppermute | solution.py:342
  48.6 20.5 %collective-permute-start.86 = (bf16[2,512,128]{2,1,0:T(8,128)(2,1)}, bf16[2,512,128]{2,1,0:T(8,128)(2,1)}, u32[]{:S(2)}, u32[]{:S(2)}) collective-permute-start(bf16[2,512,128]{2,1,0:T(8,128)(2,1)} %get-tuple-element.522.refs_17_), channel_id=1, source_target_pairs={{0,14},{1,15},{2,8},{3,9},{4,10},{5,11},{6,12},{7,13},{8,22},{9,23... | collective-permute-start | bytes 786440 | tf_op jit(solution)/shard_map/ppermute | solution.py:342
  50.5 19.8 %collective-permute-start.87 = (bf16[2,512,128]{2,1,0:T(8,128)(2,1)}, bf16[2,512,128]{2,1,0:T(8,128)(2,1)}, u32[]{:S(2)}, u32[]{:S(2)}) collective-permute-start(bf16[2,512,128]{2,1,0:T(8,128)(2,1)} %get-tuple-element.523.refs_18_), channel_id=1, source_target_pairs={{0,15},{1,8},{2,9},{3,10},{4,11},{5,12},{6,13},{7,14},{8,23},{9,16... | collective-permute-start | bytes 786440 | tf_op jit(solution)/shard_map/ppermute | solution.py:342
  75.2 11.7 %collective-permute-start.44 = (bf16[2,512,128]{2,1,0:T(8,128)(2,1)}, bf16[2,512,128]{2,1,0:T(8,128)(2,1)}, u32[]{:S(2)}, u32[]{:S(2)}) collective-permute-start(bf16[2,512,128]{2,1,0:T(8,128)(2,1)} %get-tuple-element.416), channel_id=1, source_target_pairs={{8,23},{9,16},{10,17},{11,18},{12,19},{13,20},{14,21},{15,22},{16,... | collective-permute-start | bytes 786440 | tf_op jit(solution)/shard_map/cond/branch_8_fun/ppermute | solution.py:418

commit v5 on v4

--- a/solution.py
+++ b/solution.py
@@ -36,7 +36,7 @@
 
 def first_kernel(senders, owned, rows_ref, cols_ref, source, blocks, *refs):
     slots, refs = refs[:senders], refs[senders:]
-    kept, operand, pieces, made, op_sem, in_sem, slot_sem, keep_sem = refs
+    operand, pieces, made, op_sem, in_sem, slot_sem = refs
     stored, _ = blocks.shape[:2]
     place = lax.axis_index("trace")
     batches, shots = source.shape[0], source.shape[-1]
@@ -56,9 +56,6 @@
 
     def give(block, slot):
         return pltpu.make_async_copy(made.at[block], slots[slot], slot_sem.at[block])
-
-    def keep(block, owner):
-        return pltpu.make_async_copy(made.at[block], kept.at[owner], keep_sem.at[block])
 
     @pl.loop(0, stored)
     def _(block):
@@ -82,18 +79,15 @@
             def _():
                 give(block, slot).start()
 
-        keep(block, owner).start()
-
     @pl.loop(0, stored)
     def _(block):
         give(block, 0).wait()
-        keep(block, 0).wait()
-
-
-def renew_kernel(senders, owned, others, resent, table, source, blocks, *refs):
-    recv, refs = refs[:senders], refs[senders + 1 + resent + others :]
-    slots, refs = refs[:resent], refs[resent:]
-    kept, operand, pieces, arrived, total, made, op_sem, in_sem, recv_sem, keep_sem, slot_sem = refs
+
+
+def renew_kernel(senders, owned, others, table, source, blocks, *refs):
+    recv, refs = refs[:senders], refs[2 * senders + others :]
+    slots, refs = refs[:senders], refs[senders:]
+    operand, pieces, arrived, total, made, op_sem, in_sem, recv_sem, slot_sem = refs
     stored, _ = blocks.shape[:2]
     rows, cols, place, more = read_table(table, senders, stored)
     go = more(0) > 0
@@ -115,9 +109,6 @@
 
     def take(step):
         return pltpu.make_async_copy(recv[step], arrived.at[step], recv_sem.at[step])
-
-    def keep(block, owner):
-        return pltpu.make_async_copy(made.at[block], kept.at[owner], keep_sem.at[block])
 
     def give(block, slot):
         return pltpu.make_async_copy(made.at[block], slots[slot], slot_sem.at[block])
@@ -175,8 +166,7 @@
                 for batch in range(batches):
                     made[block, batch] = product[:, batch * shots : (batch + 1) * shots].astype(made.dtype)
                 owner = owner_of(rows(place, block), owned)
-                keep(block, owner).start()
-                for slot in range(resent):
+                for slot in range(senders):
 
                     @pl.when(lax.rem(owner - place + senders, senders) == slot)
                     def _():
@@ -186,9 +176,7 @@
         def _(block):
             @pl.when(hits(block) > 0)
             def _():
-                keep(block, 0).wait()
-                if resent:
-                    give(block, 0).wait()
+                give(block, 0).wait()
 
 
 def hit_rows(rows, senders, place, owned, stored, here):
@@ -232,13 +220,14 @@
                 put(batch, row).wait()
 
 
-def write_kernel(owned, senders, stored, batches, table, recv, *refs):
-    _, out, arrived, total, made, here, in_sem, out_sem = refs
+def write_kernel(owned, senders, stored, batches, table, *refs):
+    recv, refs = refs[:senders], refs[senders + 1 :]
+    out, arrived, total, made, here, in_sem, out_sem = refs
     rows, _, place, _ = read_table(table, senders, stored)
     hit_rows(rows, senders, place, owned, stored, here)
 
-    def take(sender):
-        return pltpu.make_async_copy(recv.at[sender], arrived.at[sender], in_sem.at[sender])
+    def take(step, sender):
+        return pltpu.make_async_copy(recv[step], arrived.at[sender], in_sem.at[sender])
 
     def put(sender, batch, box):
         return pltpu.make_async_copy(box.at[sender, batch], out.at[batch, here[sender]], out_sem.at[sender, batch])
@@ -250,17 +239,18 @@
             total += same.astype(jnp.int32)
         return total
 
+    for step in range(senders):
+        sender = lax.rem(place - step + senders, senders)
+
+        @pl.when(here[sender] >= 0)
+        def _():
+            take(step, sender).start()
+
     @pl.loop(0, senders)
     def _(sender):
         @pl.when(here[sender] >= 0)
         def _():
-            take(sender).start()
-
-    @pl.loop(0, senders)
-    def _(sender):
-        @pl.when(here[sender] >= 0)
-        def _():
-            take(sender).wait()
+            take(0, sender).wait()
 
     @pl.loop(0, senders)
     def _(sender):
@@ -311,7 +301,6 @@
     dtype = sources.dtype
     tile = (batches, width, shots)
     slot = jax.ShapeDtypeStruct(tile, dtype)
-    held = jax.ShapeDtypeStruct((senders,) + tile, dtype)
 
     def pairs(step, top=0):
         return [
@@ -320,18 +309,17 @@
             for j in range(senders)
         ]
 
-    *slots, kept = pl.pallas_call(
+    slots = pl.pallas_call(
         lambda *refs: first_kernel(senders, owned, *refs),
-        out_shape=(slot,) * senders + (held,),
+        out_shape=(slot,) * senders,
         in_specs=[SMEM] * 2 + [ANY] * 2,
-        out_specs=(ANY,) * (senders + 1),
+        out_specs=(ANY,) * senders,
         scratch_shapes=[
             pltpu.VMEM((stored, width, width), dtype),
             pltpu.VMEM((stored, width, batches * shots), dtype),
             pltpu.VMEM((stored,) + tile, dtype),
             DMA((stored,)),
             DMA((stored, batches)),
-            DMA((stored,)),
             DMA((stored,)),
         ],
         compiler_params=PARAMS,
@@ -342,7 +330,7 @@
         recv[step] = lax.ppermute(slots[step], AXES, pairs(step))
 
     total = layers * senders
-    mine, kept = lax.optimization_barrier((table, kept))
+    mine, slots = lax.optimization_barrier((table, slots))
     mine = jnp.broadcast_to(mine[None], (total, mine.shape[0]))
     known = lax.all_to_all(mine, AXES, split_axis=0, concat_axis=0, tiled=True)
     known = known.reshape(layers, senders, -1)
@@ -369,13 +357,12 @@
     match = jnp.concatenate([match, jnp.max(match, axis=0, keepdims=True)])
     match = jnp.concatenate([match, jnp.max(match, axis=1, keepdims=True)], axis=1)
 
-    def renew(kept, go, slots=(), after=()):
-        resent = len(slots)
+    def renew(slots, go, after=()):
         return pl.pallas_call(
-            lambda *refs: renew_kernel(senders, owned, len(after), resent, *refs),
-            out_shape=(slot,) * resent + (held,),
-            in_specs=[SMEM] + [ANY] * (3 + senders + resent + len(after)),
-            out_specs=(ANY,) * (resent + 1),
+            lambda *refs: renew_kernel(senders, owned, len(after), *refs),
+            out_shape=(slot,) * senders,
+            in_specs=[SMEM] + [ANY] * (2 + 2 * senders + len(after)),
+            out_specs=(ANY,) * senders,
             scratch_shapes=[
                 pltpu.VMEM((stored, width, width), dtype),
                 pltpu.VMEM((stored, width, batches * shots), dtype),
@@ -386,28 +373,23 @@
                 DMA((stored, batches)),
                 DMA((senders,)),
                 DMA((stored,)),
-                DMA((stored,)),
             ],
-            input_output_aliases={3 + senders + at: at for at in range(resent + 1)},
+            input_output_aliases={3 + senders + at: at for at in range(senders)},
             compiler_params=PARAMS,
             name="renew",
-        )(jnp.concatenate([table, go[None], match.reshape(-1)]), source, blocks, *recv, *slots, kept, *after)
+        )(jnp.concatenate([table, go[None], match.reshape(-1)]), source, blocks, *recv, *slots, *after)
 
     traces = pl.pallas_call(
         lambda *refs: zero_kernel(owned, senders, stored, batches, *refs),
         out_shape=jax.ShapeDtypeStruct((batches, owned, width, shots), dtype),
         in_specs=[SMEM, ANY],
         out_specs=ANY,
-        scratch_shapes=[
-            pltpu.VMEM((width, shots), dtype),
-            pltpu.SMEM((senders,), jnp.int32),
-            DMA((batches, owned)),
-        ],
+        scratch_shapes=[pltpu.VMEM((width, shots), dtype), pltpu.SMEM((senders,), jnp.int32), DMA((batches, owned))],
         compiler_params=PARAMS,
         name="zeros",
     )(table, mine)
 
-    *slots, kept = renew(kept, jnp.int32(1), tuple(slots), (traces,))
+    slots = renew(slots, jnp.int32(1), (traces,))
     for wave, mask in enumerate(masks, 2):
         group = 4 if wave == 2 and senders <= 8 else 2
         for low in range(0, senders, group):
@@ -427,13 +409,16 @@
                 tuple(recv[low : low + group]),
             )
         go = jnp.where(depth >= wave, jnp.max(mask), 0)
-        *slots, kept = renew(kept, go, tuple(slots) if wave + 1 < layers else ())
-    arrived = lax.all_to_all(kept, "trace", split_axis=0, concat_axis=0, tiled=True)
+        slots = renew(slots, go)
+    arrived = [
+        lax.ppermute(slots[step], "trace", [(j, (j + step) % senders) for j in range(senders)]) if step else slots[0]
+        for step in range(senders)
+    ]
 
     traces = pl.pallas_call(
         lambda *refs: write_kernel(owned, senders, stored, batches, *refs),
         out_shape=jax.ShapeDtypeStruct((batches, owned, width, shots), dtype),
-        in_specs=[SMEM] + [ANY] * 2,
+        in_specs=[SMEM] + [ANY] * (senders + 1),
         out_specs=ANY,
         scratch_shapes=[
             pltpu.VMEM((senders,) + tile, dtype),
@@ -443,10 +428,10 @@
             DMA((senders,)),
             DMA((senders, batches)),
         ],
-        input_output_aliases={2: 0},
+        input_output_aliases={1 + senders: 0},
         compiler_params=PARAMS,
         name="write",
-    )(table, arrived, traces)
+    )(table, *arrived, traces)
     return traces.reshape(1, batches, local, shots)
 
 

time: 152 us -> 146 us (0.961)
  the two profiles are of different devices: /device:TPU:4 before, /device:TPU:13 now
where the time goes in v5:
time: 146 us; the launch traced here: 145 us
  waiting for transfers between devices  61.1 us (42%)
  starting transfers between devices  35.6 us (24%)
  Pallas kernels  21.1 us (14%)
  local copies, waits for them, and re-layouts  11.5 us (8%)
  between operations  11.5 us (8%)
  other arithmetic  3.68 us (3%)
    ppermute x7, waiting for transfers between devices, body(): lax.ppermute(slots[step], 'trace', [(j, (j + step) % senders) for j in ra...  41.9 us
    ppermute x8, starting transfers between devices, body(): recv[step] = lax.ppermute(slots[step], AXES, pairs(step))  17.1 us
    ppermute x8, waiting for transfers between devices, body(): recv[step] = lax.ppermute(slots[step], AXES, pairs(step))  11.3 us
    ppermute x7, starting transfers between devices, body(): lax.ppermute(slots[step], 'trace', [(j, (j + step) % senders) for j in ra...  10.5 us
    pallas_call x3, Pallas kernels, renew(): pl.pallas_call(lambda *refs: renew_kernel(senders, owned, len(after), *re...  8.77 us
    ppermute x1, waiting for transfers between devices, resend(): lax.ppermute(new[at], AXES, pairs(step, wave - 1))  7.88 us
    all_to_all x1, starting transfers between devices, body(): known = lax.all_to_all(mine, AXES, split_axis=0, concat_axis=0, tiled=True)  6.13 us
    pallas_call x1, Pallas kernels, body(): pl.pallas_call(lambda *refs: first_kernel(senders, owned, *refs), out_sha...  4.87 us
  transfers between devices with their start and end apart: 17, of which 11 were waited for; matrix products, arithmetic and copies ran while one was open for 8% of the time, Pallas kernels for 3%

profile of v5, /device:TPU:13, one launch (start us, length us, event | category | flops | bytes accessed | tf_op | source)
XLA Modules:
  0.0 144.7 jit_solution(15354207688494783062)
XLA Ops:
  0.0 0.8 copy.39.refs_0_
  0.8 0.6 copy-done
  1.4 0.6 reshape_squeeze.3
  2.0 4.9 %first.1 = (bf16[2,512,128]{2,1,0:T(8,128)(2,1)}, bf16[2,512,128]{2,1,0:T(8,128)(2,1)}, bf16[2,512,128]{2,1,0:T(8,128)(2,1)}, bf16[2,512,128]{2,1,0:T(8,128)(2,1...) custom-call(s32[1,8,6]{2,1,0:T(8,128)} %copy-done, ...), custom_call_target="tpu_custom_call" | custom-call | tf_op jit(solution)/shard_map/first/pallas_call | solution.py:312
  6.8 0.7 pad_add_fusion.1.refs_0_
  7.6 0.6 broadcast_in_dim.17
  8.2 6.1 %all-to-all-start = ((s32[32,1,55]{2,1,0:T(1,128)}), s32[32,1,55]{2,1,0:T(1,128)}, u32[]{:S(2)}, u32[]{:S(2)}) async-start(s32[32,1,55]{2,1,0:T(1,128)} %broadcast_in_dim.17), calls=%async_computation | async-start | bytes 32768 | tf_op jit(solution)/shard_map/all_to_all | solution.py:335
  14.3 3.1 %collective-permute-start.80 = (bf16[2,512,128]{2,1,0:T(8,128)(2,1)}, bf16[2,512,128]{2,1,0:T(8,128)(2,1)}, u32[]{:S(2)}, u32[]{:S(2)}) collective-permute-start(bf16[2,512,128]{2,1,0:T(8,128)(2,1)} %get-tuple-element.535.refs_11_), channel_id=1, source_target_pairs={{0,8},{1,9},{2,10},{3,11},{4,12},{5,13},{6,14},{7,15},{8,16},{9,17... | collective-permute-start | bytes 786440 | tf_op jit(solution)/shard_map/ppermute | solution.py:330
  17.4 2.5 %collective-permute-start.81 = (bf16[2,512,128]{2,1,0:T(8,128)(2,1)}, bf16[2,512,128]{2,1,0:T(8,128)(2,1)}, u32[]{:S(2)}, u32[]{:S(2)}) collective-permute-start(bf16[2,512,128]{2,1,0:T(8,128)(2,1)} %get-tuple-element.536.refs_12_), channel_id=1, source_target_pairs={{0,9},{1,10},{2,11},{3,12},{4,13},{5,14},{6,15},{7,8},{8,17},{9,18... | collective-permute-start | bytes 786440 | tf_op jit(solution)/shard_map/ppermute | solution.py:330
  19.9 1.9 %collective-permute-start.82 = (bf16[2,512,128]{2,1,0:T(8,128)(2,1)}, bf16[2,512,128]{2,1,0:T(8,128)(2,1)}, u32[]{:S(2)}, u32[]{:S(2)}) collective-permute-start(bf16[2,512,128]{2,1,0:T(8,128)(2,1)} %get-tuple-element.537.refs_13_), channel_id=1, source_target_pairs={{0,10},{1,11},{2,12},{3,13},{4,14},{5,15},{6,8},{7,9},{8,18},{9,19... | collective-permute-start | bytes 786440 | tf_op jit(solution)/shard_map/ppermute | solution.py:330
  21.9 1.9 %collective-permute-start.83 = (bf16[2,512,128]{2,1,0:T(8,128)(2,1)}, bf16[2,512,128]{2,1,0:T(8,128)(2,1)}, u32[]{:S(2)}, u32[]{:S(2)}) collective-permute-start(bf16[2,512,128]{2,1,0:T(8,128)(2,1)} %get-tuple-element.538.refs_14_), channel_id=1, source_target_pairs={{0,11},{1,12},{2,13},{3,14},{4,15},{5,8},{6,9},{7,10},{8,19},{9,20... | collective-permute-start | bytes 786440 | tf_op jit(solution)/shard_map/ppermute | solution.py:330
  23.8 1.9 %collective-permute-start.84 = (bf16[2,512,128]{2,1,0:T(8,128)(2,1)}, bf16[2,512,128]{2,1,0:T(8,128)(2,1)}, u32[]{:S(2)}, u32[]{:S(2)}) collective-permute-start(bf16[2,512,128]{2,1,0:T(8,128)(2,1)} %get-tuple-element.539.refs_15_), channel_id=1, source_target_pairs={{0,12},{1,13},{2,14},{3,15},{4,8},{5,9},{6,10},{7,11},{8,20},{9,21... | collective-permute-start | bytes 786440 | tf_op jit(solution)/shard_map/ppermute | solution.py:330
  25.7 0.6 sub.24
  26.3 0.6 broadcast_in_dim.41.refs_1_
  26.9 4.3 %zeros.1.refs_19_.refs_9_ = bf16[2,32,512,128]{3,2,1,0:T(8,128)(2,1)} custom-call(s32[55]{0:T(128)} %copy-done.1, s32[32,55]{1,0:T(8,128)} %broadcast_in_dim.41.refs_1_), custom_call_target="tpu_custom_call" | custom-call | tf_op jit(solution)/shard_map/zeros/pallas_call | solution.py:382
  31.3 0.0 all-to-all-done
  31.3 0.7 slice.90
  32.0 0.7 slice.92
  32.7 0.8 slice.91
  33.5 0.6 add_select_fusion
  34.1 0.1 eq.28
  34.2 0.1 compare_reduce_fusion.1
  34.3 0.2 fusion
  34.5 0.1 eq.62
  34.6 0.9 and_reduce_fusion
  35.6 0.1 add_reduce_fusion
  35.7 0.1 copy.41
  35.8 0.1 fusion.4
  36.0 0.7 convert_reduce_fusion.1
  36.7 6.0 %collective-permute-done.80.refs_3_ = bf16[2,512,128]{2,1,0:T(8,128)(2,1)} collective-permute-done((bf16[2,512,128]{2,1,0:T(8,128)(2,1)}, bf16[2,512,128]{2,1,0:T(8,128)(2,1)}, u32[]{:S(2)}, u32[]{:S(2)}) %collective-permute-start.80) | collective-permute-done | bytes 262176 | tf_op jit(solution)/shard_map/ppermute | solution.py:330
  42.7 1.9 %collective-permute-start.85 = (bf16[2,512,128]{2,1,0:T(8,128)(2,1)}, bf16[2,512,128]{2,1,0:T(8,128)(2,1)}, u32[]{:S(2)}, u32[]{:S(2)}) collective-permute-start(bf16[2,512,128]{2,1,0:T(8,128)(2,1)} %get-tuple-element.540.refs_16_), channel_id=1, source_target_pairs={{0,13},{1,14},{2,15},{3,8},{4,9},{5,10},{6,11},{7,12},{8,21},{9,22... | collective-permute-start | bytes 786440 | tf_op jit(solution)/shard_map/ppermute | solution.py:330
  44.6 3.4 %collective-permute-done.81.refs_4_ = bf16[2,512,128]{2,1,0:T(8,128)(2,1)} collective-permute-done((bf16[2,512,128]{2,1,0:T(8,128)(2,1)}, bf16[2,512,128]{2,1,0:T(8,128)(2,1)}, u32[]{:S(2)}, u32[]{:S(2)}) %collective-permute-start.81) | collective-permute-done | bytes 262176 | tf_op jit(solution)/shard_map/ppermute | solution.py:330
  47.9 1.9 %collective-permute-start.86 = (bf16[2,512,128]{2,1,0:T(8,128)(2,1)}, bf16[2,512,128]{2,1,0:T(8,128)(2,1)}, u32[]{:S(2)}, u32[]{:S(2)}) collective-permute-start(bf16[2,512,128]{2,1,0:T(8,128)(2,1)} %get-tuple-element.541.refs_17_), channel_id=1, source_target_pairs={{0,14},{1,15},{2,8},{3,9},{4,10},{5,11},{6,12},{7,13},{8,22},{9,23... | collective-permute-start | bytes 786440 | tf_op jit(solution)/shard_map/ppermute | solution.py:330
  49.9 0.0 collective-permute-done.82.refs_5_
  49.9 1.9 %collective-permute-start.87 = (bf16[2,512,128]{2,1,0:T(8,128)(2,1)}, bf16[2,512,128]{2,1,0:T(8,128)(2,1)}, u32[]{:S(2)}, u32[]{:S(2)}) collective-permute-start(bf16[2,512,128]{2,1,0:T(8,128)(2,1)} %get-tuple-element.542.refs_18_), channel_id=1, source_target_pairs={{0,15},{1,8},{2,9},{3,10},{4,11},{5,12},{6,13},{7,14},{8,23},{9,16... | collective-permute-start | bytes 786440 | tf_op jit(solution)/shard_map/ppermute | solution.py:330
  51.8 0.1 pad_add_fusion
  51.9 0.1 reshape.146
  53.1 1.3 concatenate.34.refs_0_
  54.4 1.2 concatenate.32.refs_0_
  55.7 1.3 concatenate.33.refs_0_
  57.0 0.7 fusion.9
  62.7 0.7 fusion.10
  68.4 0.0 collective-permute-done.83.refs_6_
  68.4 0.0 collective-permute-done.85.refs_8_
  68.4 1.8 %collective-permute-done.86.refs_9_ = bf16[2,512,128]{2,1,0:T(8,128)(2,1)} collective-permute-done((bf16[2,512,128]{2,1,0:T(8,128)(2,1)}, bf16[2,512,128]{2,1,0:T(8,128)(2,1)}, u32[]{:S(2)}, u32[]{:S(2)}) %collective-permute-start.86) | collective-permute-done | bytes 262176 | tf_op jit(solution)/shard_map/ppermute | solution.py:330
  70.2 0.1 collective-permute-done.87.refs_10_
  70.3 3.9 %renew.3 = (bf16[2,512,128]{2,1,0:T(8,128)(2,1)}, bf16[2,512,128]{2,1,0:T(8,128)(2,1)}, bf16[2,512,128]{2,1,0:T(8,128)(2,1)}, bf16[2,512,128]{2,1,0:T(8,128)(2,1...) custom-call(s32[119]{0:T(128)} %concatenate.33.refs_0_, ...), custom_call_target="tpu_custom_call", output_to_operand_aliasing={{0}: (11, {}), {1}: (12, {}), {2}: (13, {}), {3}: (14, {}),... | custom-call | tf_op jit(solution)/shard_map/renew/pallas_call | solution.py:361
  74.3 9.8 %conditional.7 = ((bf16[2,512,128]{2,1,0:T(8,128)(2,1)}, bf16[2,512,128]{2,1,0:T(8,128)(2,1)}, bf16[2,512,128]{2,1,0:T(8,128)(2,1)}, bf16[2,512,128]{2,1,0:T(8,128)(2,1)})) conditional(s32[]{:T(128)} %bitcast.11, (bf16[2,512,128]{2,1,0:T(8,128)(2,1)}, bf16[2,512,128]{2,1,0:T(8,128)(2,1)}, ...), branch_computations={%region_26.27_spmd, %region_27.28_spmd, %region_28.29_spmd, %regio... | conditional | bytes 4194504 | solution.py:405
  74.3 1.9 %collective-permute-start.44 = (bf16[2,512,128]{2,1,0:T(8,128)(2,1)}, bf16[2,512,128]{2,1,0:T(8,128)(2,1)}, u32[]{:S(2)}, u32[]{:S(2)}) collective-permute-start(bf16[2,512,128]{2,1,0:T(8,128)(2,1)} %get-tuple-element.416), channel_id=1, source_target_pairs={{8,23},{9,16},{10,17},{11,18},{12,19},{13,20},{14,21},{15,22},{16,... | collective-permute-start | bytes 786440 | tf_op jit(solution)/shard_map/cond/branch_8_fun/ppermute | solution.py:400
  76.2 7.9 %collective-permute-done.44 = bf16[2,512,128]{2,1,0:T(8,128)(2,1)} collective-permute-done((bf16[2,512,128]{2,1,0:T(8,128)(2,1)}, bf16[2,512,128]{2,1,0:T(8,128)(2,1)}, u32[]{:S(2)}, u32[]{:S(2)}) %collective-permute-start.44) | collective-permute-done | bytes 262176 | tf_op jit(solution)/shard_map/cond/branch_8_fun/ppermute | solution.py:400
  84.1 3.9 %renew.4 = (bf16[2,512,128]{2,1,0:T(8,128)(2,1)}, bf16[2,512,128]{2,1,0:T(8,128)(2,1)}, bf16[2,512,128]{2,1,0:T(8,128)(2,1)}, bf16[2,512,128]{2,1,0:T(8,128)(2,1...) custom-call(s32[119]{0:T(128)} %concatenate.34.refs_0_, ...), custom_call_target="tpu_custom_call", output_to_operand_aliasing={{0}: (11, {}), {1}: (12, {}), {2}: (13, {}), {3}: (14, {}),... | custom-call | tf_op jit(solution)/shard_map/renew/pallas_call | solution.py:361
  88.1 1.0 renew.5
  89.1 2.5 %collective-permute-start.88 = (bf16[2,512,128]{2,1,0:T(8,128)(2,1)}, bf16[2,512,128]{2,1,0:T(8,128)(2,1)}, u32[]{:S(2)}, u32[]{:S(2)}) collective-permute-start(bf16[2,512,128]{2,1,0:T(8,128)(2,1)} %get-tuple-element.576), channel_id=1, source_target_pairs={{0,1},{1,2},{2,3},{3,4},{4,5},{5,6},{6,7},{7,0},{8,9},{9,10},{10,1... | collective-permute-start | bytes 786440 | tf_op jit(solution)/shard_map/ppermute | solution.py:414
  91.6 3.9 %collective-permute-start.89 = (bf16[2,512,128]{2,1,0:T(8,128)(2,1)}, bf16[2,512,128]{2,1,0:T(8,128)(2,1)}, u32[]{:S(2)}, u32[]{:S(2)}) collective-permute-start(bf16[2,512,128]{2,1,0:T(8,128)(2,1)} %get-tuple-element.577), channel_id=1, source_target_pairs={{0,2},{1,3},{2,4},{3,5},{4,6},{5,7},{6,0},{7,1},{8,10},{9,11},{10,... | collective-permute-start | bytes 786440 | tf_op jit(solution)/shard_map/ppermute | solution.py:414
  95.4 0.2 collective-permute-start.90
  95.6 1.7 %collective-permute-start.92 = (bf16[2,512,128]{2,1,0:T(8,128)(2,1)}, bf16[2,512,128]{2,1,0:T(8,128)(2,1)}, u32[]{:S(2)}, u32[]{:S(2)}) collective-permute-start(bf16[2,512,128]{2,1,0:T(8,128)(2,1)} %get-tuple-element.580), channel_id=1, source_target_pairs={{0,5},{1,6},{2,7},{3,0},{4,1},{5,2},{6,3},{7,4},{8,13},{9,14},{10,... | collective-permute-start | bytes 786440 | tf_op jit(solution)/shard_map/ppermute | solution.py:414
  97.3 0.1 collective-permute-done.88.refs_2_
  97.4 2.3 %collective-permute-start.93 = (bf16[2,512,128]{2,1,0:T(8,128)(2,1)}, bf16[2,512,128]{2,1,0:T(8,128)(2,1)}, u32[]{:S(2)}, u32[]{:S(2)}) collective-permute-start(bf16[2,512,128]{2,1,0:T(8,128)(2,1)} %get-tuple-element.581), channel_id=1, source_target_pairs={{0,6},{1,7},{2,0},{3,1},{4,2},{5,3},{6,4},{7,5},{8,14},{9,15},{10,... | collective-permute-start | bytes 786440 | tf_op jit(solution)/shard_map/ppermute | solution.py:414
  99.6 25.8 %collective-permute-done.89.refs_3_ = bf16[2,512,128]{2,1,0:T(8,128)(2,1)} collective-permute-done((bf16[2,512,128]{2,1,0:T(8,128)(2,1)}, bf16[2,512,128]{2,1,0:T(8,128)(2,1)}, u32[]{:S(2)}, u32[]{:S(2)}) %collective-permute-start.89) | collective-permute-done | bytes 262176 | tf_op jit(solution)/shard_map/ppermute | solution.py:414
  125.5 5.6 %collective-permute-done.90.refs_4_ = bf16[2,512,128]{2,1,0:T(8,128)(2,1)} collective-permute-done((bf16[2,512,128]{2,1,0:T(8,128)(2,1)}, bf16[2,512,128]{2,1,0:T(8,128)(2,1)}, u32[]{:S(2)}, u32[]{:S(2)}) %collective-permute-start.90) | collective-permute-done | bytes 262176 | tf_op jit(solution)/shard_map/ppermute | solution.py:414
  131.1 5.6 %collective-permute-done.91.refs_5_ = bf16[2,512,128]{2,1,0:T(8,128)(2,1)} collective-permute-done((bf16[2,512,128]{2,1,0:T(8,128)(2,1)}, bf16[2,512,128]{2,1,0:T(8,128)(2,1)}, u32[]{:S(2)}, u32[]{:S(2)}) %collective-permute-start.91) | collective-permute-done | bytes 262176 | tf_op jit(solution)/shard_map/ppermute | solution.py:414
  136.7 4.7 %collective-permute-done.93.refs_7_ = bf16[2,512,128]{2,1,0:T(8,128)(2,1)} collective-permute-done((bf16[2,512,128]{2,1,0:T(8,128)(2,1)}, bf16[2,512,128]{2,1,0:T(8,128)(2,1)}, u32[]{:S(2)}, u32[]{:S(2)}) %collective-permute-start.93) | collective-permute-done | bytes 262176 | tf_op jit(solution)/shard_map/ppermute | solution.py:414
  141.4 0.1 collective-permute-done.94.refs_8_
  141.5 3.2 %write.1 = bf16[2,32,512,128]{3,2,1,0:T(8,128)(2,1)} custom-call(s32[55]{0:T(128)} %copy-done.1, bf16[2,512,128]{2,1,0:T(8,128)(2,1)} %get-tuple-element.575.refs_1_, bf16[2,512,128]{2,1,0:T(8,128)(2,1)} %collective-permute-done.88.refs_2_, bf16[2,512,128]{2,1,0:T(8,128)(2,1)} %collective-permute-done.89.refs_3_, ...), custom_call_target="tpu_custom_call", output_to_operand_aliasing={{}: (9, {})} | custom-call | tf_op jit(solution)/shard_map/write/pallas_call | solution.py:418
  (21 shorter events, 0.2 us)
Async XLA Ops:
  0.8 0.6 copy-start
  7.6 18.8 %copy-start.1 = (s32[55]{0:T(128)}, s32[55]{0:T(128)S(1)}, u32[]{:S(2)}) copy-start(s32[55]{0:T(128)S(1)} %pad_add_fusion.1.refs_0_) | copy-start | bytes 664
  8.2 23.1 %all-to-all-start = ((s32[32,1,55]{2,1,0:T(1,128)}), s32[32,1,55]{2,1,0:T(1,128)}, u32[]{:S(2)}, u32[]{:S(2)}) async-start(s32[32,1,55]{2,1,0:T(1,128)} %broadcast_in_dim.17), calls=%async_computation | async-start | bytes 32768 | tf_op jit(solution)/shard_map/all_to_all | solution.py:335
  14.3 28.3 %collective-permute-start.80 = (bf16[2,512,128]{2,1,0:T(8,128)(2,1)}, bf16[2,512,128]{2,1,0:T(8,128)(2,1)}, u32[]{:S(2)}, u32[]{:S(2)}) collective-permute-start(bf16[2,512,128]{2,1,0:T(8,128)(2,1)} %get-tuple-element.535.refs_11_), channel_id=1, source_target_pairs={{0,8},{1,9},{2,10},{3,11},{4,12},{5,13},{6,14},{7,15},{8,16},{9,17... | collective-permute-start | bytes 786440 | tf_op jit(solution)/shard_map/ppermute | solution.py:330
  17.4 30.5 %collective-permute-start.81 = (bf16[2,512,128]{2,1,0:T(8,128)(2,1)}, bf16[2,512,128]{2,1,0:T(8,128)(2,1)}, u32[]{:S(2)}, u32[]{:S(2)}) collective-permute-start(bf16[2,512,128]{2,1,0:T(8,128)(2,1)} %get-tuple-element.536.refs_12_), channel_id=1, source_target_pairs={{0,9},{1,10},{2,11},{3,12},{4,13},{5,14},{6,15},{7,8},{8,17},{9,18... | collective-permute-start | bytes 786440 | tf_op jit(solution)/shard_map/ppermute | solution.py:330
  19.9 29.9 %collective-permute-start.82 = (bf16[2,512,128]{2,1,0:T(8,128)(2,1)}, bf16[2,512,128]{2,1,0:T(8,128)(2,1)}, u32[]{:S(2)}, u32[]{:S(2)}) collective-permute-start(bf16[2,512,128]{2,1,0:T(8,128)(2,1)} %get-tuple-element.537.refs_13_), channel_id=1, source_target_pairs={{0,10},{1,11},{2,12},{3,13},{4,14},{5,15},{6,8},{7,9},{8,18},{9,19... | collective-permute-start | bytes 786440 | tf_op jit(solution)/shard_map/ppermute | solution.py:330
  21.9 46.5 %collective-permute-start.83 = (bf16[2,512,128]{2,1,0:T(8,128)(2,1)}, bf16[2,512,128]{2,1,0:T(8,128)(2,1)}, u32[]{:S(2)}, u32[]{:S(2)}) collective-permute-start(bf16[2,512,128]{2,1,0:T(8,128)(2,1)} %get-tuple-element.538.refs_14_), channel_id=1, source_target_pairs={{0,11},{1,12},{2,13},{3,14},{4,15},{5,8},{6,9},{7,10},{8,19},{9,20... | collective-permute-start | bytes 786440 | tf_op jit(solution)/shard_map/ppermute | solution.py:330
  23.8 44.6 %collective-permute-start.84 = (bf16[2,512,128]{2,1,0:T(8,128)(2,1)}, bf16[2,512,128]{2,1,0:T(8,128)(2,1)}, u32[]{:S(2)}, u32[]{:S(2)}) collective-permute-start(bf16[2,512,128]{2,1,0:T(8,128)(2,1)} %get-tuple-element.539.refs_15_), channel_id=1, source_target_pairs={{0,12},{1,13},{2,14},{3,15},{4,8},{5,9},{6,10},{7,11},{8,20},{9,21... | collective-permute-start | bytes 786440 | tf_op jit(solution)/shard_map/ppermute | solution.py:330
  42.7 25.8 %collective-permute-start.85 = (bf16[2,512,128]{2,1,0:T(8,128)(2,1)}, bf16[2,512,128]{2,1,0:T(8,128)(2,1)}, u32[]{:S(2)}, u32[]{:S(2)}) collective-permute-start(bf16[2,512,128]{2,1,0:T(8,128)(2,1)} %get-tuple-element.540.refs_16_), channel_id=1, source_target_pairs={{0,13},{1,14},{2,15},{3,8},{4,9},{5,10},{6,11},{7,12},{8,21},{9,22... | collective-permute-start | bytes 786440 | tf_op jit(solution)/shard_map/ppermute | solution.py:330
  47.9 22.3 %collective-permute-start.86 = (bf16[2,512,128]{2,1,0:T(8,128)(2,1)}, bf16[2,512,128]{2,1,0:T(8,128)(2,1)}, u32[]{:S(2)}, u32[]{:S(2)}) collective-permute-start(bf16[2,512,128]{2,1,0:T(8,128)(2,1)} %get-tuple-element.541.refs_17_), channel_id=1, source_target_pairs={{0,14},{1,15},{2,8},{3,9},{4,10},{5,11},{6,12},{7,13},{8,22},{9,23... | collective-permute-start | bytes 786440 | tf_op jit(solution)/shard_map/ppermute | solution.py:330
  49.9 20.5 %collective-permute-start.87 = (bf16[2,512,128]{2,1,0:T(8,128)(2,1)}, bf16[2,512,128]{2,1,0:T(8,128)(2,1)}, u32[]{:S(2)}, u32[]{:S(2)}) collective-permute-start(bf16[2,512,128]{2,1,0:T(8,128)(2,1)} %get-tuple-element.542.refs_18_), channel_id=1, source_target_pairs={{0,15},{1,8},{2,9},{3,10},{4,11},{5,12},{6,13},{7,14},{8,23},{9,16... | collective-permute-start | bytes 786440 | tf_op jit(solution)/shard_map/ppermute | solution.py:330
  74.3 9.8 %collective-permute-start.44 = (bf16[2,512,128]{2,1,0:T(8,128)(2,1)}, bf16[2,512,128]{2,1,0:T(8,128)(2,1)}, u32[]{:S(2)}, u32[]{:S(2)}) collective-permute-start(bf16[2,512,128]{2,1,0:T(8,128)(2,1)} %get-tuple-element.416), channel_id=1, source_target_pairs={{8,23},{9,16},{10,17},{11,18},{12,19},{13,20},{14,21},{15,22},{16,... | collective-permute-start | bytes 786440 | tf_op jit(solution)/shard_map/cond/branch_8_fun/ppermute | solution.py:400
  89.1 8.3 %collective-permute-start.88 = (bf16[2,512,128]{2,1,0:T(8,128)(2,1)}, bf16[2,512,128]{2,1,0:T(8,128)(2,1)}, u32[]{:S(2)}, u32[]{:S(2)}) collective-permute-start(bf16[2,512,128]{2,1,0:T(8,128)(2,1)} %get-tuple-element.576), channel_id=1, source_target_pairs={{0,1},{1,2},{2,3},{3,4},{4,5},{5,6},{6,7},{7,0},{8,9},{9,10},{10,1... | collective-permute-start | bytes 786440 | tf_op jit(solution)/shard_map/ppermute | solution.py:414
  91.6 33.9 %collective-permute-start.89 = (bf16[2,512,128]{2,1,0:T(8,128)(2,1)}, bf16[2,512,128]{2,1,0:T(8,128)(2,1)}, u32[]{:S(2)}, u32[]{:S(2)}) collective-permute-start(bf16[2,512,128]{2,1,0:T(8,128)(2,1)} %get-tuple-element.577), channel_id=1, source_target_pairs={{0,2},{1,3},{2,4},{3,5},{4,6},{5,7},{6,0},{7,1},{8,10},{9,11},{10,... | collective-permute-start | bytes 786440 | tf_op jit(solution)/shard_map/ppermute | solution.py:414
  95.4 35.6 %collective-permute-start.90 = (bf16[2,512,128]{2,1,0:T(8,128)(2,1)}, bf16[2,512,128]{2,1,0:T(8,128)(2,1)}, u32[]{:S(2)}, u32[]{:S(2)}) collective-permute-start(bf16[2,512,128]{2,1,0:T(8,128)(2,1)} %get-tuple-element.578), channel_id=1, source_target_pairs={{0,3},{1,4},{2,5},{3,6},{4,7},{5,0},{6,1},{7,2},{8,11},{9,12},{10,... | collective-permute-start | bytes 786440 | tf_op jit(solution)/shard_map/ppermute | solution.py:414
  95.6 41.1 %collective-permute-start.91 = (bf16[2,512,128]{2,1,0:T(8,128)(2,1)}, bf16[2,512,128]{2,1,0:T(8,128)(2,1)}, u32[]{:S(2)}, u32[]{:S(2)}) collective-permute-start(bf16[2,512,128]{2,1,0:T(8,128)(2,1)} %get-tuple-element.579), channel_id=1, source_target_pairs={{0,4},{1,5},{2,6},{3,7},{4,0},{5,1},{6,2},{7,3},{8,12},{9,13},{10,... | collective-permute-start | bytes 786440 | tf_op jit(solution)/shard_map/ppermute | solution.py:414
  95.6 41.1 %collective-permute-start.92 = (bf16[2,512,128]{2,1,0:T(8,128)(2,1)}, bf16[2,512,128]{2,1,0:T(8,128)(2,1)}, u32[]{:S(2)}, u32[]{:S(2)}) collective-permute-start(bf16[2,512,128]{2,1,0:T(8,128)(2,1)} %get-tuple-element.580), channel_id=1, source_target_pairs={{0,5},{1,6},{2,7},{3,0},{4,1},{5,2},{6,3},{7,4},{8,13},{9,14},{10,... | collective-permute-start | bytes 786440 | tf_op jit(solution)/shard_map/ppermute | solution.py:414
  97.4 44.0 %collective-permute-start.93 = (bf16[2,512,128]{2,1,0:T(8,128)(2,1)}, bf16[2,512,128]{2,1,0:T(8,128)(2,1)}, u32[]{:S(2)}, u32[]{:S(2)}) collective-permute-start(bf16[2,512,128]{2,1,0:T(8,128)(2,1)} %get-tuple-element.581), channel_id=1, source_target_pairs={{0,6},{1,7},{2,0},{3,1},{4,2},{5,3},{6,4},{7,5},{8,14},{9,15},{10,... | collective-permute-start | bytes 786440 | tf_op jit(solution)/shard_map/ppermute | solution.py:414
  125.5 16.0 %collective-permute-start.94 = (bf16[2,512,128]{2,1,0:T(8,128)(2,1)}, bf16[2,512,128]{2,1,0:T(8,128)(2,1)}, u32[]{:S(2)}, u32[]{:S(2)}) collective-permute-start(bf16[2,512,128]{2,1,0:T(8,128)(2,1)} %get-tuple-element.582), channel_id=1, source_target_pairs={{0,7},{1,0},{2,1},{3,2},{4,3},{5,4},{6,5},{7,6},{8,15},{9,8},{10,9... | collective-permute-start | bytes 786440 | tf_op jit(solution)/shard_map/ppermute | solution.py:414

commit v6 on v5

--- a/solution.py
+++ b/solution.py
@@ -17,6 +17,10 @@
     if owned & (owned - 1) == 0:
         return lax.shift_right_logical(row, jnp.int32(owned.bit_length() - 1))
     return lax.div(row, jnp.int32(owned))
+
+
+def far_first(senders):
+    return sorted(range(senders), key=lambda step: abs(2 * step - senders))
 
 
 def read_table(table, senders, stored):
@@ -326,7 +330,7 @@
         name="first",
     )(row_block, col_block, source, blocks)
     recv = [None] * senders
-    for step in sorted(range(senders), key=lambda step: abs(2 * step - senders)):
+    for step in far_first(senders):
         recv[step] = lax.ppermute(slots[step], AXES, pairs(step))
 
     total = layers * senders
@@ -410,10 +414,9 @@
             )
         go = jnp.where(depth >= wave, jnp.max(mask), 0)
         slots = renew(slots, go)
-    arrived = [
-        lax.ppermute(slots[step], "trace", [(j, (j + step) % senders) for j in range(senders)]) if step else slots[0]
-        for step in range(senders)
-    ]
+    arrived = list(slots)
+    for step in far_first(senders)[:-1]:
+        arrived[step] = lax.ppermute(slots[step], "trace", [(j, (j + step) % senders) for j in range(senders)])
 
     traces = pl.pallas_call(
         lambda *refs: write_kernel(owned, senders, stored, batches, *refs),

time: 146 us -> 146 us (level)
  no operation moved by 1% of the time
where the time goes in v6:
time: 146 us; the launch traced here: 145 us
  waiting for transfers between devices  61.1 us (42%)
  starting transfers between devices  35.6 us (24%)
  Pallas kernels  21.1 us (14%)
  local copies, waits for them, and re-layouts  11.5 us (8%)
  between operations  11.5 us (8%)
  other arithmetic  3.68 us (3%)
    ppermute x7, waiting for transfers between devices, body(): lax.ppermute(slots[step], 'trace', [(j, (j + step) % senders) for j in ra...  41.9 us
    ppermute x8, starting transfers between devices, body(): recv[step] = lax.ppermute(slots[step], AXES, pairs(step))  17.1 us
    ppermute x8, waiting for transfers between devices, body(): recv[step] = lax.ppermute(slots[step], AXES, pairs(step))  11.3 us
    ppermute x7, starting transfers between devices, body(): lax.ppermute(slots[step], 'trace', [(j, (j + step) % senders) for j in ra...  10.5 us
    pallas_call x3, Pallas kernels, renew(): pl.pallas_call(lambda *refs: renew_kernel(senders, owned, len(after), *re...  8.77 us
    ppermute x1, waiting for transfers between devices, resend(): lax.ppermute(new[at], AXES, pairs(step, wave - 1))  7.88 us
    all_to_all x1, starting transfers between devices, body(): known = lax.all_to_all(mine, AXES, split_axis=0, concat_axis=0, tiled=True)  6.13 us
    pallas_call x1, Pallas kernels, body(): pl.pallas_call(lambda *refs: first_kernel(senders, owned, *refs), out_sha...  4.87 us
  transfers between devices with their start and end apart: 17, of which 11 were waited for; matrix products, arithmetic and copies ran while one was open for 8% of the time, Pallas kernels for 3%

profile of v6, /device:TPU:13, one launch (start us, length us, event | category | flops | bytes accessed | tf_op | source)
XLA Modules:
  0.0 144.7 jit_solution(15354207688494783062)
XLA Ops:
  0.0 0.8 copy.39.refs_0_
  0.8 0.6 copy-done
  1.4 0.6 reshape_squeeze.3
  2.0 4.9 %first.1 = (bf16[2,512,128]{2,1,0:T(8,128)(2,1)}, bf16[2,512,128]{2,1,0:T(8,128)(2,1)}, bf16[2,512,128]{2,1,0:T(8,128)(2,1)}, bf16[2,512,128]{2,1,0:T(8,128)(2,1...) custom-call(s32[1,8,6]{2,1,0:T(8,128)} %copy-done, ...), custom_call_target="tpu_custom_call" | custom-call | tf_op jit(solution)/shard_map/first/pallas_call | solution.py:316
  6.8 0.7 pad_add_fusion.1.refs_0_
  7.6 0.6 broadcast_in_dim.17
  8.2 6.1 %all-to-all-start = ((s32[32,1,55]{2,1,0:T(1,128)}), s32[32,1,55]{2,1,0:T(1,128)}, u32[]{:S(2)}, u32[]{:S(2)}) async-start(s32[32,1,55]{2,1,0:T(1,128)} %broadcast_in_dim.17), calls=%async_computation | async-start | bytes 32768 | tf_op jit(solution)/shard_map/all_to_all | solution.py:339
  14.3 3.1 %collective-permute-start.80 = (bf16[2,512,128]{2,1,0:T(8,128)(2,1)}, bf16[2,512,128]{2,1,0:T(8,128)(2,1)}, u32[]{:S(2)}, u32[]{:S(2)}) collective-permute-start(bf16[2,512,128]{2,1,0:T(8,128)(2,1)} %get-tuple-element.535.refs_11_), channel_id=1, source_target_pairs={{0,8},{1,9},{2,10},{3,11},{4,12},{5,13},{6,14},{7,15},{8,16},{9,17... | collective-permute-start | bytes 786440 | tf_op jit(solution)/shard_map/ppermute | solution.py:334
  17.4 2.5 %collective-permute-start.81 = (bf16[2,512,128]{2,1,0:T(8,128)(2,1)}, bf16[2,512,128]{2,1,0:T(8,128)(2,1)}, u32[]{:S(2)}, u32[]{:S(2)}) collective-permute-start(bf16[2,512,128]{2,1,0:T(8,128)(2,1)} %get-tuple-element.536.refs_12_), channel_id=1, source_target_pairs={{0,9},{1,10},{2,11},{3,12},{4,13},{5,14},{6,15},{7,8},{8,17},{9,18... | collective-permute-start | bytes 786440 | tf_op jit(solution)/shard_map/ppermute | solution.py:334
  19.9 1.9 %collective-permute-start.82 = (bf16[2,512,128]{2,1,0:T(8,128)(2,1)}, bf16[2,512,128]{2,1,0:T(8,128)(2,1)}, u32[]{:S(2)}, u32[]{:S(2)}) collective-permute-start(bf16[2,512,128]{2,1,0:T(8,128)(2,1)} %get-tuple-element.537.refs_13_), channel_id=1, source_target_pairs={{0,10},{1,11},{2,12},{3,13},{4,14},{5,15},{6,8},{7,9},{8,18},{9,19... | collective-permute-start | bytes 786440 | tf_op jit(solution)/shard_map/ppermute | solution.py:334
  21.9 1.9 %collective-permute-start.83 = (bf16[2,512,128]{2,1,0:T(8,128)(2,1)}, bf16[2,512,128]{2,1,0:T(8,128)(2,1)}, u32[]{:S(2)}, u32[]{:S(2)}) collective-permute-start(bf16[2,512,128]{2,1,0:T(8,128)(2,1)} %get-tuple-element.538.refs_14_), channel_id=1, source_target_pairs={{0,11},{1,12},{2,13},{3,14},{4,15},{5,8},{6,9},{7,10},{8,19},{9,20... | collective-permute-start | bytes 786440 | tf_op jit(solution)/shard_map/ppermute | solution.py:334
  23.8 1.9 %collective-permute-start.84 = (bf16[2,512,128]{2,1,0:T(8,128)(2,1)}, bf16[2,512,128]{2,1,0:T(8,128)(2,1)}, u32[]{:S(2)}, u32[]{:S(2)}) collective-permute-start(bf16[2,512,128]{2,1,0:T(8,128)(2,1)} %get-tuple-element.539.refs_15_), channel_id=1, source_target_pairs={{0,12},{1,13},{2,14},{3,15},{4,8},{5,9},{6,10},{7,11},{8,20},{9,21... | collective-permute-start | bytes 786440 | tf_op jit(solution)/shard_map/ppermute | solution.py:334
  25.7 0.6 sub.24
  26.3 0.6 broadcast_in_dim.41.refs_1_
  26.9 4.3 %zeros.1.refs_19_.refs_9_ = bf16[2,32,512,128]{3,2,1,0:T(8,128)(2,1)} custom-call(s32[55]{0:T(128)} %copy-done.1, s32[32,55]{1,0:T(8,128)} %broadcast_in_dim.41.refs_1_), custom_call_target="tpu_custom_call" | custom-call | tf_op jit(solution)/shard_map/zeros/pallas_call | solution.py:386
  31.3 0.0 all-to-all-done
  31.3 0.7 slice.90
  32.0 0.7 slice.92
  32.7 0.8 slice.91
  33.5 0.6 add_select_fusion
  34.1 0.1 eq.28
  34.2 0.1 compare_reduce_fusion.1
  34.3 0.2 fusion
  34.5 0.1 eq.62
  34.6 0.9 and_reduce_fusion
  35.6 0.1 add_reduce_fusion
  35.7 0.1 copy.41
  35.8 0.1 fusion.4
  36.0 0.7 convert_reduce_fusion.1
  36.7 6.0 %collective-permute-done.80.refs_3_ = bf16[2,512,128]{2,1,0:T(8,128)(2,1)} collective-permute-done((bf16[2,512,128]{2,1,0:T(8,128)(2,1)}, bf16[2,512,128]{2,1,0:T(8,128)(2,1)}, u32[]{:S(2)}, u32[]{:S(2)}) %collective-permute-start.80) | collective-permute-done | bytes 262176 | tf_op jit(solution)/shard_map/ppermute | solution.py:334
  42.7 1.9 %collective-permute-start.85 = (bf16[2,512,128]{2,1,0:T(8,128)(2,1)}, bf16[2,512,128]{2,1,0:T(8,128)(2,1)}, u32[]{:S(2)}, u32[]{:S(2)}) collective-permute-start(bf16[2,512,128]{2,1,0:T(8,128)(2,1)} %get-tuple-element.540.refs_16_), channel_id=1, source_target_pairs={{0,13},{1,14},{2,15},{3,8},{4,9},{5,10},{6,11},{7,12},{8,21},{9,22... | collective-permute-start | bytes 786440 | tf_op jit(solution)/shard_map/ppermute | solution.py:334
  44.6 3.4 %collective-permute-done.81.refs_4_ = bf16[2,512,128]{2,1,0:T(8,128)(2,1)} collective-permute-done((bf16[2,512,128]{2,1,0:T(8,128)(2,1)}, bf16[2,512,128]{2,1,0:T(8,128)(2,1)}, u32[]{:S(2)}, u32[]{:S(2)}) %collective-permute-start.81) | collective-permute-done | bytes 262176 | tf_op jit(solution)/shard_map/ppermute | solution.py:334
  47.9 1.9 %collective-permute-start.86 = (bf16[2,512,128]{2,1,0:T(8,128)(2,1)}, bf16[2,512,128]{2,1,0:T(8,128)(2,1)}, u32[]{:S(2)}, u32[]{:S(2)}) collective-permute-start(bf16[2,512,128]{2,1,0:T(8,128)(2,1)} %get-tuple-element.541.refs_17_), channel_id=1, source_target_pairs={{0,14},{1,15},{2,8},{3,9},{4,10},{5,11},{6,12},{7,13},{8,22},{9,23... | collective-permute-start | bytes 786440 | tf_op jit(solution)/shard_map/ppermute | solution.py:334
  49.9 0.0 collective-permute-done.82.refs_5_
  49.9 1.9 %collective-permute-start.87 = (bf16[2,512,128]{2,1,0:T(8,128)(2,1)}, bf16[2,512,128]{2,1,0:T(8,128)(2,1)}, u32[]{:S(2)}, u32[]{:S(2)}) collective-permute-start(bf16[2,512,128]{2,1,0:T(8,128)(2,1)} %get-tuple-element.542.refs_18_), channel_id=1, source_target_pairs={{0,15},{1,8},{2,9},{3,10},{4,11},{5,12},{6,13},{7,14},{8,23},{9,16... | collective-permute-start | bytes 786440 | tf_op jit(solution)/shard_map/ppermute | solution.py:334
  51.8 0.1 pad_add_fusion
  51.9 0.1 reshape.146
  53.1 1.3 concatenate.34.refs_0_
  54.4 1.2 concatenate.32.refs_0_
  55.7 1.3 concatenate.33.refs_0_
  57.0 0.7 fusion.9
  62.7 0.7 fusion.10
  68.4 0.0 collective-permute-done.83.refs_6_
  68.4 0.0 collective-permute-done.85.refs_8_
  68.4 1.8 %collective-permute-done.86.refs_9_ = bf16[2,512,128]{2,1,0:T(8,128)(2,1)} collective-permute-done((bf16[2,512,128]{2,1,0:T(8,128)(2,1)}, bf16[2,512,128]{2,1,0:T(8,128)(2,1)}, u32[]{:S(2)}, u32[]{:S(2)}) %collective-permute-start.86) | collective-permute-done | bytes 262176 | tf_op jit(solution)/shard_map/ppermute | solution.py:334
  70.2 0.1 collective-permute-done.87.refs_10_
  70.3 3.9 %renew.3 = (bf16[2,512,128]{2,1,0:T(8,128)(2,1)}, bf16[2,512,128]{2,1,0:T(8,128)(2,1)}, bf16[2,512,128]{2,1,0:T(8,128)(2,1)}, bf16[2,512,128]{2,1,0:T(8,128)(2,1...) custom-call(s32[119]{0:T(128)} %concatenate.33.refs_0_, ...), custom_call_target="tpu_custom_call", output_to_operand_aliasing={{0}: (11, {}), {1}: (12, {}), {2}: (13, {}), {3}: (14, {}),... | custom-call | tf_op jit(solution)/shard_map/renew/pallas_call | solution.py:365
  74.3 9.8 %conditional.7 = ((bf16[2,512,128]{2,1,0:T(8,128)(2,1)}, bf16[2,512,128]{2,1,0:T(8,128)(2,1)}, bf16[2,512,128]{2,1,0:T(8,128)(2,1)}, bf16[2,512,128]{2,1,0:T(8,128)(2,1)})) conditional(s32[]{:T(128)} %bitcast.11, (bf16[2,512,128]{2,1,0:T(8,128)(2,1)}, bf16[2,512,128]{2,1,0:T(8,128)(2,1)}, ...), branch_computations={%region_26.27_spmd, %region_27.28_spmd, %region_28.29_spmd, %regio... | conditional | bytes 4194504 | solution.py:409
  74.3 1.9 %collective-permute-start.44 = (bf16[2,512,128]{2,1,0:T(8,128)(2,1)}, bf16[2,512,128]{2,1,0:T(8,128)(2,1)}, u32[]{:S(2)}, u32[]{:S(2)}) collective-permute-start(bf16[2,512,128]{2,1,0:T(8,128)(2,1)} %get-tuple-element.416), channel_id=1, source_target_pairs={{8,23},{9,16},{10,17},{11,18},{12,19},{13,20},{14,21},{15,22},{16,... | collective-permute-start | bytes 786440 | tf_op jit(solution)/shard_map/cond/branch_8_fun/ppermute | solution.py:404
  76.2 7.9 %collective-permute-done.44 = bf16[2,512,128]{2,1,0:T(8,128)(2,1)} collective-permute-done((bf16[2,512,128]{2,1,0:T(8,128)(2,1)}, bf16[2,512,128]{2,1,0:T(8,128)(2,1)}, u32[]{:S(2)}, u32[]{:S(2)}) %collective-permute-start.44) | collective-permute-done | bytes 262176 | tf_op jit(solution)/shard_map/cond/branch_8_fun/ppermute | solution.py:404
  84.1 3.9 %renew.4 = (bf16[2,512,128]{2,1,0:T(8,128)(2,1)}, bf16[2,512,128]{2,1,0:T(8,128)(2,1)}, bf16[2,512,128]{2,1,0:T(8,128)(2,1)}, bf16[2,512,128]{2,1,0:T(8,128)(2,1...) custom-call(s32[119]{0:T(128)} %concatenate.34.refs_0_, ...), custom_call_target="tpu_custom_call", output_to_operand_aliasing={{0}: (11, {}), {1}: (12, {}), {2}: (13, {}), {3}: (14, {}),... | custom-call | tf_op jit(solution)/shard_map/renew/pallas_call | solution.py:365
  88.1 1.0 renew.5
  89.1 2.5 %collective-permute-start.88 = (bf16[2,512,128]{2,1,0:T(8,128)(2,1)}, bf16[2,512,128]{2,1,0:T(8,128)(2,1)}, u32[]{:S(2)}, u32[]{:S(2)}) collective-permute-start(bf16[2,512,128]{2,1,0:T(8,128)(2,1)} %get-tuple-element.576), channel_id=1, source_target_pairs={{0,1},{1,2},{2,3},{3,4},{4,5},{5,6},{6,7},{7,0},{8,9},{9,10},{10,1... | collective-permute-start | bytes 786440 | tf_op jit(solution)/shard_map/ppermute | solution.py:419
  91.6 3.9 %collective-permute-start.89 = (bf16[2,512,128]{2,1,0:T(8,128)(2,1)}, bf16[2,512,128]{2,1,0:T(8,128)(2,1)}, u32[]{:S(2)}, u32[]{:S(2)}) collective-permute-start(bf16[2,512,128]{2,1,0:T(8,128)(2,1)} %get-tuple-element.577), channel_id=1, source_target_pairs={{0,2},{1,3},{2,4},{3,5},{4,6},{5,7},{6,0},{7,1},{8,10},{9,11},{10,... | collective-permute-start | bytes 786440 | tf_op jit(solution)/shard_map/ppermute | solution.py:419
  95.4 0.2 collective-permute-start.90
  95.6 1.7 %collective-permute-start.92 = (bf16[2,512,128]{2,1,0:T(8,128)(2,1)}, bf16[2,512,128]{2,1,0:T(8,128)(2,1)}, u32[]{:S(2)}, u32[]{:S(2)}) collective-permute-start(bf16[2,512,128]{2,1,0:T(8,128)(2,1)} %get-tuple-element.580), channel_id=1, source_target_pairs={{0,5},{1,6},{2,7},{3,0},{4,1},{5,2},{6,3},{7,4},{8,13},{9,14},{10,... | collective-permute-start | bytes 786440 | tf_op jit(solution)/shard_map/ppermute | solution.py:419
  97.3 0.1 collective-permute-done.88.refs_2_
  97.4 2.3 %collective-permute-start.93 = (bf16[2,512,128]{2,1,0:T(8,128)(2,1)}, bf16[2,512,128]{2,1,0:T(8,128)(2,1)}, u32[]{:S(2)}, u32[]{:S(2)}) collective-permute-start(bf16[2,512,128]{2,1,0:T(8,128)(2,1)} %get-tuple-element.581), channel_id=1, source_target_pairs={{0,6},{1,7},{2,0},{3,1},{4,2},{5,3},{6,4},{7,5},{8,14},{9,15},{10,... | collective-permute-start | bytes 786440 | tf_op jit(solution)/shard_map/ppermute | solution.py:419
  99.6 25.8 %collective-permute-done.89.refs_3_ = bf16[2,512,128]{2,1,0:T(8,128)(2,1)} collective-permute-done((bf16[2,512,128]{2,1,0:T(8,128)(2,1)}, bf16[2,512,128]{2,1,0:T(8,128)(2,1)}, u32[]{:S(2)}, u32[]{:S(2)}) %collective-permute-start.89) | collective-permute-done | bytes 262176 | tf_op jit(solution)/shard_map/ppermute | solution.py:419
  125.5 5.6 %collective-permute-done.90.refs_4_ = bf16[2,512,128]{2,1,0:T(8,128)(2,1)} collective-permute-done((bf16[2,512,128]{2,1,0:T(8,128)(2,1)}, bf16[2,512,128]{2,1,0:T(8,128)(2,1)}, u32[]{:S(2)}, u32[]{:S(2)}) %collective-permute-start.90) | collective-permute-done | bytes 262176 | tf_op jit(solution)/shard_map/ppermute | solution.py:419
  131.1 5.6 %collective-permute-done.91.refs_5_ = bf16[2,512,128]{2,1,0:T(8,128)(2,1)} collective-permute-done((bf16[2,512,128]{2,1,0:T(8,128)(2,1)}, bf16[2,512,128]{2,1,0:T(8,128)(2,1)}, u32[]{:S(2)}, u32[]{:S(2)}) %collective-permute-start.91) | collective-permute-done | bytes 262176 | tf_op jit(solution)/shard_map/ppermute | solution.py:419
  136.7 4.7 %collective-permute-done.93.refs_7_ = bf16[2,512,128]{2,1,0:T(8,128)(2,1)} collective-permute-done((bf16[2,512,128]{2,1,0:T(8,128)(2,1)}, bf16[2,512,128]{2,1,0:T(8,128)(2,1)}, u32[]{:S(2)}, u32[]{:S(2)}) %collective-permute-start.93) | collective-permute-done | bytes 262176 | tf_op jit(solution)/shard_map/ppermute | solution.py:419
  141.4 0.1 collective-permute-done.94.refs_8_
  141.5 3.2 %write.1 = bf16[2,32,512,128]{3,2,1,0:T(8,128)(2,1)} custom-call(s32[55]{0:T(128)} %copy-done.1, bf16[2,512,128]{2,1,0:T(8,128)(2,1)} %get-tuple-element.575.refs_1_, bf16[2,512,128]{2,1,0:T(8,128)(2,1)} %collective-permute-done.88.refs_2_, bf16[2,512,128]{2,1,0:T(8,128)(2,1)} %collective-permute-done.89.refs_3_, ...), custom_call_target="tpu_custom_call", output_to_operand_aliasing={{}: (9, {})} | custom-call | tf_op jit(solution)/shard_map/write/pallas_call | solution.py:421
  (21 shorter events, 0.2 us)
Async XLA Ops:
  0.8 0.6 copy-start
  7.6 18.8 %copy-start.1 = (s32[55]{0:T(128)}, s32[55]{0:T(128)S(1)}, u32[]{:S(2)}) copy-start(s32[55]{0:T(128)S(1)} %pad_add_fusion.1.refs_0_) | copy-start | bytes 664
  8.2 23.1 %all-to-all-start = ((s32[32,1,55]{2,1,0:T(1,128)}), s32[32,1,55]{2,1,0:T(1,128)}, u32[]{:S(2)}, u32[]{:S(2)}) async-start(s32[32,1,55]{2,1,0:T(1,128)} %broadcast_in_dim.17), calls=%async_computation | async-start | bytes 32768 | tf_op jit(solution)/shard_map/all_to_all | solution.py:339
  14.3 28.3 %collective-permute-start.80 = (bf16[2,512,128]{2,1,0:T(8,128)(2,1)}, bf16[2,512,128]{2,1,0:T(8,128)(2,1)}, u32[]{:S(2)}, u32[]{:S(2)}) collective-permute-start(bf16[2,512,128]{2,1,0:T(8,128)(2,1)} %get-tuple-element.535.refs_11_), channel_id=1, source_target_pairs={{0,8},{1,9},{2,10},{3,11},{4,12},{5,13},{6,14},{7,15},{8,16},{9,17... | collective-permute-start | bytes 786440 | tf_op jit(solution)/shard_map/ppermute | solution.py:334
  17.4 30.5 %collective-permute-start.81 = (bf16[2,512,128]{2,1,0:T(8,128)(2,1)}, bf16[2,512,128]{2,1,0:T(8,128)(2,1)}, u32[]{:S(2)}, u32[]{:S(2)}) collective-permute-start(bf16[2,512,128]{2,1,0:T(8,128)(2,1)} %get-tuple-element.536.refs_12_), channel_id=1, source_target_pairs={{0,9},{1,10},{2,11},{3,12},{4,13},{5,14},{6,15},{7,8},{8,17},{9,18... | collective-permute-start | bytes 786440 | tf_op jit(solution)/shard_map/ppermute | solution.py:334
  19.9 29.9 %collective-permute-start.82 = (bf16[2,512,128]{2,1,0:T(8,128)(2,1)}, bf16[2,512,128]{2,1,0:T(8,128)(2,1)}, u32[]{:S(2)}, u32[]{:S(2)}) collective-permute-start(bf16[2,512,128]{2,1,0:T(8,128)(2,1)} %get-tuple-element.537.refs_13_), channel_id=1, source_target_pairs={{0,10},{1,11},{2,12},{3,13},{4,14},{5,15},{6,8},{7,9},{8,18},{9,19... | collective-permute-start | bytes 786440 | tf_op jit(solution)/shard_map/ppermute | solution.py:334
  21.9 46.5 %collective-permute-start.83 = (bf16[2,512,128]{2,1,0:T(8,128)(2,1)}, bf16[2,512,128]{2,1,0:T(8,128)(2,1)}, u32[]{:S(2)}, u32[]{:S(2)}) collective-permute-start(bf16[2,512,128]{2,1,0:T(8,128)(2,1)} %get-tuple-element.538.refs_14_), channel_id=1, source_target_pairs={{0,11},{1,12},{2,13},{3,14},{4,15},{5,8},{6,9},{7,10},{8,19},{9,20... | collective-permute-start | bytes 786440 | tf_op jit(solution)/shard_map/ppermute | solution.py:334
  23.8 44.6 %collective-permute-start.84 = (bf16[2,512,128]{2,1,0:T(8,128)(2,1)}, bf16[2,512,128]{2,1,0:T(8,128)(2,1)}, u32[]{:S(2)}, u32[]{:S(2)}) collective-permute-start(bf16[2,512,128]{2,1,0:T(8,128)(2,1)} %get-tuple-element.539.refs_15_), channel_id=1, source_target_pairs={{0,12},{1,13},{2,14},{3,15},{4,8},{5,9},{6,10},{7,11},{8,20},{9,21... | collective-permute-start | bytes 786440 | tf_op jit(solution)/shard_map/ppermute | solution.py:334
  42.7 25.8 %collective-permute-start.85 = (bf16[2,512,128]{2,1,0:T(8,128)(2,1)}, bf16[2,512,128]{2,1,0:T(8,128)(2,1)}, u32[]{:S(2)}, u32[]{:S(2)}) collective-permute-start(bf16[2,512,128]{2,1,0:T(8,128)(2,1)} %get-tuple-element.540.refs_16_), channel_id=1, source_target_pairs={{0,13},{1,14},{2,15},{3,8},{4,9},{5,10},{6,11},{7,12},{8,21},{9,22... | collective-permute-start | bytes 786440 | tf_op jit(solution)/shard_map/ppermute | solution.py:334
  47.9 22.3 %collective-permute-start.86 = (bf16[2,512,128]{2,1,0:T(8,128)(2,1)}, bf16[2,512,128]{2,1,0:T(8,128)(2,1)}, u32[]{:S(2)}, u32[]{:S(2)}) collective-permute-start(bf16[2,512,128]{2,1,0:T(8,128)(2,1)} %get-tuple-element.541.refs_17_), channel_id=1, source_target_pairs={{0,14},{1,15},{2,8},{3,9},{4,10},{5,11},{6,12},{7,13},{8,22},{9,23... | collective-permute-start | bytes 786440 | tf_op jit(solution)/shard_map/ppermute | solution.py:334
  49.9 20.5 %collective-permute-start.87 = (bf16[2,512,128]{2,1,0:T(8,128)(2,1)}, bf16[2,512,128]{2,1,0:T(8,128)(2,1)}, u32[]{:S(2)}, u32[]{:S(2)}) collective-permute-start(bf16[2,512,128]{2,1,0:T(8,128)(2,1)} %get-tuple-element.542.refs_18_), channel_id=1, source_target_pairs={{0,15},{1,8},{2,9},{3,10},{4,11},{5,12},{6,13},{7,14},{8,23},{9,16... | collective-permute-start | bytes 786440 | tf_op jit(solution)/shard_map/ppermute | solution.py:334
  74.3 9.8 %collective-permute-start.44 = (bf16[2,512,128]{2,1,0:T(8,128)(2,1)}, bf16[2,512,128]{2,1,0:T(8,128)(2,1)}, u32[]{:S(2)}, u32[]{:S(2)}) collective-permute-start(bf16[2,512,128]{2,1,0:T(8,128)(2,1)} %get-tuple-element.416), channel_id=1, source_target_pairs={{8,23},{9,16},{10,17},{11,18},{12,19},{13,20},{14,21},{15,22},{16,... | collective-permute-start | bytes 786440 | tf_op jit(solution)/shard_map/cond/branch_8_fun/ppermute | solution.py:404
  89.1 8.3 %collective-permute-start.88 = (bf16[2,512,128]{2,1,0:T(8,128)(2,1)}, bf16[2,512,128]{2,1,0:T(8,128)(2,1)}, u32[]{:S(2)}, u32[]{:S(2)}) collective-permute-start(bf16[2,512,128]{2,1,0:T(8,128)(2,1)} %get-tuple-element.576), channel_id=1, source_target_pairs={{0,1},{1,2},{2,3},{3,4},{4,5},{5,6},{6,7},{7,0},{8,9},{9,10},{10,1... | collective-permute-start | bytes 786440 | tf_op jit(solution)/shard_map/ppermute | solution.py:419
  91.6 33.9 %collective-permute-start.89 = (bf16[2,512,128]{2,1,0:T(8,128)(2,1)}, bf16[2,512,128]{2,1,0:T(8,128)(2,1)}, u32[]{:S(2)}, u32[]{:S(2)}) collective-permute-start(bf16[2,512,128]{2,1,0:T(8,128)(2,1)} %get-tuple-element.577), channel_id=1, source_target_pairs={{0,2},{1,3},{2,4},{3,5},{4,6},{5,7},{6,0},{7,1},{8,10},{9,11},{10,... | collective-permute-start | bytes 786440 | tf_op jit(solution)/shard_map/ppermute | solution.py:419
  95.4 35.6 %collective-permute-start.90 = (bf16[2,512,128]{2,1,0:T(8,128)(2,1)}, bf16[2,512,128]{2,1,0:T(8,128)(2,1)}, u32[]{:S(2)}, u32[]{:S(2)}) collective-permute-start(bf16[2,512,128]{2,1,0:T(8,128)(2,1)} %get-tuple-element.578), channel_id=1, source_target_pairs={{0,3},{1,4},{2,5},{3,6},{4,7},{5,0},{6,1},{7,2},{8,11},{9,12},{10,... | collective-permute-start | bytes 786440 | tf_op jit(solution)/shard_map/ppermute | solution.py:419
  95.6 41.1 %collective-permute-start.91 = (bf16[2,512,128]{2,1,0:T(8,128)(2,1)}, bf16[2,512,128]{2,1,0:T(8,128)(2,1)}, u32[]{:S(2)}, u32[]{:S(2)}) collective-permute-start(bf16[2,512,128]{2,1,0:T(8,128)(2,1)} %get-tuple-element.579), channel_id=1, source_target_pairs={{0,4},{1,5},{2,6},{3,7},{4,0},{5,1},{6,2},{7,3},{8,12},{9,13},{10,... | collective-permute-start | bytes 786440 | tf_op jit(solution)/shard_map/ppermute | solution.py:419
  95.6 41.1 %collective-permute-start.92 = (bf16[2,512,128]{2,1,0:T(8,128)(2,1)}, bf16[2,512,128]{2,1,0:T(8,128)(2,1)}, u32[]{:S(2)}, u32[]{:S(2)}) collective-permute-start(bf16[2,512,128]{2,1,0:T(8,128)(2,1)} %get-tuple-element.580), channel_id=1, source_target_pairs={{0,5},{1,6},{2,7},{3,0},{4,1},{5,2},{6,3},{7,4},{8,13},{9,14},{10,... | collective-permute-start | bytes 786440 | tf_op jit(solution)/shard_map/ppermute | solution.py:419
  97.4 44.0 %collective-permute-start.93 = (bf16[2,512,128]{2,1,0:T(8,128)(2,1)}, bf16[2,512,128]{2,1,0:T(8,128)(2,1)}, u32[]{:S(2)}, u32[]{:S(2)}) collective-permute-start(bf16[2,512,128]{2,1,0:T(8,128)(2,1)} %get-tuple-element.581), channel_id=1, source_target_pairs={{0,6},{1,7},{2,0},{3,1},{4,2},{5,3},{6,4},{7,5},{8,14},{9,15},{10,... | collective-permute-start | bytes 786440 | tf_op jit(solution)/shard_map/ppermute | solution.py:419
  125.5 16.0 %collective-permute-start.94 = (bf16[2,512,128]{2,1,0:T(8,128)(2,1)}, bf16[2,512,128]{2,1,0:T(8,128)(2,1)}, u32[]{:S(2)}, u32[]{:S(2)}) collective-permute-start(bf16[2,512,128]{2,1,0:T(8,128)(2,1)} %get-tuple-element.582), channel_id=1, source_target_pairs={{0,7},{1,0},{2,1},{3,2},{4,3},{5,4},{6,5},{7,6},{8,15},{9,8},{10,9... | collective-permute-start | bytes 786440 | tf_op jit(solution)/shard_map/ppermute | solution.py:419

commit v7 on v6

--- a/solution.py
+++ b/solution.py
@@ -252,15 +252,10 @@
 
     @pl.loop(0, senders)
     def _(sender):
-        @pl.when(here[sender] >= 0)
-        def _():
-            take(0, sender).wait()
-
-    @pl.loop(0, senders)
-    def _(sender):
         @pl.when((here[sender] >= 0) & (count(sender, 0, sender) == 0))
         def _():
             more = count(sender, sender + 1, senders)
+            take(0, sender).wait()
 
             @pl.when(more == 0)
             def _():
@@ -275,6 +270,7 @@
                 def _(other):
                     @pl.when(here[other] == here[sender])
                     def _():
+                        take(0, other).wait()
                         total[...] += arrived[other].astype(jnp.float32)
 
                 made[sender] = total[...].astype(made.dtype)

time: 146 us -> 145 us (level)
  no operation moved by 1% of the time
where the time goes in v7:
time: 145 us
  waiting for transfers between devices  61.1 us (42%)
  starting transfers between devices  35.6 us (25%)
  Pallas kernels  21.1 us (15%)
  local copies, waits for them, and re-layouts  11.5 us (8%)
  between operations  11.5 us (8%)
  other arithmetic  3.68 us (3%)
    ppermute x7, waiting for transfers between devices, body(): lax.ppermute(slots[step], 'trace', [(j, (j + step) % senders) for j in ra...  41.9 us
    ppermute x8, starting transfers between devices, body(): recv[step] = lax.ppermute(slots[step], AXES, pairs(step))  17.1 us
    ppermute x8, waiting for transfers between devices, body(): recv[step] = lax.ppermute(slots[step], AXES, pairs(step))  11.3 us
    ppermute x7, starting transfers between devices, body(): lax.ppermute(slots[step], 'trace', [(j, (j + step) % senders) for j in ra...  10.5 us
    pallas_call x3, Pallas kernels, renew(): pl.pallas_call(lambda *refs: renew_kernel(senders, owned, len(after), *re...  8.77 us
    ppermute x1, waiting for transfers between devices, resend(): lax.ppermute(new[at], AXES, pairs(step, wave - 1))  7.88 us
    all_to_all x1, starting transfers between devices, body(): known = lax.all_to_all(mine, AXES, split_axis=0, concat_axis=0, tiled=True)  6.13 us
    pallas_call x1, Pallas kernels, body(): pl.pallas_call(lambda *refs: first_kernel(senders, owned, *refs), out_sha...  4.87 us
  transfers between devices with their start and end apart: 17, of which 11 were waited for; matrix products, arithmetic and copies ran while one was open for 8% of the time, Pallas kernels for 3%

profile of v7, /device:TPU:13, one launch (start us, length us, event | category | flops | bytes accessed | tf_op | source)
XLA Modules:
  0.0 144.6 jit_solution(15315236285118949475)
XLA Ops:
  0.0 0.8 copy.39.refs_0_
  0.8 0.6 copy-done
  1.4 0.6 reshape_squeeze.3
  2.0 4.9 %first.1 = (bf16[2,512,128]{2,1,0:T(8,128)(2,1)}, bf16[2,512,128]{2,1,0:T(8,128)(2,1)}, bf16[2,512,128]{2,1,0:T(8,128)(2,1)}, bf16[2,512,128]{2,1,0:T(8,128)(2,1...) custom-call(s32[1,8,6]{2,1,0:T(8,128)} %copy-done, ...), custom_call_target="tpu_custom_call" | custom-call | tf_op jit(solution)/shard_map/first/pallas_call | solution.py:312
  6.8 0.7 pad_add_fusion.1.refs_0_
  7.6 0.6 broadcast_in_dim.17
  8.2 6.1 %all-to-all-start = ((s32[32,1,55]{2,1,0:T(1,128)}), s32[32,1,55]{2,1,0:T(1,128)}, u32[]{:S(2)}, u32[]{:S(2)}) async-start(s32[32,1,55]{2,1,0:T(1,128)} %broadcast_in_dim.17), calls=%async_computation | async-start | bytes 32768 | tf_op jit(solution)/shard_map/all_to_all | solution.py:335
  14.3 3.1 %collective-permute-start.80 = (bf16[2,512,128]{2,1,0:T(8,128)(2,1)}, bf16[2,512,128]{2,1,0:T(8,128)(2,1)}, u32[]{:S(2)}, u32[]{:S(2)}) collective-permute-start(bf16[2,512,128]{2,1,0:T(8,128)(2,1)} %get-tuple-element.535.refs_11_), channel_id=1, source_target_pairs={{0,8},{1,9},{2,10},{3,11},{4,12},{5,13},{6,14},{7,15},{8,16},{9,17... | collective-permute-start | bytes 786440 | tf_op jit(solution)/shard_map/ppermute | solution.py:330
  17.4 2.5 %collective-permute-start.81 = (bf16[2,512,128]{2,1,0:T(8,128)(2,1)}, bf16[2,512,128]{2,1,0:T(8,128)(2,1)}, u32[]{:S(2)}, u32[]{:S(2)}) collective-permute-start(bf16[2,512,128]{2,1,0:T(8,128)(2,1)} %get-tuple-element.536.refs_12_), channel_id=1, source_target_pairs={{0,9},{1,10},{2,11},{3,12},{4,13},{5,14},{6,15},{7,8},{8,17},{9,18... | collective-permute-start | bytes 786440 | tf_op jit(solution)/shard_map/ppermute | solution.py:330
  19.9 1.9 %collective-permute-start.82 = (bf16[2,512,128]{2,1,0:T(8,128)(2,1)}, bf16[2,512,128]{2,1,0:T(8,128)(2,1)}, u32[]{:S(2)}, u32[]{:S(2)}) collective-permute-start(bf16[2,512,128]{2,1,0:T(8,128)(2,1)} %get-tuple-element.537.refs_13_), channel_id=1, source_target_pairs={{0,10},{1,11},{2,12},{3,13},{4,14},{5,15},{6,8},{7,9},{8,18},{9,19... | collective-permute-start | bytes 786440 | tf_op jit(solution)/shard_map/ppermute | solution.py:330
  21.9 1.9 %collective-permute-start.83 = (bf16[2,512,128]{2,1,0:T(8,128)(2,1)}, bf16[2,512,128]{2,1,0:T(8,128)(2,1)}, u32[]{:S(2)}, u32[]{:S(2)}) collective-permute-start(bf16[2,512,128]{2,1,0:T(8,128)(2,1)} %get-tuple-element.538.refs_14_), channel_id=1, source_target_pairs={{0,11},{1,12},{2,13},{3,14},{4,15},{5,8},{6,9},{7,10},{8,19},{9,20... | collective-permute-start | bytes 786440 | tf_op jit(solution)/shard_map/ppermute | solution.py:330
  23.8 1.9 %collective-permute-start.84 = (bf16[2,512,128]{2,1,0:T(8,128)(2,1)}, bf16[2,512,128]{2,1,0:T(8,128)(2,1)}, u32[]{:S(2)}, u32[]{:S(2)}) collective-permute-start(bf16[2,512,128]{2,1,0:T(8,128)(2,1)} %get-tuple-element.539.refs_15_), channel_id=1, source_target_pairs={{0,12},{1,13},{2,14},{3,15},{4,8},{5,9},{6,10},{7,11},{8,20},{9,21... | collective-permute-start | bytes 786440 | tf_op jit(solution)/shard_map/ppermute | solution.py:330
  25.7 0.6 sub.24
  26.3 0.6 broadcast_in_dim.41.refs_1_
  26.9 4.3 %zeros.1.refs_19_.refs_9_ = bf16[2,32,512,128]{3,2,1,0:T(8,128)(2,1)} custom-call(s32[55]{0:T(128)} %copy-done.1, s32[32,55]{1,0:T(8,128)} %broadcast_in_dim.41.refs_1_), custom_call_target="tpu_custom_call" | custom-call | tf_op jit(solution)/shard_map/zeros/pallas_call | solution.py:382
  31.3 0.0 all-to-all-done
  31.3 0.7 slice.90
  32.0 0.7 slice.92
  32.7 0.8 slice.91
  33.5 0.6 add_select_fusion
  34.1 0.1 eq.28
  34.2 0.1 compare_reduce_fusion.1
  34.3 0.2 fusion
  34.5 0.1 eq.62
  34.6 0.9 and_reduce_fusion
  35.6 0.1 add_reduce_fusion
  35.7 0.1 copy.41
  35.8 0.1 fusion.4
  36.0 0.7 convert_reduce_fusion.1
  36.7 6.0 %collective-permute-done.80.refs_3_ = bf16[2,512,128]{2,1,0:T(8,128)(2,1)} collective-permute-done((bf16[2,512,128]{2,1,0:T(8,128)(2,1)}, bf16[2,512,128]{2,1,0:T(8,128)(2,1)}, u32[]{:S(2)}, u32[]{:S(2)}) %collective-permute-start.80) | collective-permute-done | bytes 262176 | tf_op jit(solution)/shard_map/ppermute | solution.py:330
  42.7 1.9 %collective-permute-start.85 = (bf16[2,512,128]{2,1,0:T(8,128)(2,1)}, bf16[2,512,128]{2,1,0:T(8,128)(2,1)}, u32[]{:S(2)}, u32[]{:S(2)}) collective-permute-start(bf16[2,512,128]{2,1,0:T(8,128)(2,1)} %get-tuple-element.540.refs_16_), channel_id=1, source_target_pairs={{0,13},{1,14},{2,15},{3,8},{4,9},{5,10},{6,11},{7,12},{8,21},{9,22... | collective-permute-start | bytes 786440 | tf_op jit(solution)/shard_map/ppermute | solution.py:330
  44.6 3.4 %collective-permute-done.81.refs_4_ = bf16[2,512,128]{2,1,0:T(8,128)(2,1)} collective-permute-done((bf16[2,512,128]{2,1,0:T(8,128)(2,1)}, bf16[2,512,128]{2,1,0:T(8,128)(2,1)}, u32[]{:S(2)}, u32[]{:S(2)}) %collective-permute-start.81) | collective-permute-done | bytes 262176 | tf_op jit(solution)/shard_map/ppermute | solution.py:330
  47.9 1.9 %collective-permute-start.86 = (bf16[2,512,128]{2,1,0:T(8,128)(2,1)}, bf16[2,512,128]{2,1,0:T(8,128)(2,1)}, u32[]{:S(2)}, u32[]{:S(2)}) collective-permute-start(bf16[2,512,128]{2,1,0:T(8,128)(2,1)} %get-tuple-element.541.refs_17_), channel_id=1, source_target_pairs={{0,14},{1,15},{2,8},{3,9},{4,10},{5,11},{6,12},{7,13},{8,22},{9,23... | collective-permute-start | bytes 786440 | tf_op jit(solution)/shard_map/ppermute | solution.py:330
  49.9 0.0 collective-permute-done.82.refs_5_
  49.9 1.9 %collective-permute-start.87 = (bf16[2,512,128]{2,1,0:T(8,128)(2,1)}, bf16[2,512,128]{2,1,0:T(8,128)(2,1)}, u32[]{:S(2)}, u32[]{:S(2)}) collective-permute-start(bf16[2,512,128]{2,1,0:T(8,128)(2,1)} %get-tuple-element.542.refs_18_), channel_id=1, source_target_pairs={{0,15},{1,8},{2,9},{3,10},{4,11},{5,12},{6,13},{7,14},{8,23},{9,16... | collective-permute-start | bytes 786440 | tf_op jit(solution)/shard_map/ppermute | solution.py:330
  51.8 0.1 pad_add_fusion
  51.9 0.1 reshape.146
  53.1 1.3 concatenate.34.refs_0_
  54.4 1.2 concatenate.32.refs_0_
  55.7 1.3 concatenate.33.refs_0_
  57.0 0.7 fusion.9
  62.7 0.7 fusion.10
  68.4 0.0 collective-permute-done.83.refs_6_
  68.4 0.0 collective-permute-done.85.refs_8_
  68.4 1.8 %collective-permute-done.86.refs_9_ = bf16[2,512,128]{2,1,0:T(8,128)(2,1)} collective-permute-done((bf16[2,512,128]{2,1,0:T(8,128)(2,1)}, bf16[2,512,128]{2,1,0:T(8,128)(2,1)}, u32[]{:S(2)}, u32[]{:S(2)}) %collective-permute-start.86) | collective-permute-done | bytes 262176 | tf_op jit(solution)/shard_map/ppermute | solution.py:330
  70.2 0.1 collective-permute-done.87.refs_10_
  70.3 3.9 %renew.3 = (bf16[2,512,128]{2,1,0:T(8,128)(2,1)}, bf16[2,512,128]{2,1,0:T(8,128)(2,1)}, bf16[2,512,128]{2,1,0:T(8,128)(2,1)}, bf16[2,512,128]{2,1,0:T(8,128)(2,1...) custom-call(s32[119]{0:T(128)} %concatenate.33.refs_0_, ...), custom_call_target="tpu_custom_call", output_to_operand_aliasing={{0}: (11, {}), {1}: (12, {}), {2}: (13, {}), {3}: (14, {}),... | custom-call | tf_op jit(solution)/shard_map/renew/pallas_call | solution.py:361
  74.3 9.8 %conditional.7 = ((bf16[2,512,128]{2,1,0:T(8,128)(2,1)}, bf16[2,512,128]{2,1,0:T(8,128)(2,1)}, bf16[2,512,128]{2,1,0:T(8,128)(2,1)}, bf16[2,512,128]{2,1,0:T(8,128)(2,1)})) conditional(s32[]{:T(128)} %bitcast.11, (bf16[2,512,128]{2,1,0:T(8,128)(2,1)}, bf16[2,512,128]{2,1,0:T(8,128)(2,1)}, ...), branch_computations={%region_26.27_spmd, %region_27.28_spmd, %region_28.29_spmd, %regio... | conditional | bytes 4194504 | solution.py:405
  74.3 1.9 %collective-permute-start.44 = (bf16[2,512,128]{2,1,0:T(8,128)(2,1)}, bf16[2,512,128]{2,1,0:T(8,128)(2,1)}, u32[]{:S(2)}, u32[]{:S(2)}) collective-permute-start(bf16[2,512,128]{2,1,0:T(8,128)(2,1)} %get-tuple-element.416), channel_id=1, source_target_pairs={{8,23},{9,16},{10,17},{11,18},{12,19},{13,20},{14,21},{15,22},{16,... | collective-permute-start | bytes 786440 | tf_op jit(solution)/shard_map/cond/branch_8_fun/ppermute | solution.py:400
  76.2 7.9 %collective-permute-done.44 = bf16[2,512,128]{2,1,0:T(8,128)(2,1)} collective-permute-done((bf16[2,512,128]{2,1,0:T(8,128)(2,1)}, bf16[2,512,128]{2,1,0:T(8,128)(2,1)}, u32[]{:S(2)}, u32[]{:S(2)}) %collective-permute-start.44) | collective-permute-done | bytes 262176 | tf_op jit(solution)/shard_map/cond/branch_8_fun/ppermute | solution.py:400
  84.1 3.9 %renew.4 = (bf16[2,512,128]{2,1,0:T(8,128)(2,1)}, bf16[2,512,128]{2,1,0:T(8,128)(2,1)}, bf16[2,512,128]{2,1,0:T(8,128)(2,1)}, bf16[2,512,128]{2,1,0:T(8,128)(2,1...) custom-call(s32[119]{0:T(128)} %concatenate.34.refs_0_, ...), custom_call_target="tpu_custom_call", output_to_operand_aliasing={{0}: (11, {}), {1}: (12, {}), {2}: (13, {}), {3}: (14, {}),... | custom-call | tf_op jit(solution)/shard_map/renew/pallas_call | solution.py:361
  88.1 1.0 renew.5
  89.1 2.5 %collective-permute-start.88 = (bf16[2,512,128]{2,1,0:T(8,128)(2,1)}, bf16[2,512,128]{2,1,0:T(8,128)(2,1)}, u32[]{:S(2)}, u32[]{:S(2)}) collective-permute-start(bf16[2,512,128]{2,1,0:T(8,128)(2,1)} %get-tuple-element.576), channel_id=1, source_target_pairs={{0,1},{1,2},{2,3},{3,4},{4,5},{5,6},{6,7},{7,0},{8,9},{9,10},{10,1... | collective-permute-start | bytes 786440 | tf_op jit(solution)/shard_map/ppermute | solution.py:415
  91.6 3.9 %collective-permute-start.89 = (bf16[2,512,128]{2,1,0:T(8,128)(2,1)}, bf16[2,512,128]{2,1,0:T(8,128)(2,1)}, u32[]{:S(2)}, u32[]{:S(2)}) collective-permute-start(bf16[2,512,128]{2,1,0:T(8,128)(2,1)} %get-tuple-element.577), channel_id=1, source_target_pairs={{0,2},{1,3},{2,4},{3,5},{4,6},{5,7},{6,0},{7,1},{8,10},{9,11},{10,... | collective-permute-start | bytes 786440 | tf_op jit(solution)/shard_map/ppermute | solution.py:415
  95.4 0.2 collective-permute-start.90
  95.6 1.7 %collective-permute-start.92 = (bf16[2,512,128]{2,1,0:T(8,128)(2,1)}, bf16[2,512,128]{2,1,0:T(8,128)(2,1)}, u32[]{:S(2)}, u32[]{:S(2)}) collective-permute-start(bf16[2,512,128]{2,1,0:T(8,128)(2,1)} %get-tuple-element.580), channel_id=1, source_target_pairs={{0,5},{1,6},{2,7},{3,0},{4,1},{5,2},{6,3},{7,4},{8,13},{9,14},{10,... | collective-permute-start | bytes 786440 | tf_op jit(solution)/shard_map/ppermute | solution.py:415
  97.3 0.1 collective-permute-done.88.refs_2_
  97.4 2.3 %collective-permute-start.93 = (bf16[2,512,128]{2,1,0:T(8,128)(2,1)}, bf16[2,512,128]{2,1,0:T(8,128)(2,1)}, u32[]{:S(2)}, u32[]{:S(2)}) collective-permute-start(bf16[2,512,128]{2,1,0:T(8,128)(2,1)} %get-tuple-element.581), channel_id=1, source_target_pairs={{0,6},{1,7},{2,0},{3,1},{4,2},{5,3},{6,4},{7,5},{8,14},{9,15},{10,... | collective-permute-start | bytes 786440 | tf_op jit(solution)/shard_map/ppermute | solution.py:415
  99.6 25.8 %collective-permute-done.89.refs_3_ = bf16[2,512,128]{2,1,0:T(8,128)(2,1)} collective-permute-done((bf16[2,512,128]{2,1,0:T(8,128)(2,1)}, bf16[2,512,128]{2,1,0:T(8,128)(2,1)}, u32[]{:S(2)}, u32[]{:S(2)}) %collective-permute-start.89) | collective-permute-done | bytes 262176 | tf_op jit(solution)/shard_map/ppermute | solution.py:415
  125.5 5.6 %collective-permute-done.90.refs_4_ = bf16[2,512,128]{2,1,0:T(8,128)(2,1)} collective-permute-done((bf16[2,512,128]{2,1,0:T(8,128)(2,1)}, bf16[2,512,128]{2,1,0:T(8,128)(2,1)}, u32[]{:S(2)}, u32[]{:S(2)}) %collective-permute-start.90) | collective-permute-done | bytes 262176 | tf_op jit(solution)/shard_map/ppermute | solution.py:415
  131.1 5.6 %collective-permute-done.91.refs_5_ = bf16[2,512,128]{2,1,0:T(8,128)(2,1)} collective-permute-done((bf16[2,512,128]{2,1,0:T(8,128)(2,1)}, bf16[2,512,128]{2,1,0:T(8,128)(2,1)}, u32[]{:S(2)}, u32[]{:S(2)}) %collective-permute-start.91) | collective-permute-done | bytes 262176 | tf_op jit(solution)/shard_map/ppermute | solution.py:415
  136.7 4.7 %collective-permute-done.93.refs_7_ = bf16[2,512,128]{2,1,0:T(8,128)(2,1)} collective-permute-done((bf16[2,512,128]{2,1,0:T(8,128)(2,1)}, bf16[2,512,128]{2,1,0:T(8,128)(2,1)}, u32[]{:S(2)}, u32[]{:S(2)}) %collective-permute-start.93) | collective-permute-done | bytes 262176 | tf_op jit(solution)/shard_map/ppermute | solution.py:415
  141.4 0.1 collective-permute-done.94.refs_8_
  141.5 3.1 %write.1 = bf16[2,32,512,128]{3,2,1,0:T(8,128)(2,1)} custom-call(s32[55]{0:T(128)} %copy-done.1, bf16[2,512,128]{2,1,0:T(8,128)(2,1)} %get-tuple-element.575.refs_1_, bf16[2,512,128]{2,1,0:T(8,128)(2,1)} %collective-permute-done.88.refs_2_, bf16[2,512,128]{2,1,0:T(8,128)(2,1)} %collective-permute-done.89.refs_3_, ...), custom_call_target="tpu_custom_call", output_to_operand_aliasing={{}: (9, {})} | custom-call | tf_op jit(solution)/shard_map/write/pallas_call | solution.py:417
  (21 shorter events, 0.2 us)
Async XLA Ops:
  0.8 0.6 copy-start
  7.6 18.8 %copy-start.1 = (s32[55]{0:T(128)}, s32[55]{0:T(128)S(1)}, u32[]{:S(2)}) copy-start(s32[55]{0:T(128)S(1)} %pad_add_fusion.1.refs_0_) | copy-start | bytes 664
  8.2 23.1 %all-to-all-start = ((s32[32,1,55]{2,1,0:T(1,128)}), s32[32,1,55]{2,1,0:T(1,128)}, u32[]{:S(2)}, u32[]{:S(2)}) async-start(s32[32,1,55]{2,1,0:T(1,128)} %broadcast_in_dim.17), calls=%async_computation | async-start | bytes 32768 | tf_op jit(solution)/shard_map/all_to_all | solution.py:335
  14.3 28.3 %collective-permute-start.80 = (bf16[2,512,128]{2,1,0:T(8,128)(2,1)}, bf16[2,512,128]{2,1,0:T(8,128)(2,1)}, u32[]{:S(2)}, u32[]{:S(2)}) collective-permute-start(bf16[2,512,128]{2,1,0:T(8,128)(2,1)} %get-tuple-element.535.refs_11_), channel_id=1, source_target_pairs={{0,8},{1,9},{2,10},{3,11},{4,12},{5,13},{6,14},{7,15},{8,16},{9,17... | collective-permute-start | bytes 786440 | tf_op jit(solution)/shard_map/ppermute | solution.py:330
  17.4 30.5 %collective-permute-start.81 = (bf16[2,512,128]{2,1,0:T(8,128)(2,1)}, bf16[2,512,128]{2,1,0:T(8,128)(2,1)}, u32[]{:S(2)}, u32[]{:S(2)}) collective-permute-start(bf16[2,512,128]{2,1,0:T(8,128)(2,1)} %get-tuple-element.536.refs_12_), channel_id=1, source_target_pairs={{0,9},{1,10},{2,11},{3,12},{4,13},{5,14},{6,15},{7,8},{8,17},{9,18... | collective-permute-start | bytes 786440 | tf_op jit(solution)/shard_map/ppermute | solution.py:330
  19.9 29.9 %collective-permute-start.82 = (bf16[2,512,128]{2,1,0:T(8,128)(2,1)}, bf16[2,512,128]{2,1,0:T(8,128)(2,1)}, u32[]{:S(2)}, u32[]{:S(2)}) collective-permute-start(bf16[2,512,128]{2,1,0:T(8,128)(2,1)} %get-tuple-element.537.refs_13_), channel_id=1, source_target_pairs={{0,10},{1,11},{2,12},{3,13},{4,14},{5,15},{6,8},{7,9},{8,18},{9,19... | collective-permute-start | bytes 786440 | tf_op jit(solution)/shard_map/ppermute | solution.py:330
  21.9 46.5 %collective-permute-start.83 = (bf16[2,512,128]{2,1,0:T(8,128)(2,1)}, bf16[2,512,128]{2,1,0:T(8,128)(2,1)}, u32[]{:S(2)}, u32[]{:S(2)}) collective-permute-start(bf16[2,512,128]{2,1,0:T(8,128)(2,1)} %get-tuple-element.538.refs_14_), channel_id=1, source_target_pairs={{0,11},{1,12},{2,13},{3,14},{4,15},{5,8},{6,9},{7,10},{8,19},{9,20... | collective-permute-start | bytes 786440 | tf_op jit(solution)/shard_map/ppermute | solution.py:330
  23.8 44.6 %collective-permute-start.84 = (bf16[2,512,128]{2,1,0:T(8,128)(2,1)}, bf16[2,512,128]{2,1,0:T(8,128)(2,1)}, u32[]{:S(2)}, u32[]{:S(2)}) collective-permute-start(bf16[2,512,128]{2,1,0:T(8,128)(2,1)} %get-tuple-element.539.refs_15_), channel_id=1, source_target_pairs={{0,12},{1,13},{2,14},{3,15},{4,8},{5,9},{6,10},{7,11},{8,20},{9,21... | collective-permute-start | bytes 786440 | tf_op jit(solution)/shard_map/ppermute | solution.py:330
  42.7 25.8 %collective-permute-start.85 = (bf16[2,512,128]{2,1,0:T(8,128)(2,1)}, bf16[2,512,128]{2,1,0:T(8,128)(2,1)}, u32[]{:S(2)}, u32[]{:S(2)}) collective-permute-start(bf16[2,512,128]{2,1,0:T(8,128)(2,1)} %get-tuple-element.540.refs_16_), channel_id=1, source_target_pairs={{0,13},{1,14},{2,15},{3,8},{4,9},{5,10},{6,11},{7,12},{8,21},{9,22... | collective-permute-start | bytes 786440 | tf_op jit(solution)/shard_map/ppermute | solution.py:330
  47.9 22.3 %collective-permute-start.86 = (bf16[2,512,128]{2,1,0:T(8,128)(2,1)}, bf16[2,512,128]{2,1,0:T(8,128)(2,1)}, u32[]{:S(2)}, u32[]{:S(2)}) collective-permute-start(bf16[2,512,128]{2,1,0:T(8,128)(2,1)} %get-tuple-element.541.refs_17_), channel_id=1, source_target_pairs={{0,14},{1,15},{2,8},{3,9},{4,10},{5,11},{6,12},{7,13},{8,22},{9,23... | collective-permute-start | bytes 786440 | tf_op jit(solution)/shard_map/ppermute | solution.py:330
  49.9 20.5 %collective-permute-start.87 = (bf16[2,512,128]{2,1,0:T(8,128)(2,1)}, bf16[2,512,128]{2,1,0:T(8,128)(2,1)}, u32[]{:S(2)}, u32[]{:S(2)}) collective-permute-start(bf16[2,512,128]{2,1,0:T(8,128)(2,1)} %get-tuple-element.542.refs_18_), channel_id=1, source_target_pairs={{0,15},{1,8},{2,9},{3,10},{4,11},{5,12},{6,13},{7,14},{8,23},{9,16... | collective-permute-start | bytes 786440 | tf_op jit(solution)/shard_map/ppermute | solution.py:330
  74.3 9.8 %collective-permute-start.44 = (bf16[2,512,128]{2,1,0:T(8,128)(2,1)}, bf16[2,512,128]{2,1,0:T(8,128)(2,1)}, u32[]{:S(2)}, u32[]{:S(2)}) collective-permute-start(bf16[2,512,128]{2,1,0:T(8,128)(2,1)} %get-tuple-element.416), channel_id=1, source_target_pairs={{8,23},{9,16},{10,17},{11,18},{12,19},{13,20},{14,21},{15,22},{16,... | collective-permute-start | bytes 786440 | tf_op jit(solution)/shard_map/cond/branch_8_fun/ppermute | solution.py:400
  89.1 8.3 %collective-permute-start.88 = (bf16[2,512,128]{2,1,0:T(8,128)(2,1)}, bf16[2,512,128]{2,1,0:T(8,128)(2,1)}, u32[]{:S(2)}, u32[]{:S(2)}) collective-permute-start(bf16[2,512,128]{2,1,0:T(8,128)(2,1)} %get-tuple-element.576), channel_id=1, source_target_pairs={{0,1},{1,2},{2,3},{3,4},{4,5},{5,6},{6,7},{7,0},{8,9},{9,10},{10,1... | collective-permute-start | bytes 786440 | tf_op jit(solution)/shard_map/ppermute | solution.py:415
  91.6 33.9 %collective-permute-start.89 = (bf16[2,512,128]{2,1,0:T(8,128)(2,1)}, bf16[2,512,128]{2,1,0:T(8,128)(2,1)}, u32[]{:S(2)}, u32[]{:S(2)}) collective-permute-start(bf16[2,512,128]{2,1,0:T(8,128)(2,1)} %get-tuple-element.577), channel_id=1, source_target_pairs={{0,2},{1,3},{2,4},{3,5},{4,6},{5,7},{6,0},{7,1},{8,10},{9,11},{10,... | collective-permute-start | bytes 786440 | tf_op jit(solution)/shard_map/ppermute | solution.py:415
  95.4 35.6 %collective-permute-start.90 = (bf16[2,512,128]{2,1,0:T(8,128)(2,1)}, bf16[2,512,128]{2,1,0:T(8,128)(2,1)}, u32[]{:S(2)}, u32[]{:S(2)}) collective-permute-start(bf16[2,512,128]{2,1,0:T(8,128)(2,1)} %get-tuple-element.578), channel_id=1, source_target_pairs={{0,3},{1,4},{2,5},{3,6},{4,7},{5,0},{6,1},{7,2},{8,11},{9,12},{10,... | collective-permute-start | bytes 786440 | tf_op jit(solution)/shard_map/ppermute | solution.py:415
  95.6 41.1 %collective-permute-start.91 = (bf16[2,512,128]{2,1,0:T(8,128)(2,1)}, bf16[2,512,128]{2,1,0:T(8,128)(2,1)}, u32[]{:S(2)}, u32[]{:S(2)}) collective-permute-start(bf16[2,512,128]{2,1,0:T(8,128)(2,1)} %get-tuple-element.579), channel_id=1, source_target_pairs={{0,4},{1,5},{2,6},{3,7},{4,0},{5,1},{6,2},{7,3},{8,12},{9,13},{10,... | collective-permute-start | bytes 786440 | tf_op jit(solution)/shard_map/ppermute | solution.py:415
  95.6 41.1 %collective-permute-start.92 = (bf16[2,512,128]{2,1,0:T(8,128)(2,1)}, bf16[2,512,128]{2,1,0:T(8,128)(2,1)}, u32[]{:S(2)}, u32[]{:S(2)}) collective-permute-start(bf16[2,512,128]{2,1,0:T(8,128)(2,1)} %get-tuple-element.580), channel_id=1, source_target_pairs={{0,5},{1,6},{2,7},{3,0},{4,1},{5,2},{6,3},{7,4},{8,13},{9,14},{10,... | collective-permute-start | bytes 786440 | tf_op jit(solution)/shard_map/ppermute | solution.py:415
  97.4 44.0 %collective-permute-start.93 = (bf16[2,512,128]{2,1,0:T(8,128)(2,1)}, bf16[2,512,128]{2,1,0:T(8,128)(2,1)}, u32[]{:S(2)}, u32[]{:S(2)}) collective-permute-start(bf16[2,512,128]{2,1,0:T(8,128)(2,1)} %get-tuple-element.581), channel_id=1, source_target_pairs={{0,6},{1,7},{2,0},{3,1},{4,2},{5,3},{6,4},{7,5},{8,14},{9,15},{10,... | collective-permute-start | bytes 786440 | tf_op jit(solution)/shard_map/ppermute | solution.py:415
  125.5 16.0 %collective-permute-start.94 = (bf16[2,512,128]{2,1,0:T(8,128)(2,1)}, bf16[2,512,128]{2,1,0:T(8,128)(2,1)}, u32[]{:S(2)}, u32[]{:S(2)}) collective-permute-start(bf16[2,512,128]{2,1,0:T(8,128)(2,1)} %get-tuple-element.582), channel_id=1, source_target_pairs={{0,7},{1,0},{2,1},{3,2},{4,3},{5,4},{6,5},{7,6},{8,15},{9,8},{10,9... | collective-permute-start | bytes 786440 | tf_op jit(solution)/shard_map/ppermute | solution.py:415
